TPU v7x, 32 devices: a whole 2x2x4 slice. The times are simulated.
32 devices in a mesh: stream: 2 (over core), batch: 16 (over z, y, x).
Axes of the slice: x: 2, y: 2, z: 4, core: 2. Of those that a mesh axis runs over, the one named last changes fastest.
Arguments:
- inputs: bfloat16 [2, 16, 1024, 768], P('stream', 'batch'), may hold values from -6 to 6
- lengths: int32 [16], P('batch'), may hold values from 128 to 1024, as said below
- cotangent: bfloat16 [2, 16, 1024, 768], P('stream', 'batch'), may hold values from -6 to 6
- qkv_weight: bfloat16 [768, 2304], replicated, may hold values from -0.21875 to 0.21875
- out_weight: bfloat16 [768, 768], replicated, may hold values from -2 to 2
- up_weight: bfloat16 [768, 3072], replicated, may hold values from -0.21875 to 0.21875
- down_weight: bfloat16 [3072, 768], replicated, may hold values from -0.109375 to 0.109375
- attn_gain: float32 [768], replicated, may hold values from 0.5 to 1.5
- mlp_gain: float32 [768], replicated, may hold values from 0.5 to 1.5
Outputs:
- outputs: bfloat16 [2, 16, 1024, 768], P('stream', 'batch')
- input_grad: bfloat16 [2, 16, 1024, 768], P('stream', 'batch')
- qkv_grad: float32 [768, 2304], P(('stream', 'batch'))
- out_grad: float32 [768, 768], P(('stream', 'batch'))
- up_grad: float32 [768, 3072], P(None, ('stream', 'batch'))
- down_grad: float32 [3072, 768], P(('stream', 'batch'))
- attn_gain_grad: float32 [768], replicated
- mlp_gain_grad: float32 [768], replicated
- rms: float32 [3], replicated
Inputs may be any that keep to these rules, and one draw needn't show every extreme that they name: `lengths`: each length is a multiple of 16; some row has length 1024.
All inputs are finite; a program needn't handle non-finite values.
Results may differ from a plain program's by a relative error of at most 0.014.
Values may be sent and summed in bfloat16 or wider, within the bound.
No kernel may reach another device: no remote copies, remote signals or barrier semaphores. Data moves between devices by JAX's collectives and lax.ppermute only.
A program may use at most 384 MiB of HBM per device.

v0:
```python
import functools

import jax
import jax.numpy as jnp
import numpy as np
from jax import lax
from jax.experimental import pallas as pl
from jax.experimental.pallas import tpu as pltpu
from jax.sharding import PartitionSpec as P

f32 = jnp.float32
bf16 = jnp.bfloat16

HD = 64
BLK = 16
EPS = 1e-06
NEG = -1e30
PW = 2 * HD
T = 128
R = 256
AHEAD = 2
FC = 768
SCALE = HD**-0.5
BIG = 61
GROUPS = 3

COST = pl.CostEstimate(flops=1 << 20, bytes_accessed=1 << 16, transcendentals=0)
LONG = pl.CostEstimate(flops=1 << 35, bytes_accessed=1 << 26, transcendentals=0)

SMEM = pl.BlockSpec(memory_space=pltpu.SMEM)
IN_VMEM = pl.BlockSpec(memory_space=pltpu.VMEM)


def params(mib):
    return pltpu.CompilerParams(vmem_limit_bytes=mib << 20)


def shape(dims, dtype):
    return jax.ShapeDtypeStruct(dims, dtype)


def pinned(*arrays):
    return [pltpu.with_memory_space_constraint(a, pltpu.HBM) for a in arrays]


def nn(a, b):
    return jnp.dot(a, b, preferred_element_type=f32)


def nt(a, b):
    return lax.dot_general(a, b, (((1,), (1,)), ((), ())), preferred_element_type=f32)


def tn(a, b):
    return lax.dot_general(a, b, (((0,), (0,)), ((), ())), preferred_element_type=f32)


def whole(dims):
    return pl.BlockSpec(dims, lambda *_: (0,) * len(dims), pipeline_mode=pl.Buffered(1))


def inv_rms(v):
    return lax.rsqrt(jnp.mean(v * v, axis=-1, keepdims=True) + EPS)


def norm_back(v, gain, grad):
    r = inv_rms(v)
    unit = v * r
    scaled = grad * gain
    inner = jnp.mean(scaled * unit, axis=-1, keepdims=True)
    return r * (scaled - unit * inner), grad * unit


def rotary_tables(length):
    half = HD // 2
    freqs = np.exp(-np.log(10000.0) * np.arange(half) / half).astype(np.float32)
    angles = (np.arange(length, dtype=np.float32)[:, None] * freqs[None, :]).astype(np.float64)
    return np.cos(angles).astype(np.float32), np.sin(angles).astype(np.float32)


def rotated(v, cosine, signed, sign):
    first = lax.broadcasted_iota(jnp.int32, (1, PW), 1) % HD < HD // 2
    outs = []
    for c in range(0, v.shape[1], PW):
        part = v[:, c : c + PW]
        partner = jnp.where(first, pltpu.roll(part, PW - HD // 2, 1), pltpu.roll(part, HD // 2, 1))
        outs.append(part * cosine + partner * (signed * sign))
    return outs[0] if len(outs) == 1 else jnp.concatenate(outs, axis=1)


def in_turn(count, *stages):
    def turn(t, carry):
        state = ()
        for stage in stages:
            state = stage(t, *state)
        return carry

    lax.fori_loop(0, count, turn, 0)


def token_weight(start, length, rows):
    return lax.broadcasted_iota(jnp.int32, (rows, 1), 0) + start < length


def row_sum(v):
    return jnp.sum(v, axis=0, keepdims=True)


def by_pairs(ref, rows, value):
    for p in range(ref.shape[0]):
        ref[p, rows, :] = value[:, p * PW : (p + 1) * PW].astype(ref.dtype)


def stacked(tile, low):
    zero = jnp.zeros_like(tile)
    return jnp.concatenate([jnp.where(low, tile, zero), jnp.where(low, zero, tile)], axis=0)


def unstacked(tile_t):
    half = lax.broadcasted_iota(jnp.int32, (PW, 1), 0) < HD
    return jnp.where(half, tile_t[:, :T], tile_t[:, T:])


def chunks_of(i):
    out, j = [], 0
    while j < i:
        n = 2 if i - j >= 2 else 1
        out.append((j * T, n * T))
        j += n
    return out


def edge_bias(ref, noisy):
    row = lax.broadcasted_iota(jnp.int32, (T, 2 * T), 0) // BLK
    col = (lax.broadcasted_iota(jnp.int32, (T, 2 * T), 1) % T) // BLK
    own = jnp.logical_or(row == col, jnp.logical_and(row < col, noisy == 0))
    other = jnp.logical_and(row < col, noisy == 1)
    ref[:T, :] = jnp.where(own, 0.0, NEG)
    ref[T:, :] = jnp.where(other, 0.0, NEG)


def masked(s, start, length):
    pos = lax.broadcasted_iota(jnp.int32, s.shape, 0) + start
    return jnp.where(pos < length, s, NEG)


def over_rows(op, v):
    return op(v.reshape(v.shape[0] // 8, 8, v.shape[1]), axis=0)


def attend_pair(length, q, ko, vo, kc, vc, store, lse, vo_t, vc_t, scores, bias):
    seq = q.shape[0]
    low = lax.broadcasted_iota(jnp.int32, (1, PW), 1) < HD
    vo_t[...] = vo[...].T
    vc_t[...] = vc[...].T

    def score(i):
        at = pl.ds(i * T, T)
        q2 = stacked(q[at, :] * bf16(SCALE), low)
        buf = scores.at[i % AHEAD]
        edge = nt(jnp.concatenate([ko[at, :], kc[at, :]], 0), q2) + bias[...]
        own = masked(edge[:T], i * T, length)
        other = masked(edge[T:], i * T, length)
        buf[pl.ds(0, T), :] = own
        buf[pl.ds(T, T), :] = other
        top = over_rows(jnp.max, jnp.maximum(own, other))
        for start, size in chunks_of(i):
            s = masked(nt(kc[pl.ds(start, size), :], q2), start, length)
            buf[pl.ds(2 * T + start, size), :] = s
            top = jnp.maximum(top, over_rows(jnp.max, s))
        return jnp.max(top, axis=0, keepdims=True)

    def mix(i, top):
        at = pl.ds(i * T, T)
        buf = scores.at[i % AHEAD]
        p = jnp.exp(buf[pl.ds(0, 2 * T), :] - top)
        total = over_rows(jnp.sum, p)
        acc = nn(jnp.concatenate([vo_t[:, at], vc_t[:, at]], 1), p.astype(bf16))
        for start, size in chunks_of(i):
            p = jnp.exp(buf[pl.ds(2 * T + start, size), :] - top)
            total = total + over_rows(jnp.sum, p)
            acc = acc + nn(vc_t[:, pl.ds(start, size)], p.astype(bf16))
        total = row_sum(total)
        lse[0, pl.ds(i, 1), :] = top + jnp.log(total)
        store(at, unstacked(acc * (1.0 / total)))

    tops = {}
    for i in range(seq // T + AHEAD - 1):
        if i < seq // T:
            tops[i] = score(i)
        if i >= AHEAD - 1:
            mix(i - AHEAD + 1, tops.pop(i - AHEAD + 1))


def turned_back(v, cosine, sine):
    quarter = HD // 2
    a, b, c, d = (v[i * quarter : (i + 1) * quarter] for i in range(4))
    return jnp.concatenate(
        [a * cosine + b * sine, b * cosine - a * sine, c * cosine + d * sine, d * cosine - c * sine]
    )


def attend_back_kernel(
    info, q, ko, vo, kc, vc, o, do, lse, cosine, sine, dq, keep, send, ko_t, kc_t, dko, dvo, dkc, dvc, bias
):
    noisy, length = info[0], info[1]
    q, ko, vo, kc, vc = (ref.at[0] for ref in (q, ko, vo, kc, vc))
    seq = q.shape[0]
    low = lax.broadcasted_iota(jnp.int32, (1, PW), 1) < HD

    @pl.when(pl.program_id(0) == 0)
    def _():
        edge_bias(bias, noisy)

    ko_t[...] = ko[...].T
    kc_t[...] = kc[...].T

    def tile(i):
        at = pl.ds(i * T, T)
        prod = (do[at, :].astype(f32) * o[at, :].astype(f32)).T
        delta = jnp.concatenate([row_sum(prod[:HD]), row_sum(prod[HD:])], 1)
        q2 = stacked(q[at, :] * bf16(SCALE), low)
        return q2, stacked(do[at, :], low), lse[0, pl.ds(i, 1), :], delta

    def products(i, start, size, q2, do2):
        if start is None:
            at = pl.ds(i * T, T)
            s = nt(jnp.concatenate([ko[at, :], kc[at, :]], 0), q2) + bias[...]
            s = jnp.concatenate([masked(s[:T], i * T, length), masked(s[T:], i * T, length)], 0)
            return s, nt(jnp.concatenate([vo[at, :], vc[at, :]], 0), do2)
        rows = pl.ds(start, size)
        return masked(nt(kc[rows, :], q2), start, length), nt(vc[rows, :], do2)

    def gather(i, start, size, q2, do2, p, ds, dq_t):
        at = pl.ds(i * T, T)
        dv, dk = nn(p, do2), nn(ds, q2)
        if start is None:
            dvo[at, :] = dv[:T]
            dko[at, :] = dk[:T]
            dvc[at, :] = dv[T:]
            dkc[at, :] = dk[T:]
            return nn(jnp.concatenate([ko_t[:, at], kc_t[:, at]], 1), ds)
        rows = pl.ds(start, size)
        dvc[rows, :] += dv
        dkc[rows, :] += dk
        return dq_t + nn(kc_t[:, rows], ds)

    work = [(i, *c) for i in range(seq // T) for c in [(None, None)] + chunks_of(i)]
    tiles, made, weighed, dq_t = {}, {}, {}, None
    for n in range(len(work) + 2):
        if n < len(work):
            i = work[n][0]
            if i not in tiles:
                tiles[i] = tile(i)
            made[n] = products(*work[n], *tiles[i][:2])
        if 0 <= n - 1 < len(work):
            _, _, norm, delta = tiles[work[n - 1][0]]
            s, dp = made.pop(n - 1)
            p = jnp.exp(s - norm)
            weighed[n - 1] = p.astype(bf16), (p * (dp - delta)).astype(bf16)
        if n >= 2:
            i, start, size = work[n - 2]
            dq_t = gather(i, start, size, *tiles[i][:2], *weighed.pop(n - 2), dq_t)
            if n == len(work) + 1 or work[n - 1][0] != i:
                at = pl.ds(i * T, T)
                out = turned_back(unstacked(dq_t), cosine[:, at], sine[:, at]) * SCALE
                dq[at, :] = out.T.astype(bf16)
    clean = (1 - noisy).astype(f32)
    for at, own, other in ((0, dko, dkc), (1, dvo, dvc)):
        keep[at] = (own[...] + clean * other[...]).astype(bf16)
        send[at] = other[...].astype(bf16)


def attend_back(info, first, pairs, q, ko, vo, kc, vc, o, do, lse, cosine, sine):
    seq = q.shape[1]
    width = pairs * PW
    heads = pl.BlockSpec((1, seq, PW), lambda h: (first + h, 0, 0))
    source = pl.BlockSpec((seq, PW), lambda h: (0, first + h))
    both = pl.BlockSpec((2, seq, PW), lambda h: (0, 0, h))
    lines = pl.BlockSpec((1, seq // T, 2 * T), lambda h: (first + h, 0, 0))
    table = whole((HD // 2, seq))
    return pl.pallas_call(
        attend_back_kernel,
        grid=(pairs,),
        in_specs=[SMEM] + [heads] * 5 + [source] * 2 + [lines, table, table],
        out_specs=[pl.BlockSpec((seq, PW), lambda h: (0, h)), both, both],
        out_shape=[shape((seq, width), bf16)] + [shape((2, seq, width), bf16)] * 2,
        scratch_shapes=[pltpu.VMEM((PW, seq), bf16)] * 2
        + [pltpu.VMEM((seq, PW), f32)] * 4
        + [pltpu.VMEM((2 * T, 2 * T), f32)],
        compiler_params=params(24),
        cost_estimate=LONG,
        name="attend_back",
    )(info, *pinned(q, ko, vo, kc, vc, o, do), lse, cosine, sine)


C0 = 0.7978845608028654
C1 = C0 * 0.044715


def layer_kernel(
    info, gain1_line, gain2_line, cosine_t, sine_t, received, x_any, wqkv_any, wo_any, dy_any,
    w1_any, w2_any,
    q_out, ko_out, vo_out, kc_out, vc_out, h1t_out, o_out, lse_out, out_any, dx2_any, do_any,
    up_send, up_keep, down_send, down_keep, g_send, g_keep, cosine_out, signed_out, sums,
    x, wqkv, cosine, signed, q, ko, vo, h1t, wo, dy, w1, w2,
    kc, vc, vo_t, vc_t, scores, bias, o, o_t, lse, x2, h2, m, dh, act, du, up_grad, down_grad, half_grads,
    sem_in, sem_1, sem_2, sem_out, sem_up, sem_down, sem_tile,
):
    noisy, length = info[0], info[1]
    seq, width = x.shape
    chunks, pairs, tiles = w1.shape[0], kc.shape[0], seq // R
    copy = pltpu.make_async_copy
    gain1, gain2 = gain1_line[...].reshape(1, width), gain2_line[...].reshape(1, width)

    def weights(c):
        place = lax.rem(c + (chunks // 2) * (1 - noisy), chunks) * FC
        place = pl.multiple_of(place, FC)
        return (
            copy(w1_any.at[:, pl.ds(place, FC)], w1.at[c], sem_1.at[c]),
            copy(w2_any.at[pl.ds(place, FC), :], w2.at[c], sem_2.at[c]),
        )

    sources = (
        (x_any, x),
        (wqkv_any, wqkv),
        (wo_any, wo),
        (dy_any, dy),
    )
    loads = [copy(a, b, sem_in.at[i]) for i, (a, b) in enumerate(sources)]
    for load in loads[:2]:
        load.start()
    sums[...] = jnp.zeros_like(sums)
    edge_bias(bias, noisy)
    def widen(t):
        rows = pl.ds(pl.multiple_of(t * PW, PW), PW)
        c, d = cosine_t[:, rows].T, sine_t[:, rows].T
        cosine[rows, :] = jnp.concatenate([c, c, c, c], axis=1)
        signed[rows, :] = jnp.concatenate([-d, d, -d, d], axis=1)
        return ()

    in_turn(seq // PW, widen)
    tables_out = [copy(cosine, cosine_out, sem_out.at[10]), copy(signed, signed_out, sem_out.at[11])]
    span = lambda t: pl.ds(pl.multiple_of(t * R, R), R)

    loads[0].wait()

    def own_norm(t):
        value = x[span(t), :].astype(f32)
        h1 = (value * inv_rms(value) * gain1).astype(bf16)
        h2[span(t), :] = h1
        h1t[:, span(t)] = h1.T
        weight = token_weight(t * R, length, R)
        sums[0:1, :] += row_sum(jnp.where(weight, value * value, 0.0))
        return ()

    in_turn(tiles, own_norm)
    loads[1].wait()
    for load in loads[2:]:
        load.start()

    def own_product(t):
        return tuple(nn(h2[span(t), :], wqkv[:, i * width : (i + 1) * width]) for i in range(3))

    def own_turn(t, a, b, c):
        tables = (cosine[span(t), :], signed[span(t), :], 1.0)
        by_pairs(q, span(t), rotated(a, *tables))
        by_pairs(ko, span(t), rotated(b, *tables))
        by_pairs(vo, span(t), c)
        return ()

    def clean_norm(t):
        value = jnp.where(noisy == 1, received[span(t), :].astype(f32), x[span(t), :].astype(f32))
        o[span(t), :] = (value * inv_rms(value) * gain1).astype(bf16)
        return ()

    def clean_product(t):
        return tuple(nn(o[span(t), :], wqkv[:, i * width : (i + 1) * width]) for i in (1, 2))

    def clean_turn(t, a, b):
        by_pairs(kc, span(t), rotated(a, cosine[span(t), :], signed[span(t), :], 1.0))
        by_pairs(vc, span(t), b)
        return ()

    in_turn(tiles, own_product, own_turn)
    stores = [
        copy(a, b, sem_out.at[6 + i])
        for i, (a, b) in enumerate(((q, q_out), (ko, ko_out), (vo, vo_out), (h1t, h1t_out)))
    ]
    stores += tables_out
    for store in stores:
        store.start()
    in_turn(tiles, clean_norm, clean_product, clean_turn)
    more = [copy(kc, kc_out, sem_out.at[0]), copy(vc, vc_out, sem_out.at[1])]
    for store in more:
        store.start()
    stores += more

    for c in range(chunks):
        for load in weights(c):
            load.start()

    def one_pair(p, carry):
        lanes = pl.ds(pl.multiple_of(p * PW, PW), PW)

        def keep(at, tile_t):
            o_t[lanes, at] = tile_t.astype(bf16)
            o[at, lanes] = tile_t.T.astype(bf16)

        heads = (ref.at[p] for ref in (q, ko, vo, kc, vc))
        attend_pair(length, *heads, keep, lse.at[pl.ds(p, 1)], vo_t, vc_t, scores, bias)
        return carry

    lax.fori_loop(0, pairs, one_pair, 0)
    mixed_out = copy(o, o_out, sem_out.at[2])
    mixed_out.start()
    stores += [copy(lse, lse_out, sem_out.at[3])]
    stores[-1].start()

    for load in loads[2:]:
        load.wait()

    def join_product(t):
        return (nn(o[span(t), :], wo[...]),)

    def join_norm(t, branch):
        value = x[span(t), :].astype(f32) + branch
        x2[span(t), :] = value
        h2[span(t), :] = (value * inv_rms(value) * gain2).astype(bf16)
        m[span(t), :] = jnp.zeros_like(value)
        dh[span(t), :] = jnp.zeros_like(value)
        weight = token_weight(t * R, length, R)
        sums[1:2, :] += row_sum(jnp.where(weight, branch * branch, 0.0))
        return ()

    in_turn(tiles, join_product, join_norm)

    def grad_stores(c, up, down):
        slot = lax.rem(c, 2)
        rows = pl.ds(pl.multiple_of(lax.rem(c, chunks // 2) * FC, FC), FC)
        return (
            copy(up_grad.at[slot], up.at[rows, :], sem_up.at[slot]),
            copy(down_grad.at[slot], down.at[rows, :], sem_down.at[slot]),
        )

    def one_chunk(c, carry):
        for load in weights(c):
            load.wait()
        up, down = w1.at[c], w2.at[c]
        made = {}
        for t in range(-R, seq, R):
            if t + R < seq:
                rows = pl.ds(t + R, R)
                made[t + R] = nn(h2[rows, :], up[...]), nt(dy[rows, :], down[...])
            if t < 0:
                continue
            rows = pl.ds(t, R)
            u, da = made.pop(t)
            sq = u * u
            half = 0.5 * jnp.tanh(u * (C0 + C1 * sq)) + 0.5
            low = (u * half).astype(bf16)
            slope = half + u * (2.0 * half * (1.0 - half)) * (C0 + 3.0 * C1 * sq)
            back = (da * slope).astype(bf16)
            act[rows, :] = low
            du[rows, :] = back
            m[rows, :] += nn(low, down[...])
            dh[rows, :] += nt(back, up[...])

        @pl.when(c >= 2)
        def _():
            for store in grad_stores(c, up_send, down_send):
                store.wait()

        slot = lax.rem(c, 2)
        down_grad[slot] = tn(act[...], dy[...]).astype(bf16)
        up_grad[slot] = tn(du[...], h2[...]).astype(bf16)

        @pl.when(c < chunks // 2)
        def _():
            for store in grad_stores(c, up_send, down_send):
                store.start()

        @pl.when(c >= chunks // 2)
        def _():
            for store in grad_stores(c, up_keep, down_keep):
                store.start()

        return carry

    lax.fori_loop(0, chunks, one_chunk, 0)

    mixed_out.wait()

    def tile_stores(t):
        return (
            copy(h2.at[span(t), :], out_any.at[span(t), :], sem_tile.at[t, 0]),
            copy(x2.at[span(t), :], dx2_any.at[span(t), :], sem_tile.at[t, 1]),
            copy(o.at[span(t), :], do_any.at[span(t), :], sem_tile.at[t, 2]),
        )

    def middle_norm(t):
        value = x2[span(t), :]
        mixed = m[span(t), :]
        weight = token_weight(t * R, length, R)
        sums[2:3, :] += row_sum(jnp.where(weight, mixed * mixed, 0.0))
        grad, gain_terms = norm_back(value, gain2, dh[span(t), :])
        sums[3:4, :] += row_sum(gain_terms)
        grad = grad + dy[span(t), :].astype(f32)
        h2[span(t), :] = (value + mixed).astype(bf16)
        x2[span(t), :] = grad
        x[span(t), :] = grad.astype(bf16)
        return ()

    def middle_product(t):
        o[span(t), :] = nt(x[span(t), :], wo[...]).astype(bf16)
        for store in tile_stores(t):
            store.start()
        return ()

    in_turn(tiles, middle_norm, middle_product)
    half = width // 2
    mine = pl.multiple_of(noisy * half, half)
    half_grads[0] = nn(o_t[pl.ds(half - mine, half), :], x[...]).astype(bf16)
    half_grads[1] = nn(o_t[pl.ds(mine, half), :], x[...]).astype(bf16)
    more = [copy(half_grads.at[0], g_send, sem_out.at[4]), copy(half_grads.at[1], g_keep, sem_out.at[5])]
    for store in more:
        store.start()
    stores += more
    for c in range(chunks - 2, chunks):
        stores += grad_stores(c, up_keep, down_keep)
    for t in range(tiles):
        stores += tile_stores(t)
    for store in stores:
        store.wait()


def layer(info, gain1, gain2, cosine_t, sine_t, received, x, wqkv, wo, dy, w1, w2):
    seq, width = x.shape
    hidden = w1.shape[1]
    tiles, pairs, chunks = seq // R, width // PW, hidden // FC
    anywhere = pl.BlockSpec(memory_space=pl.ANY)
    vmem = pltpu.VMEM
    dma = pltpu.SemaphoreType.DMA
    heads = (pairs, seq, PW)
    flat = (seq, width)
    outs = (
        [shape(heads, bf16)] * 5
        + [shape((width, seq), bf16), shape(flat, bf16), shape((pairs, seq // T, 2 * T), f32)]
        + [shape(flat, bf16), shape(flat, f32), shape(flat, bf16)]
        + [shape((hidden // 2, width), bf16)] * 4
        + [shape((width // 2, width), bf16)] * 2
        + [shape((seq, PW), f32)] * 2
        + [shape((8, width), f32)]
    )
    return pl.pallas_call(
        layer_kernel,
        in_specs=[SMEM] + [IN_VMEM] * 5 + [anywhere] * 6,
        out_specs=[anywhere] * 19 + [IN_VMEM],
        out_shape=outs,
        scratch_shapes=[vmem(flat, bf16)]
        + [vmem(wqkv.shape, bf16), vmem((seq, PW), f32), vmem((seq, PW), f32)]
        + [vmem(heads, bf16)] * 3
        + [vmem((width, seq), bf16), vmem((width, width), bf16), vmem(flat, bf16)]
        + [vmem((chunks, width, FC), bf16), vmem((chunks, FC, width), bf16)]
        + [vmem(heads, bf16)] * 2
        + [vmem((PW, seq), bf16)] * 2
        + [vmem((AHEAD, seq + T, 2 * T), f32), vmem((2 * T, 2 * T), f32)]
        + [vmem(flat, bf16), vmem((width, seq), bf16)]
        + [vmem((pairs, seq // T, 2 * T), f32)]
        + [vmem(flat, f32), vmem(flat, bf16)]
        + [vmem(flat, f32)] * 2
        + [vmem((seq, FC), bf16)] * 2
        + [vmem((2, FC, width), bf16)] * 2
        + [vmem((2, width // 2, width), bf16)]
        + [dma((4,)), dma((chunks,)), dma((chunks,)), dma((12,)), dma((2,)), dma((2,)), dma((tiles, 3))],
        compiler_params=params(BIG),
        cost_estimate=LONG,
        name="layer",
    )(info, gain1, gain2, cosine_t, sine_t, received, *pinned(x, wqkv, wo, dy, w1, w2))


def weigh_kernel(first, info, dq, keep, got, cosine, signed, h1t, wqkv, sums, dkv, g_send, g_keep, small):
    width, half = wqkv.shape[0], wqkv.shape[0] // 2
    mine = pl.multiple_of(info[0] * half, half)
    dk = keep[0].astype(f32) + got[0].astype(f32)
    dkv[0] = rotated(dk, cosine[...], signed[...], -1.0).astype(bf16)
    dkv[1] = (keep[1].astype(f32) + got[1].astype(f32)).astype(bf16)
    small[...] = sums[...]
    for out, start in ((g_send, half - mine), (g_keep, mine)):
        rows = pl.ds(start, half)
        terms = 0.0
        for i, part in enumerate((dq, dkv.at[0], dkv.at[1])):
            total = nn(h1t[rows, :], part[...])
            out[i] = total.astype(bf16)
            at = i * width + first * PW
            weighted = total * wqkv[rows, at : at + total.shape[1]].astype(f32)
            for c in range(0, total.shape[1], PW):
                terms = terms + weighted[:, c : c + PW]
        line = jnp.sum(terms.T, axis=0, keepdims=True)
        lanes = lax.broadcasted_iota(jnp.int32, (1, width), 1)
        inside = jnp.logical_and(lanes >= start, lanes < start + half)
        small[4:5, :] += jnp.where(inside, jnp.concatenate([line, line], axis=1), 0.0)
    small[5:6, :] = jnp.full((1, width), info[1].astype(f32))


def weigh(info, first, dq, keep, got, tables, h1t, wqkv, sums):
    seq, width = dq.shape
    tall = h1t.shape[0]
    return pl.pallas_call(
        functools.partial(weigh_kernel, first),
        in_specs=[SMEM] + [IN_VMEM] * 8,
        out_specs=[IN_VMEM] * 4,
        out_shape=[shape((2, seq, width), bf16)]
        + [shape((3, tall // 2, width), bf16)] * 2
        + [shape(sums.shape, f32)],
        compiler_params=params(24),
        cost_estimate=LONG,
        name="weigh",
    )(info, dq, keep, got, *tables, h1t, wqkv, sums)


def finish_kernel(parts, tiles, x, dx2, wqkv, gain_line, *refs):
    dx_any, dx, sem = refs[-3:]
    dqs, dkvs = refs[:parts], refs[parts : 2 * parts]
    gain = gain_line[...].reshape(1, x.shape[1])

    def store(t):
        rows = pl.ds(pl.multiple_of(t * R, R), R)
        return pltpu.make_async_copy(dx.at[rows, :], dx_any.at[rows, :], sem.at[t])

    def some_rows(t, carry):
        rows = pl.ds(pl.multiple_of(t * R, R), R)
        grads = [r[rows, :] for r in dqs] + [r[0, rows, :] for r in dkvs] + [r[1, rows, :] for r in dkvs]
        dh = nt(jnp.concatenate(grads, axis=1), wqkv[...])
        grad, _ = norm_back(x[rows, :].astype(f32), gain, dh)
        dx[rows, :] = (dx2[rows, :] + grad).astype(bf16)
        store(t).start()
        return carry

    lax.fori_loop(*tiles, some_rows, 0)
    for t in range(*tiles):
        store(t).wait()


def finish(tiles, x, dx2, dqs, dkvs, weight, gain, before):
    anywhere = pl.BlockSpec(memory_space=pl.ANY)
    ins = 4 + len(dqs) + len(dkvs)
    return pl.pallas_call(
        functools.partial(finish_kernel, len(dqs), tiles),
        in_specs=[IN_VMEM] * ins + [anywhere] * len(before),
        out_specs=anywhere,
        out_shape=shape(x.shape, bf16),
        scratch_shapes=[pltpu.VMEM(x.shape, bf16), pltpu.SemaphoreType.DMA((x.shape[0] // R,))],
        input_output_aliases={ins: 0} if before else {},
        compiler_params=params(24),
        cost_estimate=COST if before else LONG,
        name="finish",
    )(x, dx2, weight, gain, *dqs, *dkvs, *before)


def bit_orders(count, groups):
    bits = [1 << i for i in range(count.bit_length() - 1)]
    if groups == 2:
        return [bits, bits[1::-1] + bits[2:]]
    return [bits[g:-1] + bits[:g] + bits[-1:] for g in range(groups)]


def exchange(value, axis, bit):
    size = lax.axis_size(axis)
    return lax.ppermute(value, axis, [(i, i ^ bit) for i in range(size)])


def distance(order, place):
    out = 0
    for i, bit in enumerate(order):
        out = out + ((place >> (len(order) - 1 - i)) & 1) * bit
    return out


SUMS = 8


def halves(value):
    high = value.astype(bf16)
    return high, (value - high.astype(f32)).astype(bf16)


def put_sums(value, kept, block):
    high, low = halves(value)
    lines = kept.shape[0]
    block[:lines, :] = high
    block[lines : 2 * lines, :] = low
    kept[...] = high.astype(f32) + low.astype(f32)


def got_sums(block):
    lines = block.shape[0] // 2
    return block[:lines, :].astype(f32) + block[lines:, :].astype(f32)


def start_kernel(orders, sources, small, me, *refs):
    groups = len(orders)
    arrays = max(a for source in sources for a, _, _ in source) + 1
    ins, outs = refs[: 2 * arrays], refs[len(refs) - 2 * groups :]
    half = outs[0].shape[0]
    for g, order in enumerate(orders):
        for side in range(2):

            def one(r, carry, g=g, order=order, side=side):
                part = me[0] ^ distance(order, r + side * half)
                out = outs[2 * g + side]
                row = 0
                for a, where, unit in sources[g]:
                    kept, got = ins[2 * a : 2 * a + 2]
                    place = where(part)
                    size, wide = kept.shape[1], out.shape[-1]
                    lanes = slice(unit * wide, (unit + 1) * wide)
                    total = kept[place, :, lanes].astype(f32) + got[place, :, lanes].astype(f32)
                    if len(out.shape) == 3:
                        out[r, row : row + size, :] = total.astype(bf16)
                    else:
                        start = pl.multiple_of(r * outs[0].shape[1] + row, 8)
                        out[pl.ds(start, size), :] = total.astype(bf16)
                    row += size
                return carry

            lax.fori_loop(0, half, one, 0)
    if small:
        here, there, kept = refs[2 * arrays : 2 * arrays + 3]
        total = here[...] + there[...]
        if small == "rides":
            wide = kept.shape[1]
            total = jnp.concatenate([total[:, c : c + wide] for c in range(0, total.shape[1], wide)], axis=0)
            put_sums(total, kept, outs[1].at[pl.ds(half * outs[0].shape[1], 2 * kept.shape[0]), :])
        else:
            kept[...] = total


def travelling(count, rows, width, lines):
    return shape((count * rows + 2 * lines, width) if lines else (count, rows, width), bf16)


def start_sum(me, kept, got, sources, width, orders, small, rides):
    count = 1 << len(orders[0])
    half = count // 2
    rows = [sum(kept[a].shape[1] for a, _, _ in source) for source in sources]
    lines = small[0].size // width if rides else 0
    cols = width // 3
    args = [a for pair in zip(kept, got, strict=True) for a in pair]
    sums = []
    for g in range(len(orders)):
        sums += [shape((half, rows[g], width), bf16), travelling(half, rows[g], width, 0 if g else lines)]
    mode = "rides" if rides else "alone" if small else ""
    if small:
        specs = dict(
            in_specs=[SMEM] + [IN_VMEM] * (len(args) + 2),
            out_specs=[IN_VMEM] * (1 + len(sums)),
            out_shape=[shape((lines, width) if rides else small[0].shape, f32)] + sums,
        )
    else:
        block = lambda a: pl.BlockSpec((a.shape[0], a.shape[1], cols), lambda c: (0, 0, c))
        specs = dict(
            grid=(width // cols,),
            in_specs=[SMEM] + [block(a) for a in args],
            out_specs=[block(a) for a in sums],
            out_shape=sums,
        )
    outs = pl.pallas_call(
        functools.partial(start_kernel, orders, sources, mode),
        compiler_params=params(30),
        cost_estimate=COST,
        name="start_sum",
        **specs,
    )(me, *args, *small)
    small, outs = list(outs[: len(outs) - len(sums)]), outs[len(outs) - len(sums) :]
    return list(outs[0::2]), list(outs[1::2]), small


def block_of(ref, r, size, row=0, step=0):
    if len(ref.shape) == 3:
        return ref.at[r, pl.ds(row, size), :]
    start = r * (step or size) + row
    return ref.at[pl.ds(start if isinstance(start, int) else pl.multiple_of(start, 8), size), :]


def step_kernel(groups, merge, mode, *refs):
    kept, got = refs[:groups], refs[groups : 2 * groups]
    outs = refs[2 * groups + (2 if mode == "alone" else 1 if mode else 0) :]
    count = kept[0].shape[0]
    half = count // 2

    def one(r, carry):
        row = 0
        for g in range(groups):
            keep, send = outs[:2] if merge else outs[2 * g : 2 * g + 2]
            size = kept[g].shape[1]
            for out, block in ((keep, r), (send, r + half)):
                total = kept[g][block].astype(f32) + block_of(got[g], block, size)[...].astype(f32)
                block_of(out, r, size, row, keep.shape[1])[...] = total.astype(bf16)
            row += size if merge else 0
        return carry

    lax.fori_loop(0, half, one, 0)
    if mode == "rides":
        total = refs[2 * groups][...] + got_sums(got[0][count * kept[0].shape[1] :])
        put_sums(total, outs[-1], outs[1].at[pl.ds(half * outs[0].shape[1], 2 * total.shape[0]), :])
    elif mode:
        outs[-1][...] = refs[2 * groups][...] + refs[2 * groups + 1][...]


def step_sum(kept, got, small, merge, rides):
    groups = len(kept)
    half = kept[0].shape[0] // 2
    rows = [a.shape[1] for a in kept]
    width = kept[0].shape[2]
    args = [*kept, *got, *small]
    sums = []
    for g, r in enumerate([sum(rows)] if merge else rows):
        sums += [shape((half, r, width), bf16), travelling(half, r, width, 0 if g or not rides else small[0].shape[0])]
    outs = pl.pallas_call(
        functools.partial(step_kernel, groups, merge, "rides" if rides else "alone" if small else ""),
        in_specs=[IN_VMEM] * len(args),
        out_specs=[IN_VMEM] * (len(sums) + len(small[:1])),
        out_shape=sums + [shape(a.shape, f32) for a in small[:1]],
        compiler_params=params(16),
        cost_estimate=COST if small or half == 1 else LONG,
        name="step_sum",
    )(*args)
    return list(outs[0 : len(sums) : 2]), list(outs[1 : len(sums) : 2]), list(outs[len(sums) :])


def feed_end_kernel(kept, got, down, up, out):
    total = kept[0].astype(f32) + got[0].astype(f32)
    tall, few = down.shape[0] // GROUPS, out.shape[0] // GROUPS
    ups = []
    for g in range(GROUPS):
        row = g * (2 * tall + few)
        down[g * tall : (g + 1) * tall, :] = total[row : row + tall]
        ups.append(total[row + tall : row + 2 * tall])
        out[g * few : (g + 1) * few, :] = total[row + 2 * tall : row + 2 * tall + few]
    up[...] = jnp.concatenate(ups, axis=0).T


def feed_end(kept, got, tall, few):
    width = kept.shape[2]
    return pl.pallas_call(
        feed_end_kernel,
        in_specs=[IN_VMEM] * 2,
        out_specs=[IN_VMEM] * 3,
        out_shape=[shape((tall, width), f32), shape((width, tall), f32), shape((few, width), f32)],
        compiler_params=params(16),
        cost_estimate=COST,
        name="feed_end",
    )(kept, got)


def qkv_end_kernel(places, rides, gain_line, kept, got, *refs):
    out, gain1, gain2, rms = refs[-4:]
    tall = out.shape[0]
    width = gain1.shape[0]
    cols = kept.shape[2]
    there = got[: kept.shape[1]] if rides else got[0]
    total = kept[0].astype(f32) + there.astype(f32)
    for i, at in enumerate(places):
        out[:, at : at + cols] = total[i * tall : (i + 1) * tall]
    if rides:
        sums = refs[0][...] + got_sums(got[kept.shape[1] :])
        sums = jnp.concatenate([sums[r : r + SUMS] for r in range(0, sums.shape[0], SUMS)], axis=1)
    else:
        sums = refs[0][...] + refs[1][...]
    gain2[...] = sums[3:4, :].reshape(width)
    gain1[...] = (sums[4:5, :] / gain_line[...].reshape(1, width)).reshape(width)
    count = jnp.max(sums[5:6, :], axis=1, keepdims=True) * width
    rms[...] = jnp.broadcast_to(jnp.sqrt(jnp.sum(sums, axis=1, keepdims=True) / count), rms.shape)


def qkv_end(places, gain, kept, got, small, tall, wide, rides):
    return pl.pallas_call(
        functools.partial(qkv_end_kernel, places, rides),
        in_specs=[IN_VMEM] * (3 + len(small)),
        out_specs=[IN_VMEM] * 4,
        out_shape=[shape((tall, wide), f32), shape(gain.shape, f32), shape(gain.shape, f32), shape((SUMS, 128), f32)],
        compiler_params=params(16),
        cost_estimate=COST,
        name="qkv_end",
    )(gain, kept, got, *small)


def after(value, *earlier):
    return lax.optimization_barrier((value, earlier))[0]


def sum_parts(me, kept, got, sources, width, small, rides):
    orders = bit_orders(lax.axis_size("batch"), len(sources))
    steps = len(orders[0])
    common = min(i for i in range(steps + 1) if all(order[i:] == orders[0][i:] for order in orders))
    keep, send, small = start_sum(me, kept, got, sources, width, orders, small, rides)
    for i in range(steps):
        got = [exchange(s, "batch", order[i]) for s, order in zip(send, orders[: len(send)], strict=True)]
        if small and not rides:
            small = [small[0], exchange(small[0], "batch", orders[0][i])]
        earlier = yield send[0], got
        if i == steps - 1:
            break
        if earlier is not None:
            keep = after(keep, earlier)
        keep, send, small = step_sum(keep, got, small, i + 1 == common, rides)
    yield keep[0], got[0], small


def on_device(
    inputs, lengths, cotangent, qkv_weight, out_weight, up_weight, down_weight, attn_gain, mlp_gain
):
    seq, width = inputs.shape[2:]
    x = inputs[0, 0]
    dy = cotangent[0, 0]
    count = lax.axis_size("batch")
    stream = lax.axis_index("stream").astype(jnp.int32)
    me = lax.axis_index("batch").astype(jnp.int32).reshape(1)
    info = jnp.stack([stream, lengths[0]])
    cosine, sine = rotary_tables(seq)
    tables_t = (jnp.asarray(cosine.T), jnp.asarray(sine.T))

    received = lax.ppermute(x, "stream", [(0, 1)])
    (
        q, ko, vo, kc, vc, h1t, o, lse, outputs, dx2, do,
        up_send, up_keep, down_send, down_keep, out_send, out_keep, *tables, sums,
    ) = layer(
        info, attn_gain, mlp_gain, *tables_t, received, x, qkv_weight, out_weight, dy, up_weight, down_weight
    )
    down_got, up_got, out_got = (exchange(a, "stream", 1) for a in (down_send, up_send, out_send))

    def by_rows(array):
        return array.reshape(count * GROUPS, array.shape[0] // (count * GROUPS), width)

    heads = (q, ko, vo, kc, vc, o)
    pairs = width // PW // 3
    dq1, keep1, send1 = attend_back(info, 0, pairs, *heads, do, lse, *tables_t)
    got1 = lax.ppermute(send1, "stream", [(1, 0)])
    early = sum_parts(
        me,
        [by_rows(after(a, dq1)) for a in (down_keep, up_keep, out_keep)],
        [by_rows(a) for a in (down_got, up_got, out_got)],
        [[(a, lambda part, g=g: part * GROUPS + g, 0) for a in range(3)] for g in range(GROUPS)],
        width,
        [],
        False,
    )
    token = next(early)[0]
    dq2, keep2, send2 = attend_back(info, pairs, 2 * pairs, *heads, after(do, token), lse, *tables_t)
    got2 = lax.ppermute(send2, "stream", [(1, 0)])
    token = early.send(dq2)[0]
    dkv1, qkv_send1, qkv_keep1, small = weigh(info, 0, dq1, after(keep1, token), got1, tables, h1t, qkv_weight, sums)
    qkv_got1 = exchange(qkv_send1, "stream", 1)
    dkv2, qkv_send2, qkv_keep2, small = weigh(info, pairs, dq2, keep2, got2, tables, h1t, qkv_weight, small)
    qkv_got2 = exchange(qkv_send2, "stream", 1)
    small_got = exchange(small, "stream", 1)
    token = early.send(dkv2)[0]

    tall = width // (2 * count)
    split = lambda a: a.reshape(3 * count, tall, a.shape[2])
    rides = tall % 8 == 0
    runs = [(0, i, 0) for i in range(3)] + [(1, i, c) for i in range(3) for c in range(2)]
    groups = runs[:4], runs[4:]
    late = sum_parts(
        me,
        [split(after(a, token)) for a in (qkv_keep1, qkv_keep2)],
        [split(a) for a in (qkv_got1, qkv_got2)],
        [[(a, lambda part, i=i: i * count + part, c) for a, i, c in group] for group in groups],
        pairs * PW,
        [small, small_got],
        rides,
    )
    token = next(late)[0]
    ends = [dq1, dq2], [dkv1, dkv2], qkv_weight, attn_gain
    tiles = seq // R
    dx = finish((0, tiles // 2), after(x, token), dx2, *ends, [])
    early_out = early.send(dx)
    dx = finish((tiles // 2, tiles), x, after(dx2, early_out[0]), *ends, [dx])
    late.send(dx)
    late_out = late.send(early_out[1])
    while len(late_out) == 2:
        late_out = late.send(None)
    while len(early_out) == 2:
        early_out = early.send(None)
    up_cols = down_keep.shape[0] // count
    down_grad, up_grad, out_grad = feed_end(*early_out[:2], up_cols, tall)
    places = [i * width + (a + c) * pairs * PW for a, i, c in runs]
    qkv_grad, gain1_grad, gain2_grad, rms = qkv_end(places, attn_gain, *late_out, tall, 3 * width, rides)
    return (
        outputs[None, None],
        dx[None, None],
        qkv_grad,
        out_grad,
        up_grad,
        down_grad,
        gain1_grad,
        gain2_grad,
        rms[:3, 0],
    )


def solution(mesh):
    rows = P("stream", "batch", None, None)
    both = ("stream", "batch")
    return jax.shard_map(
        on_device,
        mesh=mesh,
        in_specs=(rows, P("batch"), rows, P(), P(), P(), P(), P(), P()),
        out_specs=(rows, rows, P(both, None), P(both, None), P(None, both), P(both, None), P(), P(), P()),
        check_vma=False,
    )
```

profile of v0, /device:TPU:0, one launch (start us, length us, event | category | flops | bytes accessed | tf_op | source)
XLA Modules:
  0.0 178.3 jit_solution(7431384620228276818)
XLA Ops:
  0.6 2.5 %collective-permute-start = (bf16[1024,768]{1,0:T(8,128)(2,1)}, bf16[1024,768]{1,0:T(8,128)(2,1)S(1)}, u32[]{:S(2)}, u32[]{:S(2)}) collective-permute-start(bf16[1024,768]{1,0:T(8,128)(2,1)} %bitcast.20), channel_id=1, source_target_pairs={{0,16},{1,17},{2,18},{3,19},{4,20},{5,21},{6,22},{7,23},{8,24},{9,... | collective-permute-start | bytes 4718600 | tf_op jit(solution)/shard_map/ppermute | solution.py:924
  4.3 1.9 %collective-permute-done.received = bf16[1024,768]{1,0:T(8,128)(2,1)S(1)} collective-permute-done((bf16[1024,768]{1,0:T(8,128)(2,1)}, bf16[1024,768]{1,0:T(8,128)(2,1)S(1)}, u32[]{:S(2)}, u32[]{:S(2)}) %collective-permute-start) | collective-permute-done | bytes 1572896 | tf_op jit(solution)/shard_map/ppermute | solution.py:924
  6.2 1.1 copy-done.15
  7.4 70.9 %layer.1 = (bf16[6,1024,128]{2,1,0:T(8,128)(2,1)}, bf16[6,1024,128]{2,1,0:T(8,128)(2,1)}, bf16[6,1024,128]{2,1,0:T(8,128)(2,1)}, bf16[6,1024,128]{2,1,0:T(8,128)...) custom-call(s32[2]{0:T(128)} %pad_add_fusion.info, ...), custom_call_target="tpu_custom_call" | custom-call | flops 34359738368 | bytes 67108864 | tf_op jit(solution)/shard_map/layer/pallas_call | solution.py:555
  80.1 10.1 %attend_back.2 = (bf16[1024,256]{1,0:T(8,128)(2,1)S(1)}, bf16[2,1024,256]{2,1,0:T(8,128)(2,1)S(1)}, bf16[2,1024,256]{2,1,0:T(8,128)(2,1)S(1)}) custom-call(s32[2]{0:T(128)S(1)} %copy-done.9, bf16[6,1024,128]{2,1,0:T(8,128)(2,1)} %get-tuple-element.111.q, bf16[6,1024,128]{2,1,0:T(8,128)(2,1)} %get-tuple-element.112.ko, ...), custom_call_target="tpu_custom_call" | custom-call | flops 34359738368 | bytes 67108864 | tf_op jit(solution)/shard_map/attend_back/pallas_call | solution.py:282
  90.2 1.3 collective-permute-start.8
  91.5 3.9 %start_sum.2 = (bf16[8,72,768]{2,1,0:T(8,128)(2,1)S(1)}, bf16[8,72,768]{2,1,0:T(8,128)(2,1)S(1)}, bf16[8,72,768]{2,1,0:T(8,128)(2,1)S(1)}, bf16[8,72,768]{2,1,0:...) custom-call(s32[1]{0:T(128)} %bitcast.4.me, bf16[48,32,768]{2,1,0:T(8,128)(2,1)S(1)} %bitcast.17, ...), custom_call_target="tpu_custom_call" | custom-call | flops 1048576 | bytes 65536 | tf_op jit(solution)/shard_map/start_sum/pallas_call | solution.py:768
  95.5 2.4 %collective-permute-start.4 = (bf16[8,72,768]{2,1,0:T(8,128)(2,1)S(1)}, bf16[8,72,768]{2,1,0:T(8,128)(2,1)S(1)}, u32[]{:S(2)}, u32[]{:S(2)}) collective-permute-start(bf16[8,72,768]{2,1,0:T(8,128)(2,1)S(1)} %get-tuple-element.131), channel_id=1, source_target_pairs={{0,1},{1,0},{2,3},{3,2},{4,5},{5,4},{6,7},{7,6},{8,9},{9,8},{10,11... | collective-permute-start | bytes 2654216 | tf_op jit(solution)/shard_map/ppermute | solution.py:670
  97.9 1.5 collective-permute-start.5
  99.4 1.6 collective-permute-start.6
  101.0 18.0 %attend_back.3 = (bf16[1024,512]{1,0:T(8,128)(2,1)S(1)}, bf16[2,1024,512]{2,1,0:T(8,128)(2,1)S(1)}, bf16[2,1024,512]{2,1,0:T(8,128)(2,1)S(1)}) custom-call(s32[2]{0:T(128)S(1)} %copy-done.9, bf16[6,1024,128]{2,1,0:T(8,128)(2,1)} %get-tuple-element.111.q, bf16[6,1024,128]{2,1,0:T(8,128)(2,1)} %get-tuple-element.112.ko, ...), custom_call_target="tpu_custom_call" | custom-call | flops 34359738368 | bytes 67108864 | tf_op jit(solution)/shard_map/attend_back/pallas_call | solution.py:282
  119.0 1.6 collective-permute-start.7
  120.6 1.0 collective-permute-done.6.refs_5_
  122.8 1.6 collective-permute-start.10
  124.9 2.4 %weigh.2 = (bf16[2,1024,256]{2,1,0:T(8,128)(2,1)S(1)}, bf16[3,384,256]{2,1,0:T(8,128)(2,1)S(1)}, bf16[3,384,256]{2,1,0:T(8,128)(2,1)S(1)}, f32[8,768]{1,0:T(8,128)S(1)}) custom-call(s32[2]{0:T(128)S(1)} %copy-done.9, bf16[1024,256]{1,0:T(8,128)(2,1)S(1)} %get-tuple-element.119.dq.refs_0_, bf16[2,1024,256]{2,1,0:T(8,128)(2,1)S(1)} %get-tuple-element.149.keep, ...), custom_call_target="tpu_custom_call" | custom-call | flops 34359738368 | bytes 67108864 | tf_op jit(solution)/shard_map/weigh/pallas_call | solution.py:609
  127.4 3.9 %weigh.3 = (bf16[2,1024,512]{2,1,0:T(8,128)(2,1)S(1)}, bf16[3,384,512]{2,1,0:T(8,128)(2,1)S(1)}, bf16[3,384,512]{2,1,0:T(8,128)(2,1)S(1)}, f32[8,768]{1,0:T(8,128)S(1)}) custom-call(s32[2]{0:T(128)S(1)} %copy-done.9, bf16[1024,512]{1,0:T(8,128)(2,1)S(1)} %get-tuple-element.133.dq.refs_1_, bf16[2,1024,512]{2,1,0:T(8,128)(2,1)S(1)} %get-tuple-element.142.keep, ...), custom_call_target="tpu_custom_call" | custom-call | flops 34359738368 | bytes 67108864 | tf_op jit(solution)/shard_map/weigh/pallas_call | solution.py:609
  131.8 3.5 %collective-permute-done.10.refs_4_ = bf16[4,72,768]{2,1,0:T(8,128)(2,1)S(1)} collective-permute-done((bf16[4,72,768]{2,1,0:T(8,128)(2,1)S(1)}, bf16[4,72,768]{2,1,0:T(8,128)(2,1)S(1)}, u32[]{:S(2)}, u32[]{:S(2)}) %collective-permute-start.10) | collective-permute-done | bytes 442400 | tf_op jit(solution)/shard_map/ppermute | solution.py:670
  136.0 1.4 collective-permute-start.15
  137.9 1.5 collective-permute-start.17
  140.3 1.5 collective-permute-start.18
  142.3 3.5 %finish.2.refs_4_ = bf16[1024,768]{1,0:T(8,128)(2,1)} custom-call(bf16[1024,768]{1,0:T(8,128)(2,1)S(1)} %bitcast.22, f32[1024,768]{1,0:T(8,128)S(1)} %copy-done.1, bf16[768,2304]{1,0:T(8,128)(2,1)S(1)} %copy-done, f32[768]{0:T(1024)S(1)} %copy-done.6, bf16[1024,256]{1,0:T(8,128)(2,1)S(1)} %get-tuple-element.119.dq.refs_0_, ...), custom_call_target="tpu_custom_call" | custom-call | flops 34359738368 | bytes 67108864 | tf_op jit(solution)/shard_map/finish/pallas_call | solution.py:648
  146.1 2.7 %collective-permute-start.20 = (bf16[1,216,768]{2,1,0:T(8,128)(2,1)S(1)}, bf16[1,216,768]{2,1,0:T(8,128)(2,1)S(1)}, u32[]{:S(2)}, u32[]{:S(2)}) collective-permute-start(bf16[1,216,768]{2,1,0:T(8,128)(2,1)S(1)} %get-tuple-element.178), channel_id=1, source_target_pairs={{0,8},{1,9},{2,10},{3,11},{4,12},{5,13},{6,14},{7,15},{8,0},{9,1},... | collective-permute-start | bytes 995336 | tf_op jit(solution)/shard_map/ppermute | solution.py:670
  148.7 3.5 %finish.3 = bf16[1024,768]{1,0:T(8,128)(2,1)} custom-call(bf16[1024,768]{1,0:T(8,128)(2,1)S(1)} %bitcast.23, f32[1024,768]{1,0:T(8,128)S(1)} %copy-done.1, bf16[768,2304]{1,0:T(8,128)(2,1)S(1)} %copy-done, f32[768]{0:T(1024)S(1)} %copy-done.6, bf16[1024,256]{1,0:T(8,128)(2,1)S(1)} %get-tuple-element.119.dq.refs_0_, ...), custom_call_target="tpu_custom_call", output_to_operand_aliasing={{}: (8, {})} | custom-call | flops 1048576 | bytes 65536 | tf_op jit(solution)/shard_map/finish/pallas_call | solution.py:648
  152.9 1.8 %collective-permute-done.19.refs_3_ = bf16[8,120,256]{2,1,0:T(8,128)(2,1)S(1)} collective-permute-done((bf16[8,120,256]{2,1,0:T(8,128)(2,1)S(1)}, bf16[8,120,256]{2,1,0:T(8,128)(2,1)S(1)}, u32[]{:S(2)}, u32[]{:S(2)}) %collective-permute-start.19) | collective-permute-done | bytes 491552 | tf_op jit(solution)/shard_map/ppermute | solution.py:670
  155.0 1.6 collective-permute-start.22
  156.5 1.5 collective-permute-start.21
  158.0 4.1 %collective-permute-done.20.got = bf16[1,216,768]{2,1,0:T(8,128)(2,1)S(1)} collective-permute-done((bf16[1,216,768]{2,1,0:T(8,128)(2,1)S(1)}, bf16[1,216,768]{2,1,0:T(8,128)(2,1)S(1)}, u32[]{:S(2)}, u32[]{:S(2)}) %collective-permute-start.20) | collective-permute-done | bytes 331808 | tf_op jit(solution)/shard_map/ppermute | solution.py:670
  162.6 1.4 collective-permute-start.23
  164.0 5.5 %collective-permute-done.23.refs_1_ = bf16[480,256]{1,0:T(8,128)(2,1)S(1)} collective-permute-done((bf16[480,256]{1,0:T(8,128)(2,1)S(1)}, bf16[480,256]{1,0:T(8,128)(2,1)S(1)}, u32[]{:S(2)}, u32[]{:S(2)}) %collective-permute-start.23) | collective-permute-done | bytes 245792 | tf_op jit(solution)/shard_map/ppermute | solution.py:670
  169.5 2.4 %collective-permute-start.24 = (bf16[264,256]{1,0:T(8,128)(2,1)S(1)}, bf16[264,256]{1,0:T(8,128)(2,1)S(1)}, u32[]{:S(2)}, u32[]{:S(2)}) collective-permute-start(bf16[264,256]{1,0:T(8,128)(2,1)S(1)} %get-tuple-element.197), channel_id=1, source_target_pairs={{0,8},{1,9},{2,10},{3,11},{4,12},{5,13},{6,14},{7,15},{8,0},{9,1},... | collective-permute-start | bytes 405512 | tf_op jit(solution)/shard_map/ppermute | solution.py:670
  171.9 0.9 feed_end.1
  173.7 3.3 %collective-permute-done.24.got = bf16[264,256]{1,0:T(8,128)(2,1)S(1)} collective-permute-done((bf16[264,256]{1,0:T(8,128)(2,1)S(1)}, bf16[264,256]{1,0:T(8,128)(2,1)S(1)}, u32[]{:S(2)}, u32[]{:S(2)}) %collective-permute-start.24) | collective-permute-done | bytes 135200 | tf_op jit(solution)/shard_map/ppermute | solution.py:670
  (70 shorter events, 11.1 us)
Async XLA Ops:
  0.6 5.6 %collective-permute-start = (bf16[1024,768]{1,0:T(8,128)(2,1)}, bf16[1024,768]{1,0:T(8,128)(2,1)S(1)}, u32[]{:S(2)}, u32[]{:S(2)}) collective-permute-start(bf16[1024,768]{1,0:T(8,128)(2,1)} %bitcast.20), channel_id=1, source_target_pairs={{0,16},{1,17},{2,18},{3,19},{4,20},{5,21},{6,22},{7,23},{8,24},{9,... | collective-permute-start | bytes 4718600 | tf_op jit(solution)/shard_map/ppermute | solution.py:924
  7.4 71.9 %copy-start.7 = (f32[32,1024]{1,0:T(8,128)S(1)}, f32[32,1024]{1,0:T(8,128)}, u32[]{:S(2)}) copy-start(f32[32,1024]{1,0:T(8,128)} %constant.14.clone.sine_t.sine) | copy-start | bytes 393220
  7.4 71.9 %copy-start.8 = (f32[32,1024]{1,0:T(8,128)S(1)}, f32[32,1024]{1,0:T(8,128)}, u32[]{:S(2)}) copy-start(f32[32,1024]{1,0:T(8,128)} %constant.13.clone.cosine_t.cosine) | copy-start | bytes 393220
  7.4 71.9 %copy-start.9 = (s32[2]{0:T(128)S(1)}, s32[2]{0:T(128)}, u32[]{:S(2)}) copy-start(s32[2]{0:T(128)} %pad_add_fusion.info) | copy-start | bytes 28
  78.3 13.2 %collective-permute-start.3 = (bf16[384,768]{1,0:T(8,128)(2,1)}, bf16[384,768]{1,0:T(8,128)(2,1)S(1)}, u32[]{:S(2)}, u32[]{:S(2)}) collective-permute-start(bf16[384,768]{1,0:T(8,128)(2,1)} %get-tuple-element.127), channel_id=1, source_target_pairs={{0,16},{16,0},{1,17},{17,1},{2,18},{18,2},{3,19},{19,3},{4,20},{20... | collective-permute-start | bytes 1769480 | tf_op jit(solution)/shard_map/ppermute | solution.py:670
  78.8 12.7 %collective-permute-start.1 = (bf16[1536,768]{1,0:T(8,128)(2,1)}, bf16[1536,768]{1,0:T(8,128)(2,1)S(1)}, u32[]{:S(2)}, u32[]{:S(2)}) collective-permute-start(bf16[1536,768]{1,0:T(8,128)(2,1)} %get-tuple-element.121), channel_id=1, source_target_pairs={{0,16},{16,0},{1,17},{17,1},{2,18},{18,2},{3,19},{19,3},{4,20},{20... | collective-permute-start | bytes 7077896 | tf_op jit(solution)/shard_map/ppermute | solution.py:670
  78.9 12.6 %collective-permute-start.2 = (bf16[1536,768]{1,0:T(8,128)(2,1)}, bf16[1536,768]{1,0:T(8,128)(2,1)S(1)}, u32[]{:S(2)}, u32[]{:S(2)}) collective-permute-start(bf16[1536,768]{1,0:T(8,128)(2,1)} %get-tuple-element.124), channel_id=1, source_target_pairs={{0,16},{16,0},{1,17},{17,1},{2,18},{18,2},{3,19},{19,3},{4,20},{20... | collective-permute-start | bytes 7077896 | tf_op jit(solution)/shard_map/ppermute | solution.py:670
  80.1 11.4 %copy-start.2 = (bf16[1536,768]{1,0:T(8,128)(2,1)S(1)}, bf16[1536,768]{1,0:T(8,128)(2,1)}, u32[]{:S(2)}) copy-start(bf16[1536,768]{1,0:T(8,128)(2,1)} %get-tuple-element.123) | copy-start | bytes 7077892
  80.1 11.4 %copy-start.3 = (bf16[1536,768]{1,0:T(8,128)(2,1)S(1)}, bf16[1536,768]{1,0:T(8,128)(2,1)}, u32[]{:S(2)}) copy-start(bf16[1536,768]{1,0:T(8,128)(2,1)} %get-tuple-element.120) | copy-start | bytes 7077892
  80.1 11.5 %copy-start.5 = (bf16[384,768]{1,0:T(8,128)(2,1)S(1)}, bf16[384,768]{1,0:T(8,128)(2,1)}, u32[]{:S(2)}) copy-start(bf16[384,768]{1,0:T(8,128)(2,1)} %get-tuple-element.126) | copy-start | bytes 1769476
  90.2 34.7 %collective-permute-start.8 = (bf16[2,1024,256]{2,1,0:T(8,128)(2,1)S(1)}, bf16[2,1024,256]{2,1,0:T(8,128)(2,1)S(1)}, u32[]{:S(2)}, u32[]{:S(2)}) collective-permute-start(bf16[2,1024,256]{2,1,0:T(8,128)(2,1)S(1)} %get-tuple-element.150), channel_id=1, source_target_pairs={{16,0},{17,1},{18,2},{19,3},{20,4},{21,5},{22,6},{23,7},{24,8},{25... | collective-permute-start | bytes 3145736 | tf_op jit(solution)/shard_map/ppermute | solution.py:939
  95.5 26.1 %collective-permute-start.4 = (bf16[8,72,768]{2,1,0:T(8,128)(2,1)S(1)}, bf16[8,72,768]{2,1,0:T(8,128)(2,1)S(1)}, u32[]{:S(2)}, u32[]{:S(2)}) collective-permute-start(bf16[8,72,768]{2,1,0:T(8,128)(2,1)S(1)} %get-tuple-element.131), channel_id=1, source_target_pairs={{0,1},{1,0},{2,3},{3,2},{4,5},{5,4},{6,7},{7,6},{8,9},{9,8},{10,11... | collective-permute-start | bytes 2654216 | tf_op jit(solution)/shard_map/ppermute | solution.py:670
  97.9 22.7 %collective-permute-start.5 = (bf16[8,72,768]{2,1,0:T(8,128)(2,1)S(1)}, bf16[8,72,768]{2,1,0:T(8,128)(2,1)S(1)}, u32[]{:S(2)}, u32[]{:S(2)}) collective-permute-start(bf16[8,72,768]{2,1,0:T(8,128)(2,1)S(1)} %get-tuple-element.137), channel_id=1, source_target_pairs={{0,2},{1,3},{2,0},{3,1},{4,6},{5,7},{6,4},{7,5},{8,10},{9,11},{10,... | collective-permute-start | bytes 2654216 | tf_op jit(solution)/shard_map/ppermute | solution.py:670
  99.4 22.2 %collective-permute-start.6 = (bf16[8,72,768]{2,1,0:T(8,128)(2,1)S(1)}, bf16[8,72,768]{2,1,0:T(8,128)(2,1)S(1)}, u32[]{:S(2)}, u32[]{:S(2)}) collective-permute-start(bf16[8,72,768]{2,1,0:T(8,128)(2,1)S(1)} %get-tuple-element.138), channel_id=1, source_target_pairs={{0,4},{1,5},{2,6},{3,7},{4,0},{5,1},{6,2},{7,3},{8,12},{9,13},{10,... | collective-permute-start | bytes 2654216 | tf_op jit(solution)/shard_map/ppermute | solution.py:670
  119.0 8.4 %collective-permute-start.7 = (bf16[2,1024,512]{2,1,0:T(8,128)(2,1)S(1)}, bf16[2,1024,512]{2,1,0:T(8,128)(2,1)S(1)}, u32[]{:S(2)}, u32[]{:S(2)}) collective-permute-start(bf16[2,1024,512]{2,1,0:T(8,128)(2,1)S(1)} %get-tuple-element.143), channel_id=1, source_target_pairs={{16,0},{17,1},{18,2},{19,3},{20,4},{21,5},{22,6},{23,7},{24,8},{25... | collective-permute-start | bytes 6291464 | tf_op jit(solution)/shard_map/ppermute | solution.py:951
  122.2 13.5 %collective-permute-start.9 = (bf16[4,72,768]{2,1,0:T(8,128)(2,1)S(1)}, bf16[4,72,768]{2,1,0:T(8,128)(2,1)S(1)}, u32[]{:S(2)}, u32[]{:S(2)}) collective-permute-start(bf16[4,72,768]{2,1,0:T(8,128)(2,1)S(1)} %get-tuple-element.148), channel_id=1, source_target_pairs={{0,2},{1,3},{2,0},{3,1},{4,6},{5,7},{6,4},{7,5},{8,10},{9,11},{10,... | collective-permute-start | bytes 1327112 | tf_op jit(solution)/shard_map/ppermute | solution.py:670
  122.8 12.5 %collective-permute-start.10 = (bf16[4,72,768]{2,1,0:T(8,128)(2,1)S(1)}, bf16[4,72,768]{2,1,0:T(8,128)(2,1)S(1)}, u32[]{:S(2)}, u32[]{:S(2)}) collective-permute-start(bf16[4,72,768]{2,1,0:T(8,128)(2,1)S(1)} %get-tuple-element.157), channel_id=1, source_target_pairs={{0,4},{1,5},{2,6},{3,7},{4,0},{5,1},{6,2},{7,3},{8,12},{9,13},{10,... | collective-permute-start | bytes 1327112 | tf_op jit(solution)/shard_map/ppermute | solution.py:670
  124.4 11.3 %collective-permute-start.11 = (bf16[4,72,768]{2,1,0:T(8,128)(2,1)S(1)}, bf16[4,72,768]{2,1,0:T(8,128)(2,1)S(1)}, u32[]{:S(2)}, u32[]{:S(2)}) collective-permute-start(bf16[4,72,768]{2,1,0:T(8,128)(2,1)S(1)} %get-tuple-element.158), channel_id=1, source_target_pairs={{0,1},{1,0},{2,3},{3,2},{4,5},{5,4},{6,7},{7,6},{8,9},{9,8},{10,11... | collective-permute-start | bytes 1327112 | tf_op jit(solution)/shard_map/ppermute | solution.py:670
  127.3 10.6 %collective-permute-start.12 = (bf16[3,384,256]{2,1,0:T(8,128)(2,1)S(1)}, bf16[3,384,256]{2,1,0:T(8,128)(2,1)S(1)}, u32[]{:S(2)}, u32[]{:S(2)}) collective-permute-start(bf16[3,384,256]{2,1,0:T(8,128)(2,1)S(1)} %get-tuple-element.165), channel_id=1, source_target_pairs={{0,16},{16,0},{1,17},{17,1},{2,18},{18,2},{3,19},{19,3},{4,20},{20... | collective-permute-start | bytes 1769480 | tf_op jit(solution)/shard_map/ppermute | solution.py:670
  131.3 8.2 %collective-permute-start.14 = (f32[8,768]{1,0:T(8,128)S(1)}, f32[8,768]{1,0:T(8,128)S(1)}, u32[]{:S(2)}, u32[]{:S(2)}) collective-permute-start(f32[8,768]{1,0:T(8,128)S(1)} %get-tuple-element.169.refs_4_), channel_id=1, source_target_pairs={{0,16},{16,0},{1,17},{17,1},{2,18},{18,2},{3,19},{19,3},{4,20},{20... | collective-permute-start | bytes 73736 | tf_op jit(solution)/shard_map/ppermute | solution.py:670
  135.3 4.2 %collective-permute-start.13 = (bf16[3,384,512]{2,1,0:T(8,128)(2,1)S(1)}, bf16[3,384,512]{2,1,0:T(8,128)(2,1)S(1)}, u32[]{:S(2)}, u32[]{:S(2)}) collective-permute-start(bf16[3,384,512]{2,1,0:T(8,128)(2,1)S(1)} %get-tuple-element.168), channel_id=1, source_target_pairs={{0,16},{16,0},{1,17},{17,1},{2,18},{18,2},{3,19},{19,3},{4,20},{20... | collective-permute-start | bytes 3538952 | tf_op jit(solution)/shard_map/ppermute | solution.py:670
  135.7 6.6 %copy-start.4 = (bf16[1,1,1024,768]{3,2,1,0:T(8,128)(2,1)S(1)}, bf16[1,1,1024,768]{3,2,1,0:T(8,128)(2,1)}, u32[]{:S(2)}) copy-start(bf16[1,1,1024,768]{3,2,1,0:T(8,128)(2,1)} %param.11) | copy-start | bytes 4718596
  136.0 9.8 %collective-permute-start.15 = (bf16[2,72,768]{2,1,0:T(8,128)(2,1)S(1)}, bf16[2,72,768]{2,1,0:T(8,128)(2,1)S(1)}, u32[]{:S(2)}, u32[]{:S(2)}) collective-permute-start(bf16[2,72,768]{2,1,0:T(8,128)(2,1)S(1)} %get-tuple-element.163), channel_id=1, source_target_pairs={{0,4},{1,5},{2,6},{3,7},{4,0},{5,1},{6,2},{7,3},{8,12},{9,13},{10,... | collective-permute-start | bytes 663560 | tf_op jit(solution)/shard_map/ppermute | solution.py:670
  137.4 8.4 %collective-permute-start.16 = (bf16[2,72,768]{2,1,0:T(8,128)(2,1)S(1)}, bf16[2,72,768]{2,1,0:T(8,128)(2,1)S(1)}, u32[]{:S(2)}, u32[]{:S(2)}) collective-permute-start(bf16[2,72,768]{2,1,0:T(8,128)(2,1)S(1)} %get-tuple-element.176), channel_id=1, source_target_pairs={{0,1},{1,0},{2,3},{3,2},{4,5},{5,4},{6,7},{7,6},{8,9},{9,8},{10,11... | collective-permute-start | bytes 663560 | tf_op jit(solution)/shard_map/ppermute | solution.py:670
  137.9 7.9 %collective-permute-start.17 = (bf16[2,72,768]{2,1,0:T(8,128)(2,1)S(1)}, bf16[2,72,768]{2,1,0:T(8,128)(2,1)S(1)}, u32[]{:S(2)}, u32[]{:S(2)}) collective-permute-start(bf16[2,72,768]{2,1,0:T(8,128)(2,1)S(1)} %get-tuple-element.177), channel_id=1, source_target_pairs={{0,2},{1,3},{2,0},{3,1},{4,6},{5,7},{6,4},{7,5},{8,10},{9,11},{10,... | collective-permute-start | bytes 663560 | tf_op jit(solution)/shard_map/ppermute | solution.py:670
  140.3 12.7 %collective-permute-start.18 = (bf16[816,256]{1,0:T(8,128)(2,1)S(1)}, bf16[816,256]{1,0:T(8,128)(2,1)S(1)}, u32[]{:S(2)}, u32[]{:S(2)}) collective-permute-start(bf16[816,256]{1,0:T(8,128)(2,1)S(1)} %get-tuple-element.170), channel_id=1, source_target_pairs={{0,1},{1,0},{2,3},{3,2},{4,5},{5,4},{6,7},{7,6},{8,9},{9,8},{10,11... | collective-permute-start | bytes 1253384 | tf_op jit(solution)/shard_map/ppermute | solution.py:670
  141.8 13.0 %collective-permute-start.19 = (bf16[8,120,256]{2,1,0:T(8,128)(2,1)S(1)}, bf16[8,120,256]{2,1,0:T(8,128)(2,1)S(1)}, u32[]{:S(2)}, u32[]{:S(2)}) collective-permute-start(bf16[8,120,256]{2,1,0:T(8,128)(2,1)S(1)} %get-tuple-element.184), channel_id=1, source_target_pairs={{0,2},{1,3},{2,0},{3,1},{4,6},{5,7},{6,4},{7,5},{8,10},{9,11},{10,... | collective-permute-start | bytes 1474568 | tf_op jit(solution)/shard_map/ppermute | solution.py:670
  146.1 16.0 %collective-permute-start.20 = (bf16[1,216,768]{2,1,0:T(8,128)(2,1)S(1)}, bf16[1,216,768]{2,1,0:T(8,128)(2,1)S(1)}, u32[]{:S(2)}, u32[]{:S(2)}) collective-permute-start(bf16[1,216,768]{2,1,0:T(8,128)(2,1)S(1)} %get-tuple-element.178), channel_id=1, source_target_pairs={{0,8},{1,9},{2,10},{3,11},{4,12},{5,13},{6,14},{7,15},{8,0},{9,1},... | collective-permute-start | bytes 995336 | tf_op jit(solution)/shard_map/ppermute | solution.py:670
  155.0 7.5 %collective-permute-start.22 = (bf16[4,120,256]{2,1,0:T(8,128)(2,1)S(1)}, bf16[4,120,256]{2,1,0:T(8,128)(2,1)S(1)}, u32[]{:S(2)}, u32[]{:S(2)}) collective-permute-start(bf16[4,120,256]{2,1,0:T(8,128)(2,1)S(1)} %get-tuple-element.191), channel_id=1, source_target_pairs={{0,1},{1,0},{2,3},{3,2},{4,5},{5,4},{6,7},{7,6},{8,9},{9,8},{10,11... | collective-permute-start | bytes 737288 | tf_op jit(solution)/shard_map/ppermute | solution.py:670
  156.5 5.9 %collective-permute-start.21 = (bf16[432,256]{1,0:T(8,128)(2,1)S(1)}, bf16[432,256]{1,0:T(8,128)(2,1)S(1)}, u32[]{:S(2)}, u32[]{:S(2)}) collective-permute-start(bf16[432,256]{1,0:T(8,128)(2,1)S(1)} %get-tuple-element.190), channel_id=1, source_target_pairs={{0,2},{1,3},{2,0},{3,1},{4,6},{5,7},{6,4},{7,5},{8,10},{9,11},{10,... | collective-permute-start | bytes 663560 | tf_op jit(solution)/shard_map/ppermute | solution.py:670
  162.6 6.9 %collective-permute-start.23 = (bf16[480,256]{1,0:T(8,128)(2,1)S(1)}, bf16[480,256]{1,0:T(8,128)(2,1)S(1)}, u32[]{:S(2)}, u32[]{:S(2)}) collective-permute-start(bf16[480,256]{1,0:T(8,128)(2,1)S(1)} %get-tuple-element.194), channel_id=1, source_target_pairs={{0,4},{1,5},{2,6},{3,7},{4,0},{5,1},{6,2},{7,3},{8,12},{9,13},{10,... | collective-permute-start | bytes 737288 | tf_op jit(solution)/shard_map/ppermute | solution.py:670
  169.5 7.4 %collective-permute-start.24 = (bf16[264,256]{1,0:T(8,128)(2,1)S(1)}, bf16[264,256]{1,0:T(8,128)(2,1)S(1)}, u32[]{:S(2)}, u32[]{:S(2)}) collective-permute-start(bf16[264,256]{1,0:T(8,128)(2,1)S(1)} %get-tuple-element.197), channel_id=1, source_target_pairs={{0,8},{1,9},{2,10},{3,11},{4,12},{5,13},{6,14},{7,15},{8,0},{9,1},... | collective-permute-start | bytes 405512 | tf_op jit(solution)/shard_map/ppermute | solution.py:670
  (9 other events, 37.3 us)
where the time goes:
time: 179 us; the launch traced here: 178 us
  Pallas kernels  120 us (67%)
  starting transfers between devices  30 us (17%)
  waiting for transfers between devices  22.5 us (13%)
  local copies, waits for them, and re-layouts  3.49 us (2%)
    pallas_call x1, Pallas kernels, layer(): pl.pallas_call(layer_kernel, in_specs=[SMEM] + [IN_VMEM] * 5 + [anywhere]...  70.9 us
    pallas_call x2, Pallas kernels, attend_back(): pl.pallas_call(attend_back_kernel, grid=(pairs,), in_specs=[SMEM] + [head...  28.1 us
    ppermute x22, starting transfers between devices, exchange(): return lax.ppermute(value, axis, [(i, i ^ bit) for i in range(size)])  24.7 us
    ppermute x22, waiting for transfers between devices, exchange(): return lax.ppermute(value, axis, [(i, i ^ bit) for i in range(size)])  20.6 us
    pallas_call x2, Pallas kernels, finish(): pl.pallas_call(functools.partial(finish_kernel, len(dqs), tiles), in_spec...  7.04 us
    pallas_call x2, Pallas kernels, weigh(): pl.pallas_call(functools.partial(weigh_kernel, first), in_specs=[SMEM] +...  6.26 us
    pallas_call x2, Pallas kernels, start_sum(): pl.pallas_call(functools.partial(start_kernel, orders, sources, mode), co...  4.67 us
  transfers between devices with their start and end apart: 25, of which 10 were waited for; matrix products, arithmetic and copies ran while one was open for 1% of the time, Pallas kernels for 27%

commit v1 on v0

--- a/solution.py
+++ b/solution.py
@@ -21,7 +21,7 @@
 AHEAD = 2
 FC = 768
 SCALE = HD**-0.5
-BIG = 61
+BIG = 58
 GROUPS = 3
 
 COST = pl.CostEstimate(flops=1 << 20, bytes_accessed=1 << 16, transcendentals=0)
@@ -88,14 +88,16 @@
     return outs[0] if len(outs) == 1 else jnp.concatenate(outs, axis=1)
 
 
-def in_turn(count, *stages):
-    def turn(t, carry):
-        state = ()
-        for stage in stages:
-            state = stage(t, *state)
+def in_turn(count, *stages, at_once=1):
+    def turn(n, carry):
+        state = [()] * at_once
+        for step in range(at_once + len(stages) - 1):
+            for k, stage in enumerate(stages):
+                if 0 <= step - k < at_once:
+                    state[step - k] = stage(at_once * n + step - k, *state[step - k])
         return carry
 
-    lax.fori_loop(0, count, turn, 0)
+    lax.fori_loop(0, count // at_once, turn, 0)
 
 
 def token_weight(start, length, rows):
@@ -433,7 +435,7 @@
         sums[1:2, :] += row_sum(jnp.where(weight, branch * branch, 0.0))
         return ()
 
-    in_turn(tiles, join_product, join_norm)
+    in_turn(tiles, join_product, join_norm, at_once=2)
 
     def grad_stores(c, up, down):
         slot = lax.rem(c, 2)
@@ -517,7 +519,7 @@
             store.start()
         return ()
 
-    in_turn(tiles, middle_norm, middle_product)
+    in_turn(tiles, middle_norm, middle_product, at_once=2)
     half = width // 2
     mine = pl.multiple_of(noisy * half, half)
     half_grads[0] = nn(o_t[pl.ds(half - mine, half), :], x[...]).astype(bf16)
@@ -936,7 +938,6 @@
     heads = (q, ko, vo, kc, vc, o)
     pairs = width // PW // 3
     dq1, keep1, send1 = attend_back(info, 0, pairs, *heads, do, lse, *tables_t)
-    got1 = lax.ppermute(send1, "stream", [(1, 0)])
     early = sum_parts(
         me,
         [by_rows(after(a, dq1)) for a in (down_keep, up_keep, out_keep)],
@@ -947,6 +948,7 @@
         False,
     )
     token = next(early)[0]
+    got1 = lax.ppermute(after(send1, token), "stream", [(1, 0)])
     dq2, keep2, send2 = attend_back(info, pairs, 2 * pairs, *heads, after(do, token), lse, *tables_t)
     got2 = lax.ppermute(send2, "stream", [(1, 0)])
     token = early.send(dq2)[0]

time: 179 us -> 178 us (level)
  waiting for transfers between devices: 22.5 us -> 25.3 us
  starting transfers between devices: 30 us -> 27.8 us
    ppermute x22, waiting for transfers between devices: 20.6 us -> 23.4 us  [exchange(): return lax.ppermute(value, axis, [(i, i ^ bit) for i in range(size)])]
    ppermute x22, starting transfers between devices: 24.7 us -> 22.5 us  [exchange(): return lax.ppermute(value, axis, [(i, i ^ bit) for i in range(size)])]
  transfers between devices with their start and end apart: 25 -> 25, of which waited for: 10 -> 10; matrix products, arithmetic and copies ran while one was open for 1% -> 1% of each run, Pallas kernels for 27% -> 25%
where the time goes in v1:
time: 178 us
  Pallas kernels  119 us (67%)
  starting transfers between devices  27.8 us (16%)
  waiting for transfers between devices  25.3 us (14%)
  local copies, waits for them, and re-layouts  3.49 us (2%)
    pallas_call x1, Pallas kernels, layer(): pl.pallas_call(layer_kernel, in_specs=[SMEM] + [IN_VMEM] * 5 + [anywhere]...  70 us
    pallas_call x2, Pallas kernels, attend_back(): pl.pallas_call(attend_back_kernel, grid=(pairs,), in_specs=[SMEM] + [head...  28.1 us
    ppermute x22, waiting for transfers between devices, exchange(): return lax.ppermute(value, axis, [(i, i ^ bit) for i in range(size)])  23.4 us
    ppermute x22, starting transfers between devices, exchange(): return lax.ppermute(value, axis, [(i, i ^ bit) for i in range(size)])  22.5 us
    pallas_call x2, Pallas kernels, finish(): pl.pallas_call(functools.partial(finish_kernel, len(dqs), tiles), in_spec...  7.04 us
    pallas_call x2, Pallas kernels, weigh(): pl.pallas_call(functools.partial(weigh_kernel, first), in_specs=[SMEM] +...  6.3 us
    pallas_call x2, Pallas kernels, start_sum(): pl.pallas_call(functools.partial(start_kernel, orders, sources, mode), co...  4.67 us
  transfers between devices with their start and end apart: 25, of which 10 were waited for; matrix products, arithmetic and copies ran while one was open for 1% of the time, Pallas kernels for 25%

profile of v1, /device:TPU:0, one launch (start us, length us, event | category | flops | bytes accessed | tf_op | source)
XLA Modules:
  0.0 178.2 jit_solution(4033162297018557714)
XLA Ops:
  0.6 2.5 %collective-permute-start = (bf16[1024,768]{1,0:T(8,128)(2,1)}, bf16[1024,768]{1,0:T(8,128)(2,1)S(1)}, u32[]{:S(2)}, u32[]{:S(2)}) collective-permute-start(bf16[1024,768]{1,0:T(8,128)(2,1)} %bitcast.20), channel_id=1, source_target_pairs={{0,16},{1,17},{2,18},{3,19},{4,20},{5,21},{6,22},{7,23},{8,24},{9,... | collective-permute-start | bytes 4718600 | tf_op jit(solution)/shard_map/ppermute | solution.py:926
  4.3 1.9 %collective-permute-done.received = bf16[1024,768]{1,0:T(8,128)(2,1)S(1)} collective-permute-done((bf16[1024,768]{1,0:T(8,128)(2,1)}, bf16[1024,768]{1,0:T(8,128)(2,1)S(1)}, u32[]{:S(2)}, u32[]{:S(2)}) %collective-permute-start) | collective-permute-done | bytes 1572896 | tf_op jit(solution)/shard_map/ppermute | solution.py:926
  6.2 1.1 copy-done.15
  7.4 70.0 %layer.1 = (bf16[6,1024,128]{2,1,0:T(8,128)(2,1)}, bf16[6,1024,128]{2,1,0:T(8,128)(2,1)}, bf16[6,1024,128]{2,1,0:T(8,128)(2,1)}, bf16[6,1024,128]{2,1,0:T(8,128)...) custom-call(s32[2]{0:T(128)} %pad_add_fusion.info, ...), custom_call_target="tpu_custom_call" | custom-call | flops 34359738368 | bytes 67108864 | tf_op jit(solution)/shard_map/layer/pallas_call | solution.py:557
  79.1 10.1 %attend_back.2 = (bf16[1024,256]{1,0:T(8,128)(2,1)S(1)}, bf16[2,1024,256]{2,1,0:T(8,128)(2,1)S(1)}, bf16[2,1024,256]{2,1,0:T(8,128)(2,1)S(1)}) custom-call(s32[2]{0:T(128)S(1)} %copy-done.9, bf16[6,1024,128]{2,1,0:T(8,128)(2,1)} %get-tuple-element.112.q, bf16[6,1024,128]{2,1,0:T(8,128)(2,1)} %get-tuple-element.113.ko, ...), custom_call_target="tpu_custom_call" | custom-call | flops 34359738368 | bytes 67108864 | tf_op jit(solution)/shard_map/attend_back/pallas_call | solution.py:284
  89.3 3.9 %start_sum.2 = (bf16[8,72,768]{2,1,0:T(8,128)(2,1)S(1)}, bf16[8,72,768]{2,1,0:T(8,128)(2,1)S(1)}, bf16[8,72,768]{2,1,0:T(8,128)(2,1)S(1)}, bf16[8,72,768]{2,1,0:...) custom-call(s32[1]{0:T(128)} %bitcast.4.me, bf16[48,32,768]{2,1,0:T(8,128)(2,1)S(1)} %bitcast.17, ...), custom_call_target="tpu_custom_call" | custom-call | flops 1048576 | bytes 65536 | tf_op jit(solution)/shard_map/start_sum/pallas_call | solution.py:770
  93.2 2.4 %collective-permute-start.4 = (bf16[8,72,768]{2,1,0:T(8,128)(2,1)S(1)}, bf16[8,72,768]{2,1,0:T(8,128)(2,1)S(1)}, u32[]{:S(2)}, u32[]{:S(2)}) collective-permute-start(bf16[8,72,768]{2,1,0:T(8,128)(2,1)S(1)} %get-tuple-element.132), channel_id=1, source_target_pairs={{0,1},{1,0},{2,3},{3,2},{4,5},{5,4},{6,7},{7,6},{8,9},{9,8},{10,11... | collective-permute-start | bytes 2654216 | tf_op jit(solution)/shard_map/ppermute | solution.py:672
  95.6 1.5 collective-permute-start.5
  97.1 1.6 collective-permute-start.6
  98.7 18.0 %attend_back.3 = (bf16[1024,512]{1,0:T(8,128)(2,1)S(1)}, bf16[2,1024,512]{2,1,0:T(8,128)(2,1)S(1)}, bf16[2,1024,512]{2,1,0:T(8,128)(2,1)S(1)}) custom-call(s32[2]{0:T(128)S(1)} %copy-done.9, bf16[6,1024,128]{2,1,0:T(8,128)(2,1)} %get-tuple-element.112.q, bf16[6,1024,128]{2,1,0:T(8,128)(2,1)} %get-tuple-element.113.ko, ...), custom_call_target="tpu_custom_call" | custom-call | flops 34359738368 | bytes 67108864 | tf_op jit(solution)/shard_map/attend_back/pallas_call | solution.py:284
  116.7 1.3 collective-permute-start.8
  118.0 1.6 collective-permute-start.7
  119.6 0.9 step_sum.6
  121.7 2.4 %weigh.2 = (bf16[2,1024,256]{2,1,0:T(8,128)(2,1)S(1)}, bf16[3,384,256]{2,1,0:T(8,128)(2,1)S(1)}, bf16[3,384,256]{2,1,0:T(8,128)(2,1)S(1)}, f32[8,768]{1,0:T(8,128)S(1)}) custom-call(s32[2]{0:T(128)S(1)} %copy-done.9, bf16[1024,256]{1,0:T(8,128)(2,1)S(1)} %get-tuple-element.120.dq.refs_0_, bf16[2,1024,256]{2,1,0:T(8,128)(2,1)S(1)} %get-tuple-element.150.keep, ...), custom_call_target="tpu_custom_call" | custom-call | flops 34359738368 | bytes 67108864 | tf_op jit(solution)/shard_map/weigh/pallas_call | solution.py:611
  124.1 0.9 collective-permute-start.12
  125.0 3.9 %weigh.3 = (bf16[2,1024,512]{2,1,0:T(8,128)(2,1)S(1)}, bf16[3,384,512]{2,1,0:T(8,128)(2,1)S(1)}, bf16[3,384,512]{2,1,0:T(8,128)(2,1)S(1)}, f32[8,768]{1,0:T(8,128)S(1)}) custom-call(s32[2]{0:T(128)S(1)} %copy-done.9, bf16[1024,512]{1,0:T(8,128)(2,1)S(1)} %get-tuple-element.134.dq.refs_1_, bf16[2,1024,512]{2,1,0:T(8,128)(2,1)S(1)} %get-tuple-element.143.keep, ...), custom_call_target="tpu_custom_call" | custom-call | flops 34359738368 | bytes 67108864 | tf_op jit(solution)/shard_map/weigh/pallas_call | solution.py:611
  129.0 5.0 %collective-permute-done.10.refs_4_ = bf16[4,72,768]{2,1,0:T(8,128)(2,1)S(1)} collective-permute-done((bf16[4,72,768]{2,1,0:T(8,128)(2,1)S(1)}, bf16[4,72,768]{2,1,0:T(8,128)(2,1)S(1)}, u32[]{:S(2)}, u32[]{:S(2)}) %collective-permute-start.10) | collective-permute-done | bytes 442400 | tf_op jit(solution)/shard_map/ppermute | solution.py:672
  134.8 1.6 collective-permute-start.15
  136.9 1.5 collective-permute-start.17
  139.2 1.6 collective-permute-start.18
  141.3 3.5 %finish.2.refs_4_ = bf16[1024,768]{1,0:T(8,128)(2,1)} custom-call(bf16[1024,768]{1,0:T(8,128)(2,1)S(1)} %bitcast.22, f32[1024,768]{1,0:T(8,128)S(1)} %copy-done.1, bf16[768,2304]{1,0:T(8,128)(2,1)S(1)} %copy-done, f32[768]{0:T(1024)S(1)} %copy-done.6, bf16[1024,256]{1,0:T(8,128)(2,1)S(1)} %get-tuple-element.120.dq.refs_0_, ...), custom_call_target="tpu_custom_call" | custom-call | flops 34359738368 | bytes 67108864 | tf_op jit(solution)/shard_map/finish/pallas_call | solution.py:650
  145.2 2.7 %collective-permute-start.20 = (bf16[1,216,768]{2,1,0:T(8,128)(2,1)S(1)}, bf16[1,216,768]{2,1,0:T(8,128)(2,1)S(1)}, u32[]{:S(2)}, u32[]{:S(2)}) collective-permute-start(bf16[1,216,768]{2,1,0:T(8,128)(2,1)S(1)} %get-tuple-element.180), channel_id=1, source_target_pairs={{0,8},{1,9},{2,10},{3,11},{4,12},{5,13},{6,14},{7,15},{8,0},{9,1},... | collective-permute-start | bytes 995336 | tf_op jit(solution)/shard_map/ppermute | solution.py:672
  147.9 3.5 %finish.3 = bf16[1024,768]{1,0:T(8,128)(2,1)} custom-call(bf16[1024,768]{1,0:T(8,128)(2,1)S(1)} %bitcast.23, f32[1024,768]{1,0:T(8,128)S(1)} %copy-done.1, bf16[768,2304]{1,0:T(8,128)(2,1)S(1)} %copy-done, f32[768]{0:T(1024)S(1)} %copy-done.6, bf16[1024,256]{1,0:T(8,128)(2,1)S(1)} %get-tuple-element.120.dq.refs_0_, ...), custom_call_target="tpu_custom_call", output_to_operand_aliasing={{}: (8, {})} | custom-call | flops 1048576 | bytes 65536 | tf_op jit(solution)/shard_map/finish/pallas_call | solution.py:650
  151.4 0.9 collective-permute-done.18.refs_2_
  152.4 1.8 %collective-permute-done.19.refs_3_ = bf16[8,120,256]{2,1,0:T(8,128)(2,1)S(1)} collective-permute-done((bf16[8,120,256]{2,1,0:T(8,128)(2,1)S(1)}, bf16[8,120,256]{2,1,0:T(8,128)(2,1)S(1)}, u32[]{:S(2)}, u32[]{:S(2)}) %collective-permute-start.19) | collective-permute-done | bytes 491552 | tf_op jit(solution)/shard_map/ppermute | solution.py:672
  154.5 1.6 collective-permute-start.22
  156.0 1.5 collective-permute-start.21
  157.5 3.8 %collective-permute-done.20.got = bf16[1,216,768]{2,1,0:T(8,128)(2,1)S(1)} collective-permute-done((bf16[1,216,768]{2,1,0:T(8,128)(2,1)S(1)}, bf16[1,216,768]{2,1,0:T(8,128)(2,1)S(1)}, u32[]{:S(2)}, u32[]{:S(2)}) %collective-permute-start.20) | collective-permute-done | bytes 331808 | tf_op jit(solution)/shard_map/ppermute | solution.py:672
  162.7 6.7 %collective-permute-done.23.refs_1_ = bf16[480,256]{1,0:T(8,128)(2,1)S(1)} collective-permute-done((bf16[480,256]{1,0:T(8,128)(2,1)S(1)}, bf16[480,256]{1,0:T(8,128)(2,1)S(1)}, u32[]{:S(2)}, u32[]{:S(2)}) %collective-permute-start.23) | collective-permute-done | bytes 245792 | tf_op jit(solution)/shard_map/ppermute | solution.py:672
  169.5 1.6 collective-permute-start.24
  171.0 0.9 feed_end.1
  172.8 4.0 %collective-permute-done.24.got = bf16[264,256]{1,0:T(8,128)(2,1)S(1)} collective-permute-done((bf16[264,256]{1,0:T(8,128)(2,1)S(1)}, bf16[264,256]{1,0:T(8,128)(2,1)S(1)}, u32[]{:S(2)}, u32[]{:S(2)}) %collective-permute-start.24) | collective-permute-done | bytes 135200 | tf_op jit(solution)/shard_map/ppermute | solution.py:672
  (70 shorter events, 10.4 us)
Async XLA Ops:
  0.6 5.6 %collective-permute-start = (bf16[1024,768]{1,0:T(8,128)(2,1)}, bf16[1024,768]{1,0:T(8,128)(2,1)S(1)}, u32[]{:S(2)}, u32[]{:S(2)}) collective-permute-start(bf16[1024,768]{1,0:T(8,128)(2,1)} %bitcast.20), channel_id=1, source_target_pairs={{0,16},{1,17},{2,18},{3,19},{4,20},{5,21},{6,22},{7,23},{8,24},{9,... | collective-permute-start | bytes 4718600 | tf_op jit(solution)/shard_map/ppermute | solution.py:926
  7.4 70.9 %copy-start.7 = (f32[32,1024]{1,0:T(8,128)S(1)}, f32[32,1024]{1,0:T(8,128)}, u32[]{:S(2)}) copy-start(f32[32,1024]{1,0:T(8,128)} %constant.14.clone.sine_t.sine) | copy-start | bytes 393220
  7.4 70.9 %copy-start.8 = (f32[32,1024]{1,0:T(8,128)S(1)}, f32[32,1024]{1,0:T(8,128)}, u32[]{:S(2)}) copy-start(f32[32,1024]{1,0:T(8,128)} %constant.13.clone.cosine_t.cosine) | copy-start | bytes 393220
  7.4 70.9 %copy-start.9 = (s32[2]{0:T(128)S(1)}, s32[2]{0:T(128)}, u32[]{:S(2)}) copy-start(s32[2]{0:T(128)} %pad_add_fusion.info) | copy-start | bytes 28
  77.3 11.8 %collective-permute-start.3 = (bf16[384,768]{1,0:T(8,128)(2,1)}, bf16[384,768]{1,0:T(8,128)(2,1)S(1)}, u32[]{:S(2)}, u32[]{:S(2)}) collective-permute-start(bf16[384,768]{1,0:T(8,128)(2,1)} %get-tuple-element.128), channel_id=1, source_target_pairs={{0,16},{16,0},{1,17},{17,1},{2,18},{18,2},{3,19},{19,3},{4,20},{20... | collective-permute-start | bytes 1769480 | tf_op jit(solution)/shard_map/ppermute | solution.py:672
  77.8 11.4 %collective-permute-start.1 = (bf16[1536,768]{1,0:T(8,128)(2,1)}, bf16[1536,768]{1,0:T(8,128)(2,1)S(1)}, u32[]{:S(2)}, u32[]{:S(2)}) collective-permute-start(bf16[1536,768]{1,0:T(8,128)(2,1)} %get-tuple-element.122), channel_id=1, source_target_pairs={{0,16},{16,0},{1,17},{17,1},{2,18},{18,2},{3,19},{19,3},{4,20},{20... | collective-permute-start | bytes 7077896 | tf_op jit(solution)/shard_map/ppermute | solution.py:672
  77.9 11.3 %collective-permute-start.2 = (bf16[1536,768]{1,0:T(8,128)(2,1)}, bf16[1536,768]{1,0:T(8,128)(2,1)S(1)}, u32[]{:S(2)}, u32[]{:S(2)}) collective-permute-start(bf16[1536,768]{1,0:T(8,128)(2,1)} %get-tuple-element.125), channel_id=1, source_target_pairs={{0,16},{16,0},{1,17},{17,1},{2,18},{18,2},{3,19},{19,3},{4,20},{20... | collective-permute-start | bytes 7077896 | tf_op jit(solution)/shard_map/ppermute | solution.py:672
  79.1 10.1 %copy-start.2 = (bf16[1536,768]{1,0:T(8,128)(2,1)S(1)}, bf16[1536,768]{1,0:T(8,128)(2,1)}, u32[]{:S(2)}) copy-start(bf16[1536,768]{1,0:T(8,128)(2,1)} %get-tuple-element.124) | copy-start | bytes 7077892
  79.1 10.1 %copy-start.3 = (bf16[1536,768]{1,0:T(8,128)(2,1)S(1)}, bf16[1536,768]{1,0:T(8,128)(2,1)}, u32[]{:S(2)}) copy-start(bf16[1536,768]{1,0:T(8,128)(2,1)} %get-tuple-element.121) | copy-start | bytes 7077892
  79.1 10.2 %copy-start.5 = (bf16[384,768]{1,0:T(8,128)(2,1)S(1)}, bf16[384,768]{1,0:T(8,128)(2,1)}, u32[]{:S(2)}) copy-start(bf16[384,768]{1,0:T(8,128)(2,1)} %get-tuple-element.127) | copy-start | bytes 1769476
  93.2 26.4 %collective-permute-start.4 = (bf16[8,72,768]{2,1,0:T(8,128)(2,1)S(1)}, bf16[8,72,768]{2,1,0:T(8,128)(2,1)S(1)}, u32[]{:S(2)}, u32[]{:S(2)}) collective-permute-start(bf16[8,72,768]{2,1,0:T(8,128)(2,1)S(1)} %get-tuple-element.132), channel_id=1, source_target_pairs={{0,1},{1,0},{2,3},{3,2},{4,5},{5,4},{6,7},{7,6},{8,9},{9,8},{10,11... | collective-permute-start | bytes 2654216 | tf_op jit(solution)/shard_map/ppermute | solution.py:672
  95.6 24.0 %collective-permute-start.5 = (bf16[8,72,768]{2,1,0:T(8,128)(2,1)S(1)}, bf16[8,72,768]{2,1,0:T(8,128)(2,1)S(1)}, u32[]{:S(2)}, u32[]{:S(2)}) collective-permute-start(bf16[8,72,768]{2,1,0:T(8,128)(2,1)S(1)} %get-tuple-element.138), channel_id=1, source_target_pairs={{0,2},{1,3},{2,0},{3,1},{4,6},{5,7},{6,4},{7,5},{8,10},{9,11},{10,... | collective-permute-start | bytes 2654216 | tf_op jit(solution)/shard_map/ppermute | solution.py:672
  97.1 22.5 %collective-permute-start.6 = (bf16[8,72,768]{2,1,0:T(8,128)(2,1)S(1)}, bf16[8,72,768]{2,1,0:T(8,128)(2,1)S(1)}, u32[]{:S(2)}, u32[]{:S(2)}) collective-permute-start(bf16[8,72,768]{2,1,0:T(8,128)(2,1)S(1)} %get-tuple-element.139), channel_id=1, source_target_pairs={{0,4},{1,5},{2,6},{3,7},{4,0},{5,1},{6,2},{7,3},{8,12},{9,13},{10,... | collective-permute-start | bytes 2654216 | tf_op jit(solution)/shard_map/ppermute | solution.py:672
  116.7 5.0 %collective-permute-start.8 = (bf16[2,1024,256]{2,1,0:T(8,128)(2,1)S(1)}, bf16[2,1024,256]{2,1,0:T(8,128)(2,1)S(1)}, u32[]{:S(2)}, u32[]{:S(2)}) collective-permute-start(bf16[2,1024,256]{2,1,0:T(8,128)(2,1)S(1)} %get-tuple-element.152), channel_id=1, source_target_pairs={{16,0},{17,1},{18,2},{19,3},{20,4},{21,5},{22,6},{23,7},{24,8},{25... | collective-permute-start | bytes 3145736 | tf_op jit(solution)/shard_map/ppermute | solution.py:951
  118.0 7.0 %collective-permute-start.7 = (bf16[2,1024,512]{2,1,0:T(8,128)(2,1)S(1)}, bf16[2,1024,512]{2,1,0:T(8,128)(2,1)S(1)}, u32[]{:S(2)}, u32[]{:S(2)}) collective-permute-start(bf16[2,1024,512]{2,1,0:T(8,128)(2,1)S(1)} %get-tuple-element.144), channel_id=1, source_target_pairs={{16,0},{17,1},{18,2},{19,3},{20,4},{21,5},{22,6},{23,7},{24,8},{25... | collective-permute-start | bytes 6291464 | tf_op jit(solution)/shard_map/ppermute | solution.py:953
  120.5 13.9 %collective-permute-start.9 = (bf16[4,72,768]{2,1,0:T(8,128)(2,1)S(1)}, bf16[4,72,768]{2,1,0:T(8,128)(2,1)S(1)}, u32[]{:S(2)}, u32[]{:S(2)}) collective-permute-start(bf16[4,72,768]{2,1,0:T(8,128)(2,1)S(1)} %get-tuple-element.149), channel_id=1, source_target_pairs={{0,2},{1,3},{2,0},{3,1},{4,6},{5,7},{6,4},{7,5},{8,10},{9,11},{10,... | collective-permute-start | bytes 1327112 | tf_op jit(solution)/shard_map/ppermute | solution.py:672
  121.1 12.9 %collective-permute-start.10 = (bf16[4,72,768]{2,1,0:T(8,128)(2,1)S(1)}, bf16[4,72,768]{2,1,0:T(8,128)(2,1)S(1)}, u32[]{:S(2)}, u32[]{:S(2)}) collective-permute-start(bf16[4,72,768]{2,1,0:T(8,128)(2,1)S(1)} %get-tuple-element.159), channel_id=1, source_target_pairs={{0,4},{1,5},{2,6},{3,7},{4,0},{5,1},{6,2},{7,3},{8,12},{9,13},{10,... | collective-permute-start | bytes 1327112 | tf_op jit(solution)/shard_map/ppermute | solution.py:672
  121.5 12.9 %collective-permute-start.11 = (bf16[4,72,768]{2,1,0:T(8,128)(2,1)S(1)}, bf16[4,72,768]{2,1,0:T(8,128)(2,1)S(1)}, u32[]{:S(2)}, u32[]{:S(2)}) collective-permute-start(bf16[4,72,768]{2,1,0:T(8,128)(2,1)S(1)} %get-tuple-element.160), channel_id=1, source_target_pairs={{0,1},{1,0},{2,3},{3,2},{4,5},{5,4},{6,7},{7,6},{8,9},{9,8},{10,11... | collective-permute-start | bytes 1327112 | tf_op jit(solution)/shard_map/ppermute | solution.py:672
  124.1 12.8 %collective-permute-start.12 = (bf16[3,384,256]{2,1,0:T(8,128)(2,1)S(1)}, bf16[3,384,256]{2,1,0:T(8,128)(2,1)S(1)}, u32[]{:S(2)}, u32[]{:S(2)}) collective-permute-start(bf16[3,384,256]{2,1,0:T(8,128)(2,1)S(1)} %get-tuple-element.167), channel_id=1, source_target_pairs={{0,16},{16,0},{1,17},{17,1},{2,18},{18,2},{3,19},{19,3},{4,20},{20... | collective-permute-start | bytes 1769480 | tf_op jit(solution)/shard_map/ppermute | solution.py:672
  128.9 9.6 %collective-permute-start.14 = (f32[8,768]{1,0:T(8,128)S(1)}, f32[8,768]{1,0:T(8,128)S(1)}, u32[]{:S(2)}, u32[]{:S(2)}) collective-permute-start(f32[8,768]{1,0:T(8,128)S(1)} %get-tuple-element.171.refs_4_), channel_id=1, source_target_pairs={{0,16},{16,0},{1,17},{17,1},{2,18},{18,2},{3,19},{19,3},{4,20},{20... | collective-permute-start | bytes 73736 | tf_op jit(solution)/shard_map/ppermute | solution.py:672
  134.0 4.5 %collective-permute-start.13 = (bf16[3,384,512]{2,1,0:T(8,128)(2,1)S(1)}, bf16[3,384,512]{2,1,0:T(8,128)(2,1)S(1)}, u32[]{:S(2)}, u32[]{:S(2)}) collective-permute-start(bf16[3,384,512]{2,1,0:T(8,128)(2,1)S(1)} %get-tuple-element.170), channel_id=1, source_target_pairs={{0,16},{16,0},{1,17},{17,1},{2,18},{18,2},{3,19},{19,3},{4,20},{20... | collective-permute-start | bytes 3538952 | tf_op jit(solution)/shard_map/ppermute | solution.py:672
  134.4 6.9 %copy-start.4 = (bf16[1,1,1024,768]{3,2,1,0:T(8,128)(2,1)S(1)}, bf16[1,1,1024,768]{3,2,1,0:T(8,128)(2,1)}, u32[]{:S(2)}) copy-start(bf16[1,1,1024,768]{3,2,1,0:T(8,128)(2,1)} %param.11) | copy-start | bytes 4718596
  134.8 10.3 %collective-permute-start.15 = (bf16[2,72,768]{2,1,0:T(8,128)(2,1)S(1)}, bf16[2,72,768]{2,1,0:T(8,128)(2,1)S(1)}, u32[]{:S(2)}, u32[]{:S(2)}) collective-permute-start(bf16[2,72,768]{2,1,0:T(8,128)(2,1)S(1)} %get-tuple-element.165), channel_id=1, source_target_pairs={{0,4},{1,5},{2,6},{3,7},{4,0},{5,1},{6,2},{7,3},{8,12},{9,13},{10,... | collective-permute-start | bytes 663560 | tf_op jit(solution)/shard_map/ppermute | solution.py:672
  136.4 8.4 %collective-permute-start.16 = (bf16[2,72,768]{2,1,0:T(8,128)(2,1)S(1)}, bf16[2,72,768]{2,1,0:T(8,128)(2,1)S(1)}, u32[]{:S(2)}, u32[]{:S(2)}) collective-permute-start(bf16[2,72,768]{2,1,0:T(8,128)(2,1)S(1)} %get-tuple-element.178), channel_id=1, source_target_pairs={{0,1},{1,0},{2,3},{3,2},{4,5},{5,4},{6,7},{7,6},{8,9},{9,8},{10,11... | collective-permute-start | bytes 663560 | tf_op jit(solution)/shard_map/ppermute | solution.py:672
  136.9 8.1 %collective-permute-start.17 = (bf16[2,72,768]{2,1,0:T(8,128)(2,1)S(1)}, bf16[2,72,768]{2,1,0:T(8,128)(2,1)S(1)}, u32[]{:S(2)}, u32[]{:S(2)}) collective-permute-start(bf16[2,72,768]{2,1,0:T(8,128)(2,1)S(1)} %get-tuple-element.179), channel_id=1, source_target_pairs={{0,2},{1,3},{2,0},{3,1},{4,6},{5,7},{6,4},{7,5},{8,10},{9,11},{10,... | collective-permute-start | bytes 663560 | tf_op jit(solution)/shard_map/ppermute | solution.py:672
  139.2 13.2 %collective-permute-start.18 = (bf16[816,256]{1,0:T(8,128)(2,1)S(1)}, bf16[816,256]{1,0:T(8,128)(2,1)S(1)}, u32[]{:S(2)}, u32[]{:S(2)}) collective-permute-start(bf16[816,256]{1,0:T(8,128)(2,1)S(1)} %get-tuple-element.172), channel_id=1, source_target_pairs={{0,1},{1,0},{2,3},{3,2},{4,5},{5,4},{6,7},{7,6},{8,9},{9,8},{10,11... | collective-permute-start | bytes 1253384 | tf_op jit(solution)/shard_map/ppermute | solution.py:672
  140.8 13.4 %collective-permute-start.19 = (bf16[8,120,256]{2,1,0:T(8,128)(2,1)S(1)}, bf16[8,120,256]{2,1,0:T(8,128)(2,1)S(1)}, u32[]{:S(2)}, u32[]{:S(2)}) collective-permute-start(bf16[8,120,256]{2,1,0:T(8,128)(2,1)S(1)} %get-tuple-element.186), channel_id=1, source_target_pairs={{0,2},{1,3},{2,0},{3,1},{4,6},{5,7},{6,4},{7,5},{8,10},{9,11},{10,... | collective-permute-start | bytes 1474568 | tf_op jit(solution)/shard_map/ppermute | solution.py:672
  145.2 16.1 %collective-permute-start.20 = (bf16[1,216,768]{2,1,0:T(8,128)(2,1)S(1)}, bf16[1,216,768]{2,1,0:T(8,128)(2,1)S(1)}, u32[]{:S(2)}, u32[]{:S(2)}) collective-permute-start(bf16[1,216,768]{2,1,0:T(8,128)(2,1)S(1)} %get-tuple-element.180), channel_id=1, source_target_pairs={{0,8},{1,9},{2,10},{3,11},{4,12},{5,13},{6,14},{7,15},{8,0},{9,1},... | collective-permute-start | bytes 995336 | tf_op jit(solution)/shard_map/ppermute | solution.py:672
  154.5 7.5 %collective-permute-start.22 = (bf16[4,120,256]{2,1,0:T(8,128)(2,1)S(1)}, bf16[4,120,256]{2,1,0:T(8,128)(2,1)S(1)}, u32[]{:S(2)}, u32[]{:S(2)}) collective-permute-start(bf16[4,120,256]{2,1,0:T(8,128)(2,1)S(1)} %get-tuple-element.193), channel_id=1, source_target_pairs={{0,1},{1,0},{2,3},{3,2},{4,5},{5,4},{6,7},{7,6},{8,9},{9,8},{10,11... | collective-permute-start | bytes 737288 | tf_op jit(solution)/shard_map/ppermute | solution.py:672
  156.0 5.9 %collective-permute-start.21 = (bf16[432,256]{1,0:T(8,128)(2,1)S(1)}, bf16[432,256]{1,0:T(8,128)(2,1)S(1)}, u32[]{:S(2)}, u32[]{:S(2)}) collective-permute-start(bf16[432,256]{1,0:T(8,128)(2,1)S(1)} %get-tuple-element.192), channel_id=1, source_target_pairs={{0,2},{1,3},{2,0},{3,1},{4,6},{5,7},{6,4},{7,5},{8,10},{9,11},{10,... | collective-permute-start | bytes 663560 | tf_op jit(solution)/shard_map/ppermute | solution.py:672
  162.1 7.4 %collective-permute-start.23 = (bf16[480,256]{1,0:T(8,128)(2,1)S(1)}, bf16[480,256]{1,0:T(8,128)(2,1)S(1)}, u32[]{:S(2)}, u32[]{:S(2)}) collective-permute-start(bf16[480,256]{1,0:T(8,128)(2,1)S(1)} %get-tuple-element.196), channel_id=1, source_target_pairs={{0,4},{1,5},{2,6},{3,7},{4,0},{5,1},{6,2},{7,3},{8,12},{9,13},{10,... | collective-permute-start | bytes 737288 | tf_op jit(solution)/shard_map/ppermute | solution.py:672
  169.5 7.3 %collective-permute-start.24 = (bf16[264,256]{1,0:T(8,128)(2,1)S(1)}, bf16[264,256]{1,0:T(8,128)(2,1)S(1)}, u32[]{:S(2)}, u32[]{:S(2)}) collective-permute-start(bf16[264,256]{1,0:T(8,128)(2,1)S(1)} %get-tuple-element.199), channel_id=1, source_target_pairs={{0,8},{1,9},{2,10},{3,11},{4,12},{5,13},{6,14},{7,15},{8,0},{9,1},... | collective-permute-start | bytes 405512 | tf_op jit(solution)/shard_map/ppermute | solution.py:672
  (9 other events, 25.8 us)

commit v2 on v1

--- a/solution.py
+++ b/solution.py
@@ -873,15 +873,16 @@
     gain2[...] = sums[3:4, :].reshape(width)
     gain1[...] = (sums[4:5, :] / gain_line[...].reshape(1, width)).reshape(width)
     count = jnp.max(sums[5:6, :], axis=1, keepdims=True) * width
-    rms[...] = jnp.broadcast_to(jnp.sqrt(jnp.sum(sums, axis=1, keepdims=True) / count), rms.shape)
+    for i in range(3):
+        rms[i] = jnp.sum(jnp.sqrt(jnp.sum(sums[i : i + 1, :], axis=1, keepdims=True) / count))
 
 
 def qkv_end(places, gain, kept, got, small, tall, wide, rides):
     return pl.pallas_call(
         functools.partial(qkv_end_kernel, places, rides),
         in_specs=[IN_VMEM] * (3 + len(small)),
-        out_specs=[IN_VMEM] * 4,
-        out_shape=[shape((tall, wide), f32), shape(gain.shape, f32), shape(gain.shape, f32), shape((SUMS, 128), f32)],
+        out_specs=[IN_VMEM] * 3 + [SMEM],
+        out_shape=[shape((tall, wide), f32), shape(gain.shape, f32), shape(gain.shape, f32), shape((3,), f32)],
         compiler_params=params(16),
         cost_estimate=COST,
         name="qkv_end",
@@ -975,10 +976,9 @@
     )
     token = next(late)[0]
     ends = [dq1, dq2], [dkv1, dkv2], qkv_weight, attn_gain
-    tiles = seq // R
-    dx = finish((0, tiles // 2), after(x, token), dx2, *ends, [])
+    dx = finish((0, 1), after(x, token), dx2, *ends, [])
     early_out = early.send(dx)
-    dx = finish((tiles // 2, tiles), x, after(dx2, early_out[0]), *ends, [dx])
+    dx = finish((1, seq // R), x, after(dx2, early_out[0]), *ends, [dx])
     late.send(dx)
     late_out = late.send(early_out[1])
     while len(late_out) == 2:
@@ -998,7 +998,7 @@
         down_grad,
         gain1_grad,
         gain2_grad,
-        rms[:3, 0],
+        rms,
     )
 
 

time: 178 us -> 177 us (level)
  waiting for transfers between devices: 25.3 us -> 21.9 us
  starting transfers between devices: 27.8 us -> 30.3 us
    ppermute x22, waiting for transfers between devices: 23.4 us -> 20 us  [exchange(): return lax.ppermute(value, axis, [(i, i ^ bit) for i in range(size)])]
    ppermute x22, starting transfers between devices: 22.5 us -> 25 us  [exchange(): return lax.ppermute(value, axis, [(i, i ^ bit) for i in range(size)])]
where the time goes in v2:
time: 177 us
  Pallas kernels  119 us (67%)
  starting transfers between devices  30.3 us (17%)
  waiting for transfers between devices  21.9 us (12%)
  local copies, waits for them, and re-layouts  2.87 us (2%)
  between operations  1.8 us (1%)
    pallas_call x1, Pallas kernels, layer(): pl.pallas_call(layer_kernel, in_specs=[SMEM] + [IN_VMEM] * 5 + [anywhere]...  70 us
    pallas_call x2, Pallas kernels, attend_back(): pl.pallas_call(attend_back_kernel, grid=(pairs,), in_specs=[SMEM] + [head...  28.1 us
    ppermute x22, starting transfers between devices, exchange(): return lax.ppermute(value, axis, [(i, i ^ bit) for i in range(size)])  25 us
    ppermute x22, waiting for transfers between devices, exchange(): return lax.ppermute(value, axis, [(i, i ^ bit) for i in range(size)])  20 us
    pallas_call x2, Pallas kernels, finish(): pl.pallas_call(functools.partial(finish_kernel, len(dqs), tiles), in_spec...  7.04 us
    pallas_call x2, Pallas kernels, weigh(): pl.pallas_call(functools.partial(weigh_kernel, first), in_specs=[SMEM] +...  6.3 us
    pallas_call x2, Pallas kernels, start_sum(): pl.pallas_call(functools.partial(start_kernel, orders, sources, mode), co...  4.67 us
  transfers between devices with their start and end apart: 25, of which 10 were waited for; matrix products, arithmetic and copies ran while one was open for 1% of the time, Pallas kernels for 25%

profile of v2, /device:TPU:0, one launch (start us, length us, event | category | flops | bytes accessed | tf_op | source)
XLA Modules:
  0.0 176.9 jit_solution(9140821077493529479)
XLA Ops:
  0.6 2.5 %collective-permute-start = (bf16[1024,768]{1,0:T(8,128)(2,1)}, bf16[1024,768]{1,0:T(8,128)(2,1)S(1)}, u32[]{:S(2)}, u32[]{:S(2)}) collective-permute-start(bf16[1024,768]{1,0:T(8,128)(2,1)} %bitcast.20), channel_id=1, source_target_pairs={{0,16},{1,17},{2,18},{3,19},{4,20},{5,21},{6,22},{7,23},{8,24},{9,... | collective-permute-start | bytes 4718600 | tf_op jit(solution)/shard_map/ppermute | solution.py:927
  4.3 1.9 %collective-permute-done.received = bf16[1024,768]{1,0:T(8,128)(2,1)S(1)} collective-permute-done((bf16[1024,768]{1,0:T(8,128)(2,1)}, bf16[1024,768]{1,0:T(8,128)(2,1)S(1)}, u32[]{:S(2)}, u32[]{:S(2)}) %collective-permute-start) | collective-permute-done | bytes 1572896 | tf_op jit(solution)/shard_map/ppermute | solution.py:927
  6.2 1.1 copy-done.15
  7.4 70.0 %layer.1 = (bf16[6,1024,128]{2,1,0:T(8,128)(2,1)}, bf16[6,1024,128]{2,1,0:T(8,128)(2,1)}, bf16[6,1024,128]{2,1,0:T(8,128)(2,1)}, bf16[6,1024,128]{2,1,0:T(8,128)...) custom-call(s32[2]{0:T(128)} %pad_add_fusion.info, ...), custom_call_target="tpu_custom_call" | custom-call | flops 34359738368 | bytes 67108864 | tf_op jit(solution)/shard_map/layer/pallas_call | solution.py:557
  79.1 10.1 %attend_back.2 = (bf16[1024,256]{1,0:T(8,128)(2,1)S(1)}, bf16[2,1024,256]{2,1,0:T(8,128)(2,1)S(1)}, bf16[2,1024,256]{2,1,0:T(8,128)(2,1)S(1)}) custom-call(s32[2]{0:T(128)S(1)} %copy-done.9, bf16[6,1024,128]{2,1,0:T(8,128)(2,1)} %get-tuple-element.112.q, bf16[6,1024,128]{2,1,0:T(8,128)(2,1)} %get-tuple-element.113.ko, ...), custom_call_target="tpu_custom_call" | custom-call | flops 34359738368 | bytes 67108864 | tf_op jit(solution)/shard_map/attend_back/pallas_call | solution.py:284
  89.3 3.9 %start_sum.2 = (bf16[8,72,768]{2,1,0:T(8,128)(2,1)S(1)}, bf16[8,72,768]{2,1,0:T(8,128)(2,1)S(1)}, bf16[8,72,768]{2,1,0:T(8,128)(2,1)S(1)}, bf16[8,72,768]{2,1,0:...) custom-call(s32[1]{0:T(128)} %bitcast.4.me, bf16[48,32,768]{2,1,0:T(8,128)(2,1)S(1)} %bitcast.17, ...), custom_call_target="tpu_custom_call" | custom-call | flops 1048576 | bytes 65536 | tf_op jit(solution)/shard_map/start_sum/pallas_call | solution.py:770
  93.2 2.4 %collective-permute-start.4 = (bf16[8,72,768]{2,1,0:T(8,128)(2,1)S(1)}, bf16[8,72,768]{2,1,0:T(8,128)(2,1)S(1)}, u32[]{:S(2)}, u32[]{:S(2)}) collective-permute-start(bf16[8,72,768]{2,1,0:T(8,128)(2,1)S(1)} %get-tuple-element.132), channel_id=1, source_target_pairs={{0,1},{1,0},{2,3},{3,2},{4,5},{5,4},{6,7},{7,6},{8,9},{9,8},{10,11... | collective-permute-start | bytes 2654216 | tf_op jit(solution)/shard_map/ppermute | solution.py:672
  95.6 1.5 collective-permute-start.5
  97.1 1.6 collective-permute-start.6
  98.7 18.0 %attend_back.3 = (bf16[1024,512]{1,0:T(8,128)(2,1)S(1)}, bf16[2,1024,512]{2,1,0:T(8,128)(2,1)S(1)}, bf16[2,1024,512]{2,1,0:T(8,128)(2,1)S(1)}) custom-call(s32[2]{0:T(128)S(1)} %copy-done.9, bf16[6,1024,128]{2,1,0:T(8,128)(2,1)} %get-tuple-element.112.q, bf16[6,1024,128]{2,1,0:T(8,128)(2,1)} %get-tuple-element.113.ko, ...), custom_call_target="tpu_custom_call" | custom-call | flops 34359738368 | bytes 67108864 | tf_op jit(solution)/shard_map/attend_back/pallas_call | solution.py:284
  116.7 1.3 collective-permute-start.8
  118.0 1.6 collective-permute-start.7
  121.7 2.4 %weigh.2 = (bf16[2,1024,256]{2,1,0:T(8,128)(2,1)S(1)}, bf16[3,384,256]{2,1,0:T(8,128)(2,1)S(1)}, bf16[3,384,256]{2,1,0:T(8,128)(2,1)S(1)}, f32[8,768]{1,0:T(8,128)S(1)}) custom-call(s32[2]{0:T(128)S(1)} %copy-done.9, bf16[1024,256]{1,0:T(8,128)(2,1)S(1)} %get-tuple-element.120.dq.refs_0_, bf16[2,1024,256]{2,1,0:T(8,128)(2,1)S(1)} %get-tuple-element.150.keep, ...), custom_call_target="tpu_custom_call" | custom-call | flops 34359738368 | bytes 67108864 | tf_op jit(solution)/shard_map/weigh/pallas_call | solution.py:611
  124.1 0.9 collective-permute-start.12
  125.0 3.9 %weigh.3 = (bf16[2,1024,512]{2,1,0:T(8,128)(2,1)S(1)}, bf16[3,384,512]{2,1,0:T(8,128)(2,1)S(1)}, bf16[3,384,512]{2,1,0:T(8,128)(2,1)S(1)}, f32[8,768]{1,0:T(8,128)S(1)}) custom-call(s32[2]{0:T(128)S(1)} %copy-done.9, bf16[1024,512]{1,0:T(8,128)(2,1)S(1)} %get-tuple-element.134.dq.refs_1_, bf16[2,1024,512]{2,1,0:T(8,128)(2,1)S(1)} %get-tuple-element.143.keep, ...), custom_call_target="tpu_custom_call" | custom-call | flops 34359738368 | bytes 67108864 | tf_op jit(solution)/shard_map/weigh/pallas_call | solution.py:611
  129.0 5.0 %collective-permute-done.10.refs_4_ = bf16[4,72,768]{2,1,0:T(8,128)(2,1)S(1)} collective-permute-done((bf16[4,72,768]{2,1,0:T(8,128)(2,1)S(1)}, bf16[4,72,768]{2,1,0:T(8,128)(2,1)S(1)}, u32[]{:S(2)}, u32[]{:S(2)}) %collective-permute-start.10) | collective-permute-done | bytes 442400 | tf_op jit(solution)/shard_map/ppermute | solution.py:672
  134.8 1.6 collective-permute-start.15
  136.9 1.5 collective-permute-start.17
  139.2 1.6 collective-permute-start.18
  141.3 2.2 %finish.2.refs_4_ = bf16[1024,768]{1,0:T(8,128)(2,1)} custom-call(bf16[1024,768]{1,0:T(8,128)(2,1)S(1)} %bitcast.22, f32[1024,768]{1,0:T(8,128)S(1)} %copy-done.1, bf16[768,2304]{1,0:T(8,128)(2,1)S(1)} %copy-done, f32[768]{0:T(1024)S(1)} %copy-done.6, bf16[1024,256]{1,0:T(8,128)(2,1)S(1)} %get-tuple-element.120.dq.refs_0_, ...), custom_call_target="tpu_custom_call" | custom-call | flops 34359738368 | bytes 67108864 | tf_op jit(solution)/shard_map/finish/pallas_call | solution.py:650
  143.5 1.3 collective-permute-done.16.refs_4_
  145.2 2.7 %collective-permute-start.20 = (bf16[1,216,768]{2,1,0:T(8,128)(2,1)S(1)}, bf16[1,216,768]{2,1,0:T(8,128)(2,1)S(1)}, u32[]{:S(2)}, u32[]{:S(2)}) collective-permute-start(bf16[1,216,768]{2,1,0:T(8,128)(2,1)S(1)} %get-tuple-element.180), channel_id=1, source_target_pairs={{0,8},{1,9},{2,10},{3,11},{4,12},{5,13},{6,14},{7,15},{8,0},{9,1},... | collective-permute-start | bytes 995336 | tf_op jit(solution)/shard_map/ppermute | solution.py:672
  147.9 4.9 %finish.3 = bf16[1024,768]{1,0:T(8,128)(2,1)} custom-call(bf16[1024,768]{1,0:T(8,128)(2,1)S(1)} %bitcast.23, f32[1024,768]{1,0:T(8,128)S(1)} %copy-done.1, bf16[768,2304]{1,0:T(8,128)(2,1)S(1)} %copy-done, f32[768]{0:T(1024)S(1)} %copy-done.6, bf16[1024,256]{1,0:T(8,128)(2,1)S(1)} %get-tuple-element.120.dq.refs_0_, ...), custom_call_target="tpu_custom_call", output_to_operand_aliasing={{}: (8, {})} | custom-call | flops 1048576 | bytes 65536 | tf_op jit(solution)/shard_map/finish/pallas_call | solution.py:650
  152.8 1.4 collective-permute-done.19.refs_3_
  154.5 1.6 collective-permute-start.22
  156.0 1.5 collective-permute-start.21
  157.5 2.6 %collective-permute-done.20.got = bf16[1,216,768]{2,1,0:T(8,128)(2,1)S(1)} collective-permute-done((bf16[1,216,768]{2,1,0:T(8,128)(2,1)S(1)}, bf16[1,216,768]{2,1,0:T(8,128)(2,1)S(1)}, u32[]{:S(2)}, u32[]{:S(2)}) %collective-permute-start.20) | collective-permute-done | bytes 331808 | tf_op jit(solution)/shard_map/ppermute | solution.py:672
  160.2 1.8 %collective-permute-done.21.refs_2_ = bf16[432,256]{1,0:T(8,128)(2,1)S(1)} collective-permute-done((bf16[432,256]{1,0:T(8,128)(2,1)S(1)}, bf16[432,256]{1,0:T(8,128)(2,1)S(1)}, u32[]{:S(2)}, u32[]{:S(2)}) %collective-permute-start.21) | collective-permute-done | bytes 221216 | tf_op jit(solution)/shard_map/ppermute | solution.py:672
  162.7 5.6 %collective-permute-done.23.refs_1_ = bf16[480,256]{1,0:T(8,128)(2,1)S(1)} collective-permute-done((bf16[480,256]{1,0:T(8,128)(2,1)S(1)}, bf16[480,256]{1,0:T(8,128)(2,1)S(1)}, u32[]{:S(2)}, u32[]{:S(2)}) %collective-permute-start.23) | collective-permute-done | bytes 245792 | tf_op jit(solution)/shard_map/ppermute | solution.py:672
  168.4 4.1 %collective-permute-start.24 = (bf16[264,256]{1,0:T(8,128)(2,1)S(1)}, bf16[264,256]{1,0:T(8,128)(2,1)S(1)}, u32[]{:S(2)}, u32[]{:S(2)}) collective-permute-start(bf16[264,256]{1,0:T(8,128)(2,1)S(1)} %get-tuple-element.199), channel_id=1, source_target_pairs={{0,8},{1,9},{2,10},{3,11},{4,12},{5,13},{6,14},{7,15},{8,0},{9,1},... | collective-permute-start | bytes 405512 | tf_op jit(solution)/shard_map/ppermute | solution.py:672
  172.5 0.9 feed_end.1
  174.3 1.7 collective-permute-done.24.got
  (69 shorter events, 10.1 us)
Async XLA Ops:
  0.6 5.6 %collective-permute-start = (bf16[1024,768]{1,0:T(8,128)(2,1)}, bf16[1024,768]{1,0:T(8,128)(2,1)S(1)}, u32[]{:S(2)}, u32[]{:S(2)}) collective-permute-start(bf16[1024,768]{1,0:T(8,128)(2,1)} %bitcast.20), channel_id=1, source_target_pairs={{0,16},{1,17},{2,18},{3,19},{4,20},{5,21},{6,22},{7,23},{8,24},{9,... | collective-permute-start | bytes 4718600 | tf_op jit(solution)/shard_map/ppermute | solution.py:927
  7.4 70.9 %copy-start.7 = (f32[32,1024]{1,0:T(8,128)S(1)}, f32[32,1024]{1,0:T(8,128)}, u32[]{:S(2)}) copy-start(f32[32,1024]{1,0:T(8,128)} %constant.14.clone.sine_t.sine) | copy-start | bytes 393220
  7.4 70.9 %copy-start.8 = (f32[32,1024]{1,0:T(8,128)S(1)}, f32[32,1024]{1,0:T(8,128)}, u32[]{:S(2)}) copy-start(f32[32,1024]{1,0:T(8,128)} %constant.13.clone.cosine_t.cosine) | copy-start | bytes 393220
  7.4 70.9 %copy-start.9 = (s32[2]{0:T(128)S(1)}, s32[2]{0:T(128)}, u32[]{:S(2)}) copy-start(s32[2]{0:T(128)} %pad_add_fusion.info) | copy-start | bytes 28
  77.4 11.8 %collective-permute-start.3 = (bf16[384,768]{1,0:T(8,128)(2,1)}, bf16[384,768]{1,0:T(8,128)(2,1)S(1)}, u32[]{:S(2)}, u32[]{:S(2)}) collective-permute-start(bf16[384,768]{1,0:T(8,128)(2,1)} %get-tuple-element.128), channel_id=1, source_target_pairs={{0,16},{16,0},{1,17},{17,1},{2,18},{18,2},{3,19},{19,3},{4,20},{20... | collective-permute-start | bytes 1769480 | tf_op jit(solution)/shard_map/ppermute | solution.py:672
  77.8 11.4 %collective-permute-start.1 = (bf16[1536,768]{1,0:T(8,128)(2,1)}, bf16[1536,768]{1,0:T(8,128)(2,1)S(1)}, u32[]{:S(2)}, u32[]{:S(2)}) collective-permute-start(bf16[1536,768]{1,0:T(8,128)(2,1)} %get-tuple-element.122), channel_id=1, source_target_pairs={{0,16},{16,0},{1,17},{17,1},{2,18},{18,2},{3,19},{19,3},{4,20},{20... | collective-permute-start | bytes 7077896 | tf_op jit(solution)/shard_map/ppermute | solution.py:672
  77.9 11.3 %collective-permute-start.2 = (bf16[1536,768]{1,0:T(8,128)(2,1)}, bf16[1536,768]{1,0:T(8,128)(2,1)S(1)}, u32[]{:S(2)}, u32[]{:S(2)}) collective-permute-start(bf16[1536,768]{1,0:T(8,128)(2,1)} %get-tuple-element.125), channel_id=1, source_target_pairs={{0,16},{16,0},{1,17},{17,1},{2,18},{18,2},{3,19},{19,3},{4,20},{20... | collective-permute-start | bytes 7077896 | tf_op jit(solution)/shard_map/ppermute | solution.py:672
  79.1 10.1 %copy-start.2 = (bf16[1536,768]{1,0:T(8,128)(2,1)S(1)}, bf16[1536,768]{1,0:T(8,128)(2,1)}, u32[]{:S(2)}) copy-start(bf16[1536,768]{1,0:T(8,128)(2,1)} %get-tuple-element.124) | copy-start | bytes 7077892
  79.1 10.1 %copy-start.3 = (bf16[1536,768]{1,0:T(8,128)(2,1)S(1)}, bf16[1536,768]{1,0:T(8,128)(2,1)}, u32[]{:S(2)}) copy-start(bf16[1536,768]{1,0:T(8,128)(2,1)} %get-tuple-element.121) | copy-start | bytes 7077892
  79.1 10.2 %copy-start.5 = (bf16[384,768]{1,0:T(8,128)(2,1)S(1)}, bf16[384,768]{1,0:T(8,128)(2,1)}, u32[]{:S(2)}) copy-start(bf16[384,768]{1,0:T(8,128)(2,1)} %get-tuple-element.127) | copy-start | bytes 1769476
  93.2 26.4 %collective-permute-start.4 = (bf16[8,72,768]{2,1,0:T(8,128)(2,1)S(1)}, bf16[8,72,768]{2,1,0:T(8,128)(2,1)S(1)}, u32[]{:S(2)}, u32[]{:S(2)}) collective-permute-start(bf16[8,72,768]{2,1,0:T(8,128)(2,1)S(1)} %get-tuple-element.132), channel_id=1, source_target_pairs={{0,1},{1,0},{2,3},{3,2},{4,5},{5,4},{6,7},{7,6},{8,9},{9,8},{10,11... | collective-permute-start | bytes 2654216 | tf_op jit(solution)/shard_map/ppermute | solution.py:672
  95.6 24.0 %collective-permute-start.5 = (bf16[8,72,768]{2,1,0:T(8,128)(2,1)S(1)}, bf16[8,72,768]{2,1,0:T(8,128)(2,1)S(1)}, u32[]{:S(2)}, u32[]{:S(2)}) collective-permute-start(bf16[8,72,768]{2,1,0:T(8,128)(2,1)S(1)} %get-tuple-element.138), channel_id=1, source_target_pairs={{0,2},{1,3},{2,0},{3,1},{4,6},{5,7},{6,4},{7,5},{8,10},{9,11},{10,... | collective-permute-start | bytes 2654216 | tf_op jit(solution)/shard_map/ppermute | solution.py:672
  97.1 22.5 %collective-permute-start.6 = (bf16[8,72,768]{2,1,0:T(8,128)(2,1)S(1)}, bf16[8,72,768]{2,1,0:T(8,128)(2,1)S(1)}, u32[]{:S(2)}, u32[]{:S(2)}) collective-permute-start(bf16[8,72,768]{2,1,0:T(8,128)(2,1)S(1)} %get-tuple-element.139), channel_id=1, source_target_pairs={{0,4},{1,5},{2,6},{3,7},{4,0},{5,1},{6,2},{7,3},{8,12},{9,13},{10,... | collective-permute-start | bytes 2654216 | tf_op jit(solution)/shard_map/ppermute | solution.py:672
  116.7 5.0 %collective-permute-start.8 = (bf16[2,1024,256]{2,1,0:T(8,128)(2,1)S(1)}, bf16[2,1024,256]{2,1,0:T(8,128)(2,1)S(1)}, u32[]{:S(2)}, u32[]{:S(2)}) collective-permute-start(bf16[2,1024,256]{2,1,0:T(8,128)(2,1)S(1)} %get-tuple-element.152), channel_id=1, source_target_pairs={{16,0},{17,1},{18,2},{19,3},{20,4},{21,5},{22,6},{23,7},{24,8},{25... | collective-permute-start | bytes 3145736 | tf_op jit(solution)/shard_map/ppermute | solution.py:952
  118.0 7.0 %collective-permute-start.7 = (bf16[2,1024,512]{2,1,0:T(8,128)(2,1)S(1)}, bf16[2,1024,512]{2,1,0:T(8,128)(2,1)S(1)}, u32[]{:S(2)}, u32[]{:S(2)}) collective-permute-start(bf16[2,1024,512]{2,1,0:T(8,128)(2,1)S(1)} %get-tuple-element.144), channel_id=1, source_target_pairs={{16,0},{17,1},{18,2},{19,3},{20,4},{21,5},{22,6},{23,7},{24,8},{25... | collective-permute-start | bytes 6291464 | tf_op jit(solution)/shard_map/ppermute | solution.py:954
  120.5 13.9 %collective-permute-start.9 = (bf16[4,72,768]{2,1,0:T(8,128)(2,1)S(1)}, bf16[4,72,768]{2,1,0:T(8,128)(2,1)S(1)}, u32[]{:S(2)}, u32[]{:S(2)}) collective-permute-start(bf16[4,72,768]{2,1,0:T(8,128)(2,1)S(1)} %get-tuple-element.149), channel_id=1, source_target_pairs={{0,2},{1,3},{2,0},{3,1},{4,6},{5,7},{6,4},{7,5},{8,10},{9,11},{10,... | collective-permute-start | bytes 1327112 | tf_op jit(solution)/shard_map/ppermute | solution.py:672
  121.1 12.9 %collective-permute-start.10 = (bf16[4,72,768]{2,1,0:T(8,128)(2,1)S(1)}, bf16[4,72,768]{2,1,0:T(8,128)(2,1)S(1)}, u32[]{:S(2)}, u32[]{:S(2)}) collective-permute-start(bf16[4,72,768]{2,1,0:T(8,128)(2,1)S(1)} %get-tuple-element.159), channel_id=1, source_target_pairs={{0,4},{1,5},{2,6},{3,7},{4,0},{5,1},{6,2},{7,3},{8,12},{9,13},{10,... | collective-permute-start | bytes 1327112 | tf_op jit(solution)/shard_map/ppermute | solution.py:672
  121.5 12.9 %collective-permute-start.11 = (bf16[4,72,768]{2,1,0:T(8,128)(2,1)S(1)}, bf16[4,72,768]{2,1,0:T(8,128)(2,1)S(1)}, u32[]{:S(2)}, u32[]{:S(2)}) collective-permute-start(bf16[4,72,768]{2,1,0:T(8,128)(2,1)S(1)} %get-tuple-element.160), channel_id=1, source_target_pairs={{0,1},{1,0},{2,3},{3,2},{4,5},{5,4},{6,7},{7,6},{8,9},{9,8},{10,11... | collective-permute-start | bytes 1327112 | tf_op jit(solution)/shard_map/ppermute | solution.py:672
  124.1 12.8 %collective-permute-start.12 = (bf16[3,384,256]{2,1,0:T(8,128)(2,1)S(1)}, bf16[3,384,256]{2,1,0:T(8,128)(2,1)S(1)}, u32[]{:S(2)}, u32[]{:S(2)}) collective-permute-start(bf16[3,384,256]{2,1,0:T(8,128)(2,1)S(1)} %get-tuple-element.167), channel_id=1, source_target_pairs={{0,16},{16,0},{1,17},{17,1},{2,18},{18,2},{3,19},{19,3},{4,20},{20... | collective-permute-start | bytes 1769480 | tf_op jit(solution)/shard_map/ppermute | solution.py:672
  128.9 9.6 %collective-permute-start.14 = (f32[8,768]{1,0:T(8,128)S(1)}, f32[8,768]{1,0:T(8,128)S(1)}, u32[]{:S(2)}, u32[]{:S(2)}) collective-permute-start(f32[8,768]{1,0:T(8,128)S(1)} %get-tuple-element.171.refs_4_), channel_id=1, source_target_pairs={{0,16},{16,0},{1,17},{17,1},{2,18},{18,2},{3,19},{19,3},{4,20},{20... | collective-permute-start | bytes 73736 | tf_op jit(solution)/shard_map/ppermute | solution.py:672
  134.0 4.5 %collective-permute-start.13 = (bf16[3,384,512]{2,1,0:T(8,128)(2,1)S(1)}, bf16[3,384,512]{2,1,0:T(8,128)(2,1)S(1)}, u32[]{:S(2)}, u32[]{:S(2)}) collective-permute-start(bf16[3,384,512]{2,1,0:T(8,128)(2,1)S(1)} %get-tuple-element.170), channel_id=1, source_target_pairs={{0,16},{16,0},{1,17},{17,1},{2,18},{18,2},{3,19},{19,3},{4,20},{20... | collective-permute-start | bytes 3538952 | tf_op jit(solution)/shard_map/ppermute | solution.py:672
  134.4 6.9 %copy-start.4 = (bf16[1,1,1024,768]{3,2,1,0:T(8,128)(2,1)S(1)}, bf16[1,1,1024,768]{3,2,1,0:T(8,128)(2,1)}, u32[]{:S(2)}) copy-start(bf16[1,1,1024,768]{3,2,1,0:T(8,128)(2,1)} %param.11) | copy-start | bytes 4718596
  134.8 10.3 %collective-permute-start.15 = (bf16[2,72,768]{2,1,0:T(8,128)(2,1)S(1)}, bf16[2,72,768]{2,1,0:T(8,128)(2,1)S(1)}, u32[]{:S(2)}, u32[]{:S(2)}) collective-permute-start(bf16[2,72,768]{2,1,0:T(8,128)(2,1)S(1)} %get-tuple-element.165), channel_id=1, source_target_pairs={{0,4},{1,5},{2,6},{3,7},{4,0},{5,1},{6,2},{7,3},{8,12},{9,13},{10,... | collective-permute-start | bytes 663560 | tf_op jit(solution)/shard_map/ppermute | solution.py:672
  136.4 8.3 %collective-permute-start.16 = (bf16[2,72,768]{2,1,0:T(8,128)(2,1)S(1)}, bf16[2,72,768]{2,1,0:T(8,128)(2,1)S(1)}, u32[]{:S(2)}, u32[]{:S(2)}) collective-permute-start(bf16[2,72,768]{2,1,0:T(8,128)(2,1)S(1)} %get-tuple-element.178), channel_id=1, source_target_pairs={{0,1},{1,0},{2,3},{3,2},{4,5},{5,4},{6,7},{7,6},{8,9},{9,8},{10,11... | collective-permute-start | bytes 663560 | tf_op jit(solution)/shard_map/ppermute | solution.py:672
  136.9 8.1 %collective-permute-start.17 = (bf16[2,72,768]{2,1,0:T(8,128)(2,1)S(1)}, bf16[2,72,768]{2,1,0:T(8,128)(2,1)S(1)}, u32[]{:S(2)}, u32[]{:S(2)}) collective-permute-start(bf16[2,72,768]{2,1,0:T(8,128)(2,1)S(1)} %get-tuple-element.179), channel_id=1, source_target_pairs={{0,2},{1,3},{2,0},{3,1},{4,6},{5,7},{6,4},{7,5},{8,10},{9,11},{10,... | collective-permute-start | bytes 663560 | tf_op jit(solution)/shard_map/ppermute | solution.py:672
  139.2 13.6 %collective-permute-start.18 = (bf16[816,256]{1,0:T(8,128)(2,1)S(1)}, bf16[816,256]{1,0:T(8,128)(2,1)S(1)}, u32[]{:S(2)}, u32[]{:S(2)}) collective-permute-start(bf16[816,256]{1,0:T(8,128)(2,1)S(1)} %get-tuple-element.172), channel_id=1, source_target_pairs={{0,1},{1,0},{2,3},{3,2},{4,5},{5,4},{6,7},{7,6},{8,9},{9,8},{10,11... | collective-permute-start | bytes 1253384 | tf_op jit(solution)/shard_map/ppermute | solution.py:672
  140.8 13.4 %collective-permute-start.19 = (bf16[8,120,256]{2,1,0:T(8,128)(2,1)S(1)}, bf16[8,120,256]{2,1,0:T(8,128)(2,1)S(1)}, u32[]{:S(2)}, u32[]{:S(2)}) collective-permute-start(bf16[8,120,256]{2,1,0:T(8,128)(2,1)S(1)} %get-tuple-element.186), channel_id=1, source_target_pairs={{0,2},{1,3},{2,0},{3,1},{4,6},{5,7},{6,4},{7,5},{8,10},{9,11},{10,... | collective-permute-start | bytes 1474568 | tf_op jit(solution)/shard_map/ppermute | solution.py:672
  145.2 14.9 %collective-permute-start.20 = (bf16[1,216,768]{2,1,0:T(8,128)(2,1)S(1)}, bf16[1,216,768]{2,1,0:T(8,128)(2,1)S(1)}, u32[]{:S(2)}, u32[]{:S(2)}) collective-permute-start(bf16[1,216,768]{2,1,0:T(8,128)(2,1)S(1)} %get-tuple-element.180), channel_id=1, source_target_pairs={{0,8},{1,9},{2,10},{3,11},{4,12},{5,13},{6,14},{7,15},{8,0},{9,1},... | collective-permute-start | bytes 995336 | tf_op jit(solution)/shard_map/ppermute | solution.py:672
  154.5 7.5 %collective-permute-start.22 = (bf16[4,120,256]{2,1,0:T(8,128)(2,1)S(1)}, bf16[4,120,256]{2,1,0:T(8,128)(2,1)S(1)}, u32[]{:S(2)}, u32[]{:S(2)}) collective-permute-start(bf16[4,120,256]{2,1,0:T(8,128)(2,1)S(1)} %get-tuple-element.193), channel_id=1, source_target_pairs={{0,1},{1,0},{2,3},{3,2},{4,5},{5,4},{6,7},{7,6},{8,9},{9,8},{10,11... | collective-permute-start | bytes 737288 | tf_op jit(solution)/shard_map/ppermute | solution.py:672
  156.0 5.9 %collective-permute-start.21 = (bf16[432,256]{1,0:T(8,128)(2,1)S(1)}, bf16[432,256]{1,0:T(8,128)(2,1)S(1)}, u32[]{:S(2)}, u32[]{:S(2)}) collective-permute-start(bf16[432,256]{1,0:T(8,128)(2,1)S(1)} %get-tuple-element.192), channel_id=1, source_target_pairs={{0,2},{1,3},{2,0},{3,1},{4,6},{5,7},{6,4},{7,5},{8,10},{9,11},{10,... | collective-permute-start | bytes 663560 | tf_op jit(solution)/shard_map/ppermute | solution.py:672
  162.1 6.3 %collective-permute-start.23 = (bf16[480,256]{1,0:T(8,128)(2,1)S(1)}, bf16[480,256]{1,0:T(8,128)(2,1)S(1)}, u32[]{:S(2)}, u32[]{:S(2)}) collective-permute-start(bf16[480,256]{1,0:T(8,128)(2,1)S(1)} %get-tuple-element.196), channel_id=1, source_target_pairs={{0,4},{1,5},{2,6},{3,7},{4,0},{5,1},{6,2},{7,3},{8,12},{9,13},{10,... | collective-permute-start | bytes 737288 | tf_op jit(solution)/shard_map/ppermute | solution.py:672
  168.4 7.5 %collective-permute-start.24 = (bf16[264,256]{1,0:T(8,128)(2,1)S(1)}, bf16[264,256]{1,0:T(8,128)(2,1)S(1)}, u32[]{:S(2)}, u32[]{:S(2)}) collective-permute-start(bf16[264,256]{1,0:T(8,128)(2,1)S(1)} %get-tuple-element.199), channel_id=1, source_target_pairs={{0,8},{1,9},{2,10},{3,11},{4,12},{5,13},{6,14},{7,15},{8,0},{9,1},... | collective-permute-start | bytes 405512 | tf_op jit(solution)/shard_map/ppermute | solution.py:672
  (9 other events, 25.8 us)

commit v3 on v2

--- a/solution.py
+++ b/solution.py
@@ -293,7 +293,7 @@
         compiler_params=params(24),
         cost_estimate=LONG,
         name="attend_back",
-    )(info, *pinned(q, ko, vo, kc, vc, o, do), lse, cosine, sine)
+    )(info, *pinned(q, ko, vo, kc, vc, o, do, lse), cosine, sine)
 
 
 C0 = 0.7978845608028654

time: 177 us -> 176 us (level)
  no operation moved by 1% of the time
where the time goes in v3:
time: 176 us
  Pallas kernels  119 us (68%)
  starting transfers between devices  30.3 us (17%)
  waiting for transfers between devices  21.9 us (12%)
  local copies, waits for them, and re-layouts  2.08 us (1%)
  between operations  1.81 us (1%)
    pallas_call x1, Pallas kernels, layer(): pl.pallas_call(layer_kernel, in_specs=[SMEM] + [IN_VMEM] * 5 + [anywhere]...  70 us
    pallas_call x2, Pallas kernels, attend_back(): pl.pallas_call(attend_back_kernel, grid=(pairs,), in_specs=[SMEM] + [head...  28.1 us
    ppermute x22, starting transfers between devices, exchange(): return lax.ppermute(value, axis, [(i, i ^ bit) for i in range(size)])  25 us
    ppermute x22, waiting for transfers between devices, exchange(): return lax.ppermute(value, axis, [(i, i ^ bit) for i in range(size)])  20 us
    pallas_call x2, Pallas kernels, finish(): pl.pallas_call(functools.partial(finish_kernel, len(dqs), tiles), in_spec...  7.04 us
    pallas_call x2, Pallas kernels, weigh(): pl.pallas_call(functools.partial(weigh_kernel, first), in_specs=[SMEM] +...  6.3 us
    pallas_call x2, Pallas kernels, start_sum(): pl.pallas_call(functools.partial(start_kernel, orders, sources, mode), co...  4.67 us
  transfers between devices with their start and end apart: 25, of which 10 were waited for; matrix products, arithmetic and copies ran while one was open for 1% of the time, Pallas kernels for 25%

profile of v3, /device:TPU:0, one launch (start us, length us, event | category | flops | bytes accessed | tf_op | source)
XLA Modules:
  0.0 176.1 jit_solution(16619141075939406207)
XLA Ops:
  0.6 2.5 %collective-permute-start = (bf16[1024,768]{1,0:T(8,128)(2,1)}, bf16[1024,768]{1,0:T(8,128)(2,1)S(1)}, u32[]{:S(2)}, u32[]{:S(2)}) collective-permute-start(bf16[1024,768]{1,0:T(8,128)(2,1)} %bitcast.20), channel_id=1, source_target_pairs={{0,16},{1,17},{2,18},{3,19},{4,20},{5,21},{6,22},{7,23},{8,24},{9,... | collective-permute-start | bytes 4718600 | tf_op jit(solution)/shard_map/ppermute | solution.py:927
  4.3 1.9 %collective-permute-done.received = bf16[1024,768]{1,0:T(8,128)(2,1)S(1)} collective-permute-done((bf16[1024,768]{1,0:T(8,128)(2,1)}, bf16[1024,768]{1,0:T(8,128)(2,1)S(1)}, u32[]{:S(2)}, u32[]{:S(2)}) %collective-permute-start) | collective-permute-done | bytes 1572896 | tf_op jit(solution)/shard_map/ppermute | solution.py:927
  6.2 1.1 copy-done.14
  7.4 70.0 %layer.1 = (bf16[6,1024,128]{2,1,0:T(8,128)(2,1)}, bf16[6,1024,128]{2,1,0:T(8,128)(2,1)}, bf16[6,1024,128]{2,1,0:T(8,128)(2,1)}, bf16[6,1024,128]{2,1,0:T(8,128)...) custom-call(s32[2]{0:T(128)} %pad_add_fusion.info, ...), custom_call_target="tpu_custom_call" | custom-call | flops 34359738368 | bytes 67108864 | tf_op jit(solution)/shard_map/layer/pallas_call | solution.py:557
  78.3 10.1 %attend_back.2 = (bf16[1024,256]{1,0:T(8,128)(2,1)S(1)}, bf16[2,1024,256]{2,1,0:T(8,128)(2,1)S(1)}, bf16[2,1024,256]{2,1,0:T(8,128)(2,1)S(1)}) custom-call(s32[2]{0:T(128)S(1)} %copy-done.9, bf16[6,1024,128]{2,1,0:T(8,128)(2,1)} %get-tuple-element.112.q, bf16[6,1024,128]{2,1,0:T(8,128)(2,1)} %get-tuple-element.113.ko, ...), custom_call_target="tpu_custom_call" | custom-call | flops 34359738368 | bytes 67108864 | tf_op jit(solution)/shard_map/attend_back/pallas_call | solution.py:284
  88.5 3.9 %start_sum.2 = (bf16[8,72,768]{2,1,0:T(8,128)(2,1)S(1)}, bf16[8,72,768]{2,1,0:T(8,128)(2,1)S(1)}, bf16[8,72,768]{2,1,0:T(8,128)(2,1)S(1)}, bf16[8,72,768]{2,1,0:...) custom-call(s32[1]{0:T(128)} %bitcast.4.me, bf16[48,32,768]{2,1,0:T(8,128)(2,1)S(1)} %bitcast.17, ...), custom_call_target="tpu_custom_call" | custom-call | flops 1048576 | bytes 65536 | tf_op jit(solution)/shard_map/start_sum/pallas_call | solution.py:770
  92.5 2.4 %collective-permute-start.4 = (bf16[8,72,768]{2,1,0:T(8,128)(2,1)S(1)}, bf16[8,72,768]{2,1,0:T(8,128)(2,1)S(1)}, u32[]{:S(2)}, u32[]{:S(2)}) collective-permute-start(bf16[8,72,768]{2,1,0:T(8,128)(2,1)S(1)} %get-tuple-element.132), channel_id=1, source_target_pairs={{0,1},{1,0},{2,3},{3,2},{4,5},{5,4},{6,7},{7,6},{8,9},{9,8},{10,11... | collective-permute-start | bytes 2654216 | tf_op jit(solution)/shard_map/ppermute | solution.py:672
  94.9 1.5 collective-permute-start.5
  96.4 1.6 collective-permute-start.6
  97.9 18.0 %attend_back.3 = (bf16[1024,512]{1,0:T(8,128)(2,1)S(1)}, bf16[2,1024,512]{2,1,0:T(8,128)(2,1)S(1)}, bf16[2,1024,512]{2,1,0:T(8,128)(2,1)S(1)}) custom-call(s32[2]{0:T(128)S(1)} %copy-done.9, bf16[6,1024,128]{2,1,0:T(8,128)(2,1)} %get-tuple-element.112.q, bf16[6,1024,128]{2,1,0:T(8,128)(2,1)} %get-tuple-element.113.ko, ...), custom_call_target="tpu_custom_call" | custom-call | flops 34359738368 | bytes 67108864 | tf_op jit(solution)/shard_map/attend_back/pallas_call | solution.py:284
  115.9 1.3 collective-permute-start.8
  117.3 1.6 collective-permute-start.7
  120.9 2.4 %weigh.2 = (bf16[2,1024,256]{2,1,0:T(8,128)(2,1)S(1)}, bf16[3,384,256]{2,1,0:T(8,128)(2,1)S(1)}, bf16[3,384,256]{2,1,0:T(8,128)(2,1)S(1)}, f32[8,768]{1,0:T(8,128)S(1)}) custom-call(s32[2]{0:T(128)S(1)} %copy-done.9, bf16[1024,256]{1,0:T(8,128)(2,1)S(1)} %get-tuple-element.120.dq.refs_0_, bf16[2,1024,256]{2,1,0:T(8,128)(2,1)S(1)} %get-tuple-element.150.keep, ...), custom_call_target="tpu_custom_call" | custom-call | flops 34359738368 | bytes 67108864 | tf_op jit(solution)/shard_map/weigh/pallas_call | solution.py:611
  123.3 0.9 collective-permute-start.12
  124.2 3.9 %weigh.3 = (bf16[2,1024,512]{2,1,0:T(8,128)(2,1)S(1)}, bf16[3,384,512]{2,1,0:T(8,128)(2,1)S(1)}, bf16[3,384,512]{2,1,0:T(8,128)(2,1)S(1)}, f32[8,768]{1,0:T(8,128)S(1)}) custom-call(s32[2]{0:T(128)S(1)} %copy-done.9, bf16[1024,512]{1,0:T(8,128)(2,1)S(1)} %get-tuple-element.134.dq.refs_1_, bf16[2,1024,512]{2,1,0:T(8,128)(2,1)S(1)} %get-tuple-element.143.keep, ...), custom_call_target="tpu_custom_call" | custom-call | flops 34359738368 | bytes 67108864 | tf_op jit(solution)/shard_map/weigh/pallas_call | solution.py:611
  128.2 5.0 %collective-permute-done.10.refs_4_ = bf16[4,72,768]{2,1,0:T(8,128)(2,1)S(1)} collective-permute-done((bf16[4,72,768]{2,1,0:T(8,128)(2,1)S(1)}, bf16[4,72,768]{2,1,0:T(8,128)(2,1)S(1)}, u32[]{:S(2)}, u32[]{:S(2)}) %collective-permute-start.10) | collective-permute-done | bytes 442400 | tf_op jit(solution)/shard_map/ppermute | solution.py:672
  134.0 1.6 collective-permute-start.15
  136.2 1.5 collective-permute-start.17
  138.5 1.6 collective-permute-start.18
  140.5 2.2 %finish.2.refs_4_ = bf16[1024,768]{1,0:T(8,128)(2,1)} custom-call(bf16[1024,768]{1,0:T(8,128)(2,1)S(1)} %bitcast.22, f32[1024,768]{1,0:T(8,128)S(1)} %copy-done.1, bf16[768,2304]{1,0:T(8,128)(2,1)S(1)} %copy-done, f32[768]{0:T(1024)S(1)} %copy-done.6, bf16[1024,256]{1,0:T(8,128)(2,1)S(1)} %get-tuple-element.120.dq.refs_0_, ...), custom_call_target="tpu_custom_call" | custom-call | flops 34359738368 | bytes 67108864 | tf_op jit(solution)/shard_map/finish/pallas_call | solution.py:650
  142.7 1.3 collective-permute-done.16.refs_4_
  144.5 2.7 %collective-permute-start.20 = (bf16[1,216,768]{2,1,0:T(8,128)(2,1)S(1)}, bf16[1,216,768]{2,1,0:T(8,128)(2,1)S(1)}, u32[]{:S(2)}, u32[]{:S(2)}) collective-permute-start(bf16[1,216,768]{2,1,0:T(8,128)(2,1)S(1)} %get-tuple-element.180), channel_id=1, source_target_pairs={{0,8},{1,9},{2,10},{3,11},{4,12},{5,13},{6,14},{7,15},{8,0},{9,1},... | collective-permute-start | bytes 995336 | tf_op jit(solution)/shard_map/ppermute | solution.py:672
  147.2 4.9 %finish.3 = bf16[1024,768]{1,0:T(8,128)(2,1)} custom-call(bf16[1024,768]{1,0:T(8,128)(2,1)S(1)} %bitcast.23, f32[1024,768]{1,0:T(8,128)S(1)} %copy-done.1, bf16[768,2304]{1,0:T(8,128)(2,1)S(1)} %copy-done, f32[768]{0:T(1024)S(1)} %copy-done.6, bf16[1024,256]{1,0:T(8,128)(2,1)S(1)} %get-tuple-element.120.dq.refs_0_, ...), custom_call_target="tpu_custom_call", output_to_operand_aliasing={{}: (8, {})} | custom-call | flops 1048576 | bytes 65536 | tf_op jit(solution)/shard_map/finish/pallas_call | solution.py:650
  152.1 1.4 collective-permute-done.19.refs_3_
  153.7 1.6 collective-permute-start.22
  155.3 1.5 collective-permute-start.21
  156.8 2.6 %collective-permute-done.20.got = bf16[1,216,768]{2,1,0:T(8,128)(2,1)S(1)} collective-permute-done((bf16[1,216,768]{2,1,0:T(8,128)(2,1)S(1)}, bf16[1,216,768]{2,1,0:T(8,128)(2,1)S(1)}, u32[]{:S(2)}, u32[]{:S(2)}) %collective-permute-start.20) | collective-permute-done | bytes 331808 | tf_op jit(solution)/shard_map/ppermute | solution.py:672
  159.4 1.8 %collective-permute-done.21.refs_2_ = bf16[432,256]{1,0:T(8,128)(2,1)S(1)} collective-permute-done((bf16[432,256]{1,0:T(8,128)(2,1)S(1)}, bf16[432,256]{1,0:T(8,128)(2,1)S(1)}, u32[]{:S(2)}, u32[]{:S(2)}) %collective-permute-start.21) | collective-permute-done | bytes 221216 | tf_op jit(solution)/shard_map/ppermute | solution.py:672
  161.9 5.6 %collective-permute-done.23.refs_1_ = bf16[480,256]{1,0:T(8,128)(2,1)S(1)} collective-permute-done((bf16[480,256]{1,0:T(8,128)(2,1)S(1)}, bf16[480,256]{1,0:T(8,128)(2,1)S(1)}, u32[]{:S(2)}, u32[]{:S(2)}) %collective-permute-start.23) | collective-permute-done | bytes 245792 | tf_op jit(solution)/shard_map/ppermute | solution.py:672
  167.6 4.1 %collective-permute-start.24 = (bf16[264,256]{1,0:T(8,128)(2,1)S(1)}, bf16[264,256]{1,0:T(8,128)(2,1)S(1)}, u32[]{:S(2)}, u32[]{:S(2)}) collective-permute-start(bf16[264,256]{1,0:T(8,128)(2,1)S(1)} %get-tuple-element.199), channel_id=1, source_target_pairs={{0,8},{1,9},{2,10},{3,11},{4,12},{5,13},{6,14},{7,15},{8,0},{9,1},... | collective-permute-start | bytes 405512 | tf_op jit(solution)/shard_map/ppermute | solution.py:672
  171.7 0.9 feed_end.1
  173.5 1.7 collective-permute-done.24.got
  (67 shorter events, 9.4 us)
Async XLA Ops:
  0.6 5.6 %collective-permute-start = (bf16[1024,768]{1,0:T(8,128)(2,1)}, bf16[1024,768]{1,0:T(8,128)(2,1)S(1)}, u32[]{:S(2)}, u32[]{:S(2)}) collective-permute-start(bf16[1024,768]{1,0:T(8,128)(2,1)} %bitcast.20), channel_id=1, source_target_pairs={{0,16},{1,17},{2,18},{3,19},{4,20},{5,21},{6,22},{7,23},{8,24},{9,... | collective-permute-start | bytes 4718600 | tf_op jit(solution)/shard_map/ppermute | solution.py:927
  7.4 70.9 %copy-start.7 = (f32[32,1024]{1,0:T(8,128)S(1)}, f32[32,1024]{1,0:T(8,128)}, u32[]{:S(2)}) copy-start(f32[32,1024]{1,0:T(8,128)} %constant.14.clone.sine_t.sine) | copy-start | bytes 393220
  7.4 70.9 %copy-start.8 = (f32[32,1024]{1,0:T(8,128)S(1)}, f32[32,1024]{1,0:T(8,128)}, u32[]{:S(2)}) copy-start(f32[32,1024]{1,0:T(8,128)} %constant.13.clone.cosine_t.cosine) | copy-start | bytes 393220
  7.4 70.9 %copy-start.9 = (s32[2]{0:T(128)S(1)}, s32[2]{0:T(128)}, u32[]{:S(2)}) copy-start(s32[2]{0:T(128)} %pad_add_fusion.info) | copy-start | bytes 28
  77.4 11.1 %collective-permute-start.3 = (bf16[384,768]{1,0:T(8,128)(2,1)}, bf16[384,768]{1,0:T(8,128)(2,1)S(1)}, u32[]{:S(2)}, u32[]{:S(2)}) collective-permute-start(bf16[384,768]{1,0:T(8,128)(2,1)} %get-tuple-element.128), channel_id=1, source_target_pairs={{0,16},{16,0},{1,17},{17,1},{2,18},{18,2},{3,19},{19,3},{4,20},{20... | collective-permute-start | bytes 1769480 | tf_op jit(solution)/shard_map/ppermute | solution.py:672
  77.8 10.7 %collective-permute-start.1 = (bf16[1536,768]{1,0:T(8,128)(2,1)}, bf16[1536,768]{1,0:T(8,128)(2,1)S(1)}, u32[]{:S(2)}, u32[]{:S(2)}) collective-permute-start(bf16[1536,768]{1,0:T(8,128)(2,1)} %get-tuple-element.122), channel_id=1, source_target_pairs={{0,16},{16,0},{1,17},{17,1},{2,18},{18,2},{3,19},{19,3},{4,20},{20... | collective-permute-start | bytes 7077896 | tf_op jit(solution)/shard_map/ppermute | solution.py:672
  77.9 10.5 %collective-permute-start.2 = (bf16[1536,768]{1,0:T(8,128)(2,1)}, bf16[1536,768]{1,0:T(8,128)(2,1)S(1)}, u32[]{:S(2)}, u32[]{:S(2)}) collective-permute-start(bf16[1536,768]{1,0:T(8,128)(2,1)} %get-tuple-element.125), channel_id=1, source_target_pairs={{0,16},{16,0},{1,17},{17,1},{2,18},{18,2},{3,19},{19,3},{4,20},{20... | collective-permute-start | bytes 7077896 | tf_op jit(solution)/shard_map/ppermute | solution.py:672
  78.3 10.2 %copy-start.2 = (bf16[1536,768]{1,0:T(8,128)(2,1)S(1)}, bf16[1536,768]{1,0:T(8,128)(2,1)}, u32[]{:S(2)}) copy-start(bf16[1536,768]{1,0:T(8,128)(2,1)} %get-tuple-element.124) | copy-start | bytes 7077892
  78.3 10.2 %copy-start.3 = (bf16[1536,768]{1,0:T(8,128)(2,1)S(1)}, bf16[1536,768]{1,0:T(8,128)(2,1)}, u32[]{:S(2)}) copy-start(bf16[1536,768]{1,0:T(8,128)(2,1)} %get-tuple-element.121) | copy-start | bytes 7077892
  78.3 10.2 %copy-start.5 = (bf16[384,768]{1,0:T(8,128)(2,1)S(1)}, bf16[384,768]{1,0:T(8,128)(2,1)}, u32[]{:S(2)}) copy-start(bf16[384,768]{1,0:T(8,128)(2,1)} %get-tuple-element.127) | copy-start | bytes 1769476
  92.5 26.4 %collective-permute-start.4 = (bf16[8,72,768]{2,1,0:T(8,128)(2,1)S(1)}, bf16[8,72,768]{2,1,0:T(8,128)(2,1)S(1)}, u32[]{:S(2)}, u32[]{:S(2)}) collective-permute-start(bf16[8,72,768]{2,1,0:T(8,128)(2,1)S(1)} %get-tuple-element.132), channel_id=1, source_target_pairs={{0,1},{1,0},{2,3},{3,2},{4,5},{5,4},{6,7},{7,6},{8,9},{9,8},{10,11... | collective-permute-start | bytes 2654216 | tf_op jit(solution)/shard_map/ppermute | solution.py:672
  94.9 24.0 %collective-permute-start.5 = (bf16[8,72,768]{2,1,0:T(8,128)(2,1)S(1)}, bf16[8,72,768]{2,1,0:T(8,128)(2,1)S(1)}, u32[]{:S(2)}, u32[]{:S(2)}) collective-permute-start(bf16[8,72,768]{2,1,0:T(8,128)(2,1)S(1)} %get-tuple-element.138), channel_id=1, source_target_pairs={{0,2},{1,3},{2,0},{3,1},{4,6},{5,7},{6,4},{7,5},{8,10},{9,11},{10,... | collective-permute-start | bytes 2654216 | tf_op jit(solution)/shard_map/ppermute | solution.py:672
  96.4 22.5 %collective-permute-start.6 = (bf16[8,72,768]{2,1,0:T(8,128)(2,1)S(1)}, bf16[8,72,768]{2,1,0:T(8,128)(2,1)S(1)}, u32[]{:S(2)}, u32[]{:S(2)}) collective-permute-start(bf16[8,72,768]{2,1,0:T(8,128)(2,1)S(1)} %get-tuple-element.139), channel_id=1, source_target_pairs={{0,4},{1,5},{2,6},{3,7},{4,0},{5,1},{6,2},{7,3},{8,12},{9,13},{10,... | collective-permute-start | bytes 2654216 | tf_op jit(solution)/shard_map/ppermute | solution.py:672
  115.9 5.0 %collective-permute-start.8 = (bf16[2,1024,256]{2,1,0:T(8,128)(2,1)S(1)}, bf16[2,1024,256]{2,1,0:T(8,128)(2,1)S(1)}, u32[]{:S(2)}, u32[]{:S(2)}) collective-permute-start(bf16[2,1024,256]{2,1,0:T(8,128)(2,1)S(1)} %get-tuple-element.152), channel_id=1, source_target_pairs={{16,0},{17,1},{18,2},{19,3},{20,4},{21,5},{22,6},{23,7},{24,8},{25... | collective-permute-start | bytes 3145736 | tf_op jit(solution)/shard_map/ppermute | solution.py:952
  117.3 7.0 %collective-permute-start.7 = (bf16[2,1024,512]{2,1,0:T(8,128)(2,1)S(1)}, bf16[2,1024,512]{2,1,0:T(8,128)(2,1)S(1)}, u32[]{:S(2)}, u32[]{:S(2)}) collective-permute-start(bf16[2,1024,512]{2,1,0:T(8,128)(2,1)S(1)} %get-tuple-element.144), channel_id=1, source_target_pairs={{16,0},{17,1},{18,2},{19,3},{20,4},{21,5},{22,6},{23,7},{24,8},{25... | collective-permute-start | bytes 6291464 | tf_op jit(solution)/shard_map/ppermute | solution.py:954
  119.8 13.9 %collective-permute-start.9 = (bf16[4,72,768]{2,1,0:T(8,128)(2,1)S(1)}, bf16[4,72,768]{2,1,0:T(8,128)(2,1)S(1)}, u32[]{:S(2)}, u32[]{:S(2)}) collective-permute-start(bf16[4,72,768]{2,1,0:T(8,128)(2,1)S(1)} %get-tuple-element.149), channel_id=1, source_target_pairs={{0,2},{1,3},{2,0},{3,1},{4,6},{5,7},{6,4},{7,5},{8,10},{9,11},{10,... | collective-permute-start | bytes 1327112 | tf_op jit(solution)/shard_map/ppermute | solution.py:672
  120.3 12.9 %collective-permute-start.10 = (bf16[4,72,768]{2,1,0:T(8,128)(2,1)S(1)}, bf16[4,72,768]{2,1,0:T(8,128)(2,1)S(1)}, u32[]{:S(2)}, u32[]{:S(2)}) collective-permute-start(bf16[4,72,768]{2,1,0:T(8,128)(2,1)S(1)} %get-tuple-element.159), channel_id=1, source_target_pairs={{0,4},{1,5},{2,6},{3,7},{4,0},{5,1},{6,2},{7,3},{8,12},{9,13},{10,... | collective-permute-start | bytes 1327112 | tf_op jit(solution)/shard_map/ppermute | solution.py:672
  120.8 12.9 %collective-permute-start.11 = (bf16[4,72,768]{2,1,0:T(8,128)(2,1)S(1)}, bf16[4,72,768]{2,1,0:T(8,128)(2,1)S(1)}, u32[]{:S(2)}, u32[]{:S(2)}) collective-permute-start(bf16[4,72,768]{2,1,0:T(8,128)(2,1)S(1)} %get-tuple-element.160), channel_id=1, source_target_pairs={{0,1},{1,0},{2,3},{3,2},{4,5},{5,4},{6,7},{7,6},{8,9},{9,8},{10,11... | collective-permute-start | bytes 1327112 | tf_op jit(solution)/shard_map/ppermute | solution.py:672
  123.3 12.8 %collective-permute-start.12 = (bf16[3,384,256]{2,1,0:T(8,128)(2,1)S(1)}, bf16[3,384,256]{2,1,0:T(8,128)(2,1)S(1)}, u32[]{:S(2)}, u32[]{:S(2)}) collective-permute-start(bf16[3,384,256]{2,1,0:T(8,128)(2,1)S(1)} %get-tuple-element.167), channel_id=1, source_target_pairs={{0,16},{16,0},{1,17},{17,1},{2,18},{18,2},{3,19},{19,3},{4,20},{20... | collective-permute-start | bytes 1769480 | tf_op jit(solution)/shard_map/ppermute | solution.py:672
  128.1 9.6 %collective-permute-start.14 = (f32[8,768]{1,0:T(8,128)S(1)}, f32[8,768]{1,0:T(8,128)S(1)}, u32[]{:S(2)}, u32[]{:S(2)}) collective-permute-start(f32[8,768]{1,0:T(8,128)S(1)} %get-tuple-element.171.refs_4_), channel_id=1, source_target_pairs={{0,16},{16,0},{1,17},{17,1},{2,18},{18,2},{3,19},{19,3},{4,20},{20... | collective-permute-start | bytes 73736 | tf_op jit(solution)/shard_map/ppermute | solution.py:672
  133.2 4.5 %collective-permute-start.13 = (bf16[3,384,512]{2,1,0:T(8,128)(2,1)S(1)}, bf16[3,384,512]{2,1,0:T(8,128)(2,1)S(1)}, u32[]{:S(2)}, u32[]{:S(2)}) collective-permute-start(bf16[3,384,512]{2,1,0:T(8,128)(2,1)S(1)} %get-tuple-element.170), channel_id=1, source_target_pairs={{0,16},{16,0},{1,17},{17,1},{2,18},{18,2},{3,19},{19,3},{4,20},{20... | collective-permute-start | bytes 3538952 | tf_op jit(solution)/shard_map/ppermute | solution.py:672
  133.7 6.9 %copy-start.4 = (bf16[1,1,1024,768]{3,2,1,0:T(8,128)(2,1)S(1)}, bf16[1,1,1024,768]{3,2,1,0:T(8,128)(2,1)}, u32[]{:S(2)}) copy-start(bf16[1,1,1024,768]{3,2,1,0:T(8,128)(2,1)} %param.11) | copy-start | bytes 4718596
  134.0 10.3 %collective-permute-start.15 = (bf16[2,72,768]{2,1,0:T(8,128)(2,1)S(1)}, bf16[2,72,768]{2,1,0:T(8,128)(2,1)S(1)}, u32[]{:S(2)}, u32[]{:S(2)}) collective-permute-start(bf16[2,72,768]{2,1,0:T(8,128)(2,1)S(1)} %get-tuple-element.165), channel_id=1, source_target_pairs={{0,4},{1,5},{2,6},{3,7},{4,0},{5,1},{6,2},{7,3},{8,12},{9,13},{10,... | collective-permute-start | bytes 663560 | tf_op jit(solution)/shard_map/ppermute | solution.py:672
  135.7 8.3 %collective-permute-start.16 = (bf16[2,72,768]{2,1,0:T(8,128)(2,1)S(1)}, bf16[2,72,768]{2,1,0:T(8,128)(2,1)S(1)}, u32[]{:S(2)}, u32[]{:S(2)}) collective-permute-start(bf16[2,72,768]{2,1,0:T(8,128)(2,1)S(1)} %get-tuple-element.178), channel_id=1, source_target_pairs={{0,1},{1,0},{2,3},{3,2},{4,5},{5,4},{6,7},{7,6},{8,9},{9,8},{10,11... | collective-permute-start | bytes 663560 | tf_op jit(solution)/shard_map/ppermute | solution.py:672
  136.2 8.1 %collective-permute-start.17 = (bf16[2,72,768]{2,1,0:T(8,128)(2,1)S(1)}, bf16[2,72,768]{2,1,0:T(8,128)(2,1)S(1)}, u32[]{:S(2)}, u32[]{:S(2)}) collective-permute-start(bf16[2,72,768]{2,1,0:T(8,128)(2,1)S(1)} %get-tuple-element.179), channel_id=1, source_target_pairs={{0,2},{1,3},{2,0},{3,1},{4,6},{5,7},{6,4},{7,5},{8,10},{9,11},{10,... | collective-permute-start | bytes 663560 | tf_op jit(solution)/shard_map/ppermute | solution.py:672
  138.5 13.6 %collective-permute-start.18 = (bf16[816,256]{1,0:T(8,128)(2,1)S(1)}, bf16[816,256]{1,0:T(8,128)(2,1)S(1)}, u32[]{:S(2)}, u32[]{:S(2)}) collective-permute-start(bf16[816,256]{1,0:T(8,128)(2,1)S(1)} %get-tuple-element.172), channel_id=1, source_target_pairs={{0,1},{1,0},{2,3},{3,2},{4,5},{5,4},{6,7},{7,6},{8,9},{9,8},{10,11... | collective-permute-start | bytes 1253384 | tf_op jit(solution)/shard_map/ppermute | solution.py:672
  140.0 13.4 %collective-permute-start.19 = (bf16[8,120,256]{2,1,0:T(8,128)(2,1)S(1)}, bf16[8,120,256]{2,1,0:T(8,128)(2,1)S(1)}, u32[]{:S(2)}, u32[]{:S(2)}) collective-permute-start(bf16[8,120,256]{2,1,0:T(8,128)(2,1)S(1)} %get-tuple-element.186), channel_id=1, source_target_pairs={{0,2},{1,3},{2,0},{3,1},{4,6},{5,7},{6,4},{7,5},{8,10},{9,11},{10,... | collective-permute-start | bytes 1474568 | tf_op jit(solution)/shard_map/ppermute | solution.py:672
  144.5 14.9 %collective-permute-start.20 = (bf16[1,216,768]{2,1,0:T(8,128)(2,1)S(1)}, bf16[1,216,768]{2,1,0:T(8,128)(2,1)S(1)}, u32[]{:S(2)}, u32[]{:S(2)}) collective-permute-start(bf16[1,216,768]{2,1,0:T(8,128)(2,1)S(1)} %get-tuple-element.180), channel_id=1, source_target_pairs={{0,8},{1,9},{2,10},{3,11},{4,12},{5,13},{6,14},{7,15},{8,0},{9,1},... | collective-permute-start | bytes 995336 | tf_op jit(solution)/shard_map/ppermute | solution.py:672
  153.7 7.5 %collective-permute-start.22 = (bf16[4,120,256]{2,1,0:T(8,128)(2,1)S(1)}, bf16[4,120,256]{2,1,0:T(8,128)(2,1)S(1)}, u32[]{:S(2)}, u32[]{:S(2)}) collective-permute-start(bf16[4,120,256]{2,1,0:T(8,128)(2,1)S(1)} %get-tuple-element.193), channel_id=1, source_target_pairs={{0,1},{1,0},{2,3},{3,2},{4,5},{5,4},{6,7},{7,6},{8,9},{9,8},{10,11... | collective-permute-start | bytes 737288 | tf_op jit(solution)/shard_map/ppermute | solution.py:672
  155.3 5.9 %collective-permute-start.21 = (bf16[432,256]{1,0:T(8,128)(2,1)S(1)}, bf16[432,256]{1,0:T(8,128)(2,1)S(1)}, u32[]{:S(2)}, u32[]{:S(2)}) collective-permute-start(bf16[432,256]{1,0:T(8,128)(2,1)S(1)} %get-tuple-element.192), channel_id=1, source_target_pairs={{0,2},{1,3},{2,0},{3,1},{4,6},{5,7},{6,4},{7,5},{8,10},{9,11},{10,... | collective-permute-start | bytes 663560 | tf_op jit(solution)/shard_map/ppermute | solution.py:672
  161.3 6.3 %collective-permute-start.23 = (bf16[480,256]{1,0:T(8,128)(2,1)S(1)}, bf16[480,256]{1,0:T(8,128)(2,1)S(1)}, u32[]{:S(2)}, u32[]{:S(2)}) collective-permute-start(bf16[480,256]{1,0:T(8,128)(2,1)S(1)} %get-tuple-element.196), channel_id=1, source_target_pairs={{0,4},{1,5},{2,6},{3,7},{4,0},{5,1},{6,2},{7,3},{8,12},{9,13},{10,... | collective-permute-start | bytes 737288 | tf_op jit(solution)/shard_map/ppermute | solution.py:672
  167.6 7.5 %collective-permute-start.24 = (bf16[264,256]{1,0:T(8,128)(2,1)S(1)}, bf16[264,256]{1,0:T(8,128)(2,1)S(1)}, u32[]{:S(2)}, u32[]{:S(2)}) collective-permute-start(bf16[264,256]{1,0:T(8,128)(2,1)S(1)} %get-tuple-element.199), channel_id=1, source_target_pairs={{0,8},{1,9},{2,10},{3,11},{4,12},{5,13},{6,14},{7,15},{8,0},{9,1},... | collective-permute-start | bytes 405512 | tf_op jit(solution)/shard_map/ppermute | solution.py:672
  (8 other events, 25.1 us)

commit v4 on v3

--- a/solution.py
+++ b/solution.py
@@ -26,6 +26,8 @@
 
 COST = pl.CostEstimate(flops=1 << 20, bytes_accessed=1 << 16, transcendentals=0)
 LONG = pl.CostEstimate(flops=1 << 35, bytes_accessed=1 << 26, transcendentals=0)
+
+FEED = (((0, 0), (1, 0), (2, 0), (2, 1)), ((0, 1), (1, 1), (2, 2)), ((0, 2), (1, 2)))
 
 SMEM = pl.BlockSpec(memory_space=pltpu.SMEM)
 IN_VMEM = pl.BlockSpec(memory_space=pltpu.VMEM)
@@ -834,12 +836,16 @@
 def feed_end_kernel(kept, got, down, up, out):
     total = kept[0].astype(f32) + got[0].astype(f32)
     tall, few = down.shape[0] // GROUPS, out.shape[0] // GROUPS
-    ups = []
-    for g in range(GROUPS):
-        row = g * (2 * tall + few)
-        down[g * tall : (g + 1) * tall, :] = total[row : row + tall]
-        ups.append(total[row + tall : row + 2 * tall])
-        out[g * few : (g + 1) * few, :] = total[row + 2 * tall : row + 2 * tall + few]
+    ups, row = [], 0
+    for group in FEED:
+        for a, j in group:
+            size = few if a == 2 else tall
+            piece = total[row : row + size]
+            row += size
+            if a == 1:
+                ups.append(piece)
+            else:
+                (down, None, out)[a][j * size : (j + 1) * size, :] = piece
     up[...] = jnp.concatenate(ups, axis=0).T
 
 
@@ -943,7 +949,7 @@
         me,
         [by_rows(after(a, dq1)) for a in (down_keep, up_keep, out_keep)],
         [by_rows(a) for a in (down_got, up_got, out_got)],
-        [[(a, lambda part, g=g: part * GROUPS + g, 0) for a in range(3)] for g in range(GROUPS)],
+        [[(a, lambda part, j=j: part * GROUPS + j, 0) for a, j in group] for group in FEED],
         width,
         [],
         False,

time: 176 us -> 175 us (level)
  transfers between devices with their start and end apart: 25 -> 25, of which waited for: 10 -> 9; matrix products, arithmetic and copies ran while one was open for 1% -> 1% of each run, Pallas kernels for 25% -> 25%
where the time goes in v4:
time: 175 us
  Pallas kernels  119 us (68%)
  starting transfers between devices  29.5 us (17%)
  waiting for transfers between devices  21.5 us (12%)
  local copies, waits for them, and re-layouts  2.25 us (1%)
  between operations  1.83 us (1%)
    pallas_call x1, Pallas kernels, layer(): pl.pallas_call(layer_kernel, in_specs=[SMEM] + [IN_VMEM] * 5 + [anywhere]...  70 us
    pallas_call x2, Pallas kernels, attend_back(): pl.pallas_call(attend_back_kernel, grid=(pairs,), in_specs=[SMEM] + [head...  28.1 us
    ppermute x22, starting transfers between devices, exchange(): return lax.ppermute(value, axis, [(i, i ^ bit) for i in range(size)])  24.2 us
    ppermute x22, waiting for transfers between devices, exchange(): return lax.ppermute(value, axis, [(i, i ^ bit) for i in range(size)])  19.6 us
    pallas_call x2, Pallas kernels, finish(): pl.pallas_call(functools.partial(finish_kernel, len(dqs), tiles), in_spec...  7.04 us
    pallas_call x2, Pallas kernels, weigh(): pl.pallas_call(functools.partial(weigh_kernel, first), in_specs=[SMEM] +...  6.28 us
    pallas_call x2, Pallas kernels, start_sum(): pl.pallas_call(functools.partial(start_kernel, orders, sources, mode), co...  4.65 us
  transfers between devices with their start and end apart: 25, of which 9 were waited for; matrix products, arithmetic and copies ran while one was open for 1% of the time, Pallas kernels for 25%

profile of v4, /device:TPU:0, one launch (start us, length us, event | category | flops | bytes accessed | tf_op | source)
XLA Modules:
  0.0 175.1 jit_solution(14680936466348556129)
XLA Ops:
  0.6 2.5 %collective-permute-start = (bf16[1024,768]{1,0:T(8,128)(2,1)}, bf16[1024,768]{1,0:T(8,128)(2,1)S(1)}, u32[]{:S(2)}, u32[]{:S(2)}) collective-permute-start(bf16[1024,768]{1,0:T(8,128)(2,1)} %bitcast.20), channel_id=1, source_target_pairs={{0,16},{1,17},{2,18},{3,19},{4,20},{5,21},{6,22},{7,23},{8,24},{9,... | collective-permute-start | bytes 4718600 | tf_op jit(solution)/shard_map/ppermute | solution.py:933
  4.3 1.9 %collective-permute-done.received = bf16[1024,768]{1,0:T(8,128)(2,1)S(1)} collective-permute-done((bf16[1024,768]{1,0:T(8,128)(2,1)}, bf16[1024,768]{1,0:T(8,128)(2,1)S(1)}, u32[]{:S(2)}, u32[]{:S(2)}) %collective-permute-start) | collective-permute-done | bytes 1572896 | tf_op jit(solution)/shard_map/ppermute | solution.py:933
  6.2 1.1 copy-done.14
  7.4 70.0 %layer.1 = (bf16[6,1024,128]{2,1,0:T(8,128)(2,1)}, bf16[6,1024,128]{2,1,0:T(8,128)(2,1)}, bf16[6,1024,128]{2,1,0:T(8,128)(2,1)}, bf16[6,1024,128]{2,1,0:T(8,128)...) custom-call(s32[2]{0:T(128)} %pad_add_fusion.info, ...), custom_call_target="tpu_custom_call" | custom-call | flops 34359738368 | bytes 67108864 | tf_op jit(solution)/shard_map/layer/pallas_call | solution.py:559
  78.3 10.1 %attend_back.2 = (bf16[1024,256]{1,0:T(8,128)(2,1)S(1)}, bf16[2,1024,256]{2,1,0:T(8,128)(2,1)S(1)}, bf16[2,1024,256]{2,1,0:T(8,128)(2,1)S(1)}) custom-call(s32[2]{0:T(128)S(1)} %copy-done.9, bf16[6,1024,128]{2,1,0:T(8,128)(2,1)} %get-tuple-element.112.q, bf16[6,1024,128]{2,1,0:T(8,128)(2,1)} %get-tuple-element.113.ko, ...), custom_call_target="tpu_custom_call" | custom-call | flops 34359738368 | bytes 67108864 | tf_op jit(solution)/shard_map/attend_back/pallas_call | solution.py:286
  88.5 3.9 %start_sum.2 = (bf16[8,80,768]{2,1,0:T(8,128)(2,1)S(1)}, bf16[8,80,768]{2,1,0:T(8,128)(2,1)S(1)}, bf16[8,72,768]{2,1,0:T(8,128)(2,1)S(1)}, bf16[8,72,768]{2,1,0:...) custom-call(s32[1]{0:T(128)} %bitcast.4.me, bf16[48,32,768]{2,1,0:T(8,128)(2,1)S(1)} %bitcast.17, ...), custom_call_target="tpu_custom_call" | custom-call | flops 1048576 | bytes 65536 | tf_op jit(solution)/shard_map/start_sum/pallas_call | solution.py:772
  92.4 2.4 %collective-permute-start.4 = (bf16[8,80,768]{2,1,0:T(8,128)(2,1)S(1)}, bf16[8,80,768]{2,1,0:T(8,128)(2,1)S(1)}, u32[]{:S(2)}, u32[]{:S(2)}) collective-permute-start(bf16[8,80,768]{2,1,0:T(8,128)(2,1)S(1)} %get-tuple-element.132), channel_id=1, source_target_pairs={{0,1},{1,0},{2,3},{3,2},{4,5},{5,4},{6,7},{7,6},{8,9},{9,8},{10,11... | collective-permute-start | bytes 2949128 | tf_op jit(solution)/shard_map/ppermute | solution.py:674
  94.8 1.6 collective-permute-start.6
  96.4 1.5 collective-permute-start.5
  97.9 18.0 %attend_back.3 = (bf16[1024,512]{1,0:T(8,128)(2,1)S(1)}, bf16[2,1024,512]{2,1,0:T(8,128)(2,1)S(1)}, bf16[2,1024,512]{2,1,0:T(8,128)(2,1)S(1)}) custom-call(s32[2]{0:T(128)S(1)} %copy-done.9, bf16[6,1024,128]{2,1,0:T(8,128)(2,1)} %get-tuple-element.112.q, bf16[6,1024,128]{2,1,0:T(8,128)(2,1)} %get-tuple-element.113.ko, ...), custom_call_target="tpu_custom_call" | custom-call | flops 34359738368 | bytes 67108864 | tf_op jit(solution)/shard_map/attend_back/pallas_call | solution.py:286
  115.9 1.3 collective-permute-start.8
  117.2 1.6 collective-permute-start.7
  118.8 0.9 step_sum.6
  120.8 1.6 collective-permute-start.10
  122.5 2.4 %weigh.2 = (bf16[2,1024,256]{2,1,0:T(8,128)(2,1)S(1)}, bf16[3,384,256]{2,1,0:T(8,128)(2,1)S(1)}, bf16[3,384,256]{2,1,0:T(8,128)(2,1)S(1)}, f32[8,768]{1,0:T(8,128)S(1)}) custom-call(s32[2]{0:T(128)S(1)} %copy-done.9, bf16[1024,256]{1,0:T(8,128)(2,1)S(1)} %get-tuple-element.120.dq.refs_0_, bf16[2,1024,256]{2,1,0:T(8,128)(2,1)S(1)} %get-tuple-element.150.keep, ...), custom_call_target="tpu_custom_call" | custom-call | flops 34359738368 | bytes 67108864 | tf_op jit(solution)/shard_map/weigh/pallas_call | solution.py:613
  125.0 3.9 %weigh.3 = (bf16[2,1024,512]{2,1,0:T(8,128)(2,1)S(1)}, bf16[3,384,512]{2,1,0:T(8,128)(2,1)S(1)}, bf16[3,384,512]{2,1,0:T(8,128)(2,1)S(1)}, f32[8,768]{1,0:T(8,128)S(1)}) custom-call(s32[2]{0:T(128)S(1)} %copy-done.9, bf16[1024,512]{1,0:T(8,128)(2,1)S(1)} %get-tuple-element.134.dq.refs_1_, bf16[2,1024,512]{2,1,0:T(8,128)(2,1)S(1)} %get-tuple-element.143.keep, ...), custom_call_target="tpu_custom_call" | custom-call | flops 34359738368 | bytes 67108864 | tf_op jit(solution)/shard_map/weigh/pallas_call | solution.py:613
  129.4 2.8 %collective-permute-done.11.refs_5_ = bf16[4,64,768]{2,1,0:T(8,128)(2,1)S(1)} collective-permute-done((bf16[4,64,768]{2,1,0:T(8,128)(2,1)S(1)}, bf16[4,64,768]{2,1,0:T(8,128)(2,1)S(1)}, u32[]{:S(2)}, u32[]{:S(2)}) %collective-permute-start.11) | collective-permute-done | bytes 393248 | tf_op jit(solution)/shard_map/ppermute | solution.py:674
  132.4 1.3 collective-permute-done.10.refs_4_
  134.4 1.7 collective-permute-start.17
  136.1 1.5 collective-permute-start.16
  139.5 2.2 %finish.2.refs_4_ = bf16[1024,768]{1,0:T(8,128)(2,1)} custom-call(bf16[1024,768]{1,0:T(8,128)(2,1)S(1)} %bitcast.22, f32[1024,768]{1,0:T(8,128)S(1)} %copy-done.1, bf16[768,2304]{1,0:T(8,128)(2,1)S(1)} %copy-done, f32[768]{0:T(1024)S(1)} %copy-done.6, bf16[1024,256]{1,0:T(8,128)(2,1)S(1)} %get-tuple-element.120.dq.refs_0_, ...), custom_call_target="tpu_custom_call" | custom-call | flops 34359738368 | bytes 67108864 | tf_op jit(solution)/shard_map/finish/pallas_call | solution.py:652
  141.9 2.6 %collective-permute-done.16.refs_4_ = bf16[2,72,768]{2,1,0:T(8,128)(2,1)S(1)} collective-permute-done((bf16[2,72,768]{2,1,0:T(8,128)(2,1)S(1)}, bf16[2,72,768]{2,1,0:T(8,128)(2,1)S(1)}, u32[]{:S(2)}, u32[]{:S(2)}) %collective-permute-start.16) | collective-permute-done | bytes 221216 | tf_op jit(solution)/shard_map/ppermute | solution.py:674
  144.6 2.7 %collective-permute-start.20 = (bf16[1,216,768]{2,1,0:T(8,128)(2,1)S(1)}, bf16[1,216,768]{2,1,0:T(8,128)(2,1)S(1)}, u32[]{:S(2)}, u32[]{:S(2)}) collective-permute-start(bf16[1,216,768]{2,1,0:T(8,128)(2,1)S(1)} %get-tuple-element.180), channel_id=1, source_target_pairs={{0,8},{1,9},{2,10},{3,11},{4,12},{5,13},{6,14},{7,15},{8,0},{9,1},... | collective-permute-start | bytes 995336 | tf_op jit(solution)/shard_map/ppermute | solution.py:674
  147.3 4.9 %finish.3 = bf16[1024,768]{1,0:T(8,128)(2,1)} custom-call(bf16[1024,768]{1,0:T(8,128)(2,1)S(1)} %bitcast.23, f32[1024,768]{1,0:T(8,128)S(1)} %copy-done.1, bf16[768,2304]{1,0:T(8,128)(2,1)S(1)} %copy-done, f32[768]{0:T(1024)S(1)} %copy-done.6, bf16[1024,256]{1,0:T(8,128)(2,1)S(1)} %get-tuple-element.120.dq.refs_0_, ...), custom_call_target="tpu_custom_call", output_to_operand_aliasing={{}: (8, {})} | custom-call | flops 1048576 | bytes 65536 | tf_op jit(solution)/shard_map/finish/pallas_call | solution.py:652
  152.5 1.6 collective-permute-start.22
  154.0 0.9 collective-permute-start.21
  154.9 4.4 %collective-permute-done.20.got = bf16[1,216,768]{2,1,0:T(8,128)(2,1)S(1)} collective-permute-done((bf16[1,216,768]{2,1,0:T(8,128)(2,1)S(1)}, bf16[1,216,768]{2,1,0:T(8,128)(2,1)S(1)}, u32[]{:S(2)}, u32[]{:S(2)}) %collective-permute-start.20) | collective-permute-done | bytes 331808 | tf_op jit(solution)/shard_map/ppermute | solution.py:674
  160.1 1.6 collective-permute-start.23
  161.7 4.6 %collective-permute-done.23.refs_1_ = bf16[480,256]{1,0:T(8,128)(2,1)S(1)} collective-permute-done((bf16[480,256]{1,0:T(8,128)(2,1)S(1)}, bf16[480,256]{1,0:T(8,128)(2,1)S(1)}, u32[]{:S(2)}, u32[]{:S(2)}) %collective-permute-start.23) | collective-permute-done | bytes 245792 | tf_op jit(solution)/shard_map/ppermute | solution.py:674
  166.4 3.0 %collective-permute-start.24 = (bf16[264,256]{1,0:T(8,128)(2,1)S(1)}, bf16[264,256]{1,0:T(8,128)(2,1)S(1)}, u32[]{:S(2)}, u32[]{:S(2)}) collective-permute-start(bf16[264,256]{1,0:T(8,128)(2,1)S(1)} %get-tuple-element.199), channel_id=1, source_target_pairs={{0,8},{1,9},{2,10},{3,11},{4,12},{5,13},{6,14},{7,15},{8,0},{9,1},... | collective-permute-start | bytes 405512 | tf_op jit(solution)/shard_map/ppermute | solution.py:674
  169.4 0.9 feed_end.1
  171.1 3.0 %collective-permute-done.24.got = bf16[264,256]{1,0:T(8,128)(2,1)S(1)} collective-permute-done((bf16[264,256]{1,0:T(8,128)(2,1)S(1)}, bf16[264,256]{1,0:T(8,128)(2,1)S(1)}, u32[]{:S(2)}, u32[]{:S(2)}) %collective-permute-start.24) | collective-permute-done | bytes 135200 | tf_op jit(solution)/shard_map/ppermute | solution.py:674
  (67 shorter events, 9.1 us)
Async XLA Ops:
  0.6 5.6 %collective-permute-start = (bf16[1024,768]{1,0:T(8,128)(2,1)}, bf16[1024,768]{1,0:T(8,128)(2,1)S(1)}, u32[]{:S(2)}, u32[]{:S(2)}) collective-permute-start(bf16[1024,768]{1,0:T(8,128)(2,1)} %bitcast.20), channel_id=1, source_target_pairs={{0,16},{1,17},{2,18},{3,19},{4,20},{5,21},{6,22},{7,23},{8,24},{9,... | collective-permute-start | bytes 4718600 | tf_op jit(solution)/shard_map/ppermute | solution.py:933
  7.4 70.9 %copy-start.7 = (f32[32,1024]{1,0:T(8,128)S(1)}, f32[32,1024]{1,0:T(8,128)}, u32[]{:S(2)}) copy-start(f32[32,1024]{1,0:T(8,128)} %constant.14.clone.sine_t.sine) | copy-start | bytes 393220
  7.4 70.9 %copy-start.8 = (f32[32,1024]{1,0:T(8,128)S(1)}, f32[32,1024]{1,0:T(8,128)}, u32[]{:S(2)}) copy-start(f32[32,1024]{1,0:T(8,128)} %constant.13.clone.cosine_t.cosine) | copy-start | bytes 393220
  7.4 70.9 %copy-start.9 = (s32[2]{0:T(128)S(1)}, s32[2]{0:T(128)}, u32[]{:S(2)}) copy-start(s32[2]{0:T(128)} %pad_add_fusion.info) | copy-start | bytes 28
  77.4 11.1 %collective-permute-start.3 = (bf16[384,768]{1,0:T(8,128)(2,1)}, bf16[384,768]{1,0:T(8,128)(2,1)S(1)}, u32[]{:S(2)}, u32[]{:S(2)}) collective-permute-start(bf16[384,768]{1,0:T(8,128)(2,1)} %get-tuple-element.128), channel_id=1, source_target_pairs={{0,16},{16,0},{1,17},{17,1},{2,18},{18,2},{3,19},{19,3},{4,20},{20... | collective-permute-start | bytes 1769480 | tf_op jit(solution)/shard_map/ppermute | solution.py:674
  77.8 10.7 %collective-permute-start.1 = (bf16[1536,768]{1,0:T(8,128)(2,1)}, bf16[1536,768]{1,0:T(8,128)(2,1)S(1)}, u32[]{:S(2)}, u32[]{:S(2)}) collective-permute-start(bf16[1536,768]{1,0:T(8,128)(2,1)} %get-tuple-element.122), channel_id=1, source_target_pairs={{0,16},{16,0},{1,17},{17,1},{2,18},{18,2},{3,19},{19,3},{4,20},{20... | collective-permute-start | bytes 7077896 | tf_op jit(solution)/shard_map/ppermute | solution.py:674
  77.9 10.5 %collective-permute-start.2 = (bf16[1536,768]{1,0:T(8,128)(2,1)}, bf16[1536,768]{1,0:T(8,128)(2,1)S(1)}, u32[]{:S(2)}, u32[]{:S(2)}) collective-permute-start(bf16[1536,768]{1,0:T(8,128)(2,1)} %get-tuple-element.125), channel_id=1, source_target_pairs={{0,16},{16,0},{1,17},{17,1},{2,18},{18,2},{3,19},{19,3},{4,20},{20... | collective-permute-start | bytes 7077896 | tf_op jit(solution)/shard_map/ppermute | solution.py:674
  78.3 10.2 %copy-start.2 = (bf16[1536,768]{1,0:T(8,128)(2,1)S(1)}, bf16[1536,768]{1,0:T(8,128)(2,1)}, u32[]{:S(2)}) copy-start(bf16[1536,768]{1,0:T(8,128)(2,1)} %get-tuple-element.124) | copy-start | bytes 7077892
  78.3 10.2 %copy-start.3 = (bf16[1536,768]{1,0:T(8,128)(2,1)S(1)}, bf16[1536,768]{1,0:T(8,128)(2,1)}, u32[]{:S(2)}) copy-start(bf16[1536,768]{1,0:T(8,128)(2,1)} %get-tuple-element.121) | copy-start | bytes 7077892
  78.3 10.2 %copy-start.5 = (bf16[384,768]{1,0:T(8,128)(2,1)S(1)}, bf16[384,768]{1,0:T(8,128)(2,1)}, u32[]{:S(2)}) copy-start(bf16[384,768]{1,0:T(8,128)(2,1)} %get-tuple-element.127) | copy-start | bytes 1769476
  92.4 26.4 %collective-permute-start.4 = (bf16[8,80,768]{2,1,0:T(8,128)(2,1)S(1)}, bf16[8,80,768]{2,1,0:T(8,128)(2,1)S(1)}, u32[]{:S(2)}, u32[]{:S(2)}) collective-permute-start(bf16[8,80,768]{2,1,0:T(8,128)(2,1)S(1)} %get-tuple-element.132), channel_id=1, source_target_pairs={{0,1},{1,0},{2,3},{3,2},{4,5},{5,4},{6,7},{7,6},{8,9},{9,8},{10,11... | collective-permute-start | bytes 2949128 | tf_op jit(solution)/shard_map/ppermute | solution.py:674
  94.8 24.0 %collective-permute-start.6 = (bf16[8,64,768]{2,1,0:T(8,128)(2,1)S(1)}, bf16[8,64,768]{2,1,0:T(8,128)(2,1)S(1)}, u32[]{:S(2)}, u32[]{:S(2)}) collective-permute-start(bf16[8,64,768]{2,1,0:T(8,128)(2,1)S(1)} %get-tuple-element.139), channel_id=1, source_target_pairs={{0,4},{1,5},{2,6},{3,7},{4,0},{5,1},{6,2},{7,3},{8,12},{9,13},{10,... | collective-permute-start | bytes 2359304 | tf_op jit(solution)/shard_map/ppermute | solution.py:674
  96.4 22.4 %collective-permute-start.5 = (bf16[8,72,768]{2,1,0:T(8,128)(2,1)S(1)}, bf16[8,72,768]{2,1,0:T(8,128)(2,1)S(1)}, u32[]{:S(2)}, u32[]{:S(2)}) collective-permute-start(bf16[8,72,768]{2,1,0:T(8,128)(2,1)S(1)} %get-tuple-element.138), channel_id=1, source_target_pairs={{0,2},{1,3},{2,0},{3,1},{4,6},{5,7},{6,4},{7,5},{8,10},{9,11},{10,... | collective-permute-start | bytes 2654216 | tf_op jit(solution)/shard_map/ppermute | solution.py:674
  115.9 6.5 %collective-permute-start.8 = (bf16[2,1024,256]{2,1,0:T(8,128)(2,1)S(1)}, bf16[2,1024,256]{2,1,0:T(8,128)(2,1)S(1)}, u32[]{:S(2)}, u32[]{:S(2)}) collective-permute-start(bf16[2,1024,256]{2,1,0:T(8,128)(2,1)S(1)} %get-tuple-element.152), channel_id=1, source_target_pairs={{16,0},{17,1},{18,2},{19,3},{20,4},{21,5},{22,6},{23,7},{24,8},{25... | collective-permute-start | bytes 3145736 | tf_op jit(solution)/shard_map/ppermute | solution.py:958
  117.2 7.7 %collective-permute-start.7 = (bf16[2,1024,512]{2,1,0:T(8,128)(2,1)S(1)}, bf16[2,1024,512]{2,1,0:T(8,128)(2,1)S(1)}, u32[]{:S(2)}, u32[]{:S(2)}) collective-permute-start(bf16[2,1024,512]{2,1,0:T(8,128)(2,1)S(1)} %get-tuple-element.144), channel_id=1, source_target_pairs={{16,0},{17,1},{18,2},{19,3},{20,4},{21,5},{22,6},{23,7},{24,8},{25... | collective-permute-start | bytes 6291464 | tf_op jit(solution)/shard_map/ppermute | solution.py:960
  119.7 14.0 %collective-permute-start.9 = (bf16[4,80,768]{2,1,0:T(8,128)(2,1)S(1)}, bf16[4,80,768]{2,1,0:T(8,128)(2,1)S(1)}, u32[]{:S(2)}, u32[]{:S(2)}) collective-permute-start(bf16[4,80,768]{2,1,0:T(8,128)(2,1)S(1)} %get-tuple-element.149), channel_id=1, source_target_pairs={{0,2},{1,3},{2,0},{3,1},{4,6},{5,7},{6,4},{7,5},{8,10},{9,11},{10,... | collective-permute-start | bytes 1474568 | tf_op jit(solution)/shard_map/ppermute | solution.py:674
  120.3 11.8 %collective-permute-start.11 = (bf16[4,64,768]{2,1,0:T(8,128)(2,1)S(1)}, bf16[4,64,768]{2,1,0:T(8,128)(2,1)S(1)}, u32[]{:S(2)}, u32[]{:S(2)}) collective-permute-start(bf16[4,64,768]{2,1,0:T(8,128)(2,1)S(1)} %get-tuple-element.160), channel_id=1, source_target_pairs={{0,1},{1,0},{2,3},{3,2},{4,5},{5,4},{6,7},{7,6},{8,9},{9,8},{10,11... | collective-permute-start | bytes 1179656 | tf_op jit(solution)/shard_map/ppermute | solution.py:674
  120.8 12.9 %collective-permute-start.10 = (bf16[4,72,768]{2,1,0:T(8,128)(2,1)S(1)}, bf16[4,72,768]{2,1,0:T(8,128)(2,1)S(1)}, u32[]{:S(2)}, u32[]{:S(2)}) collective-permute-start(bf16[4,72,768]{2,1,0:T(8,128)(2,1)S(1)} %get-tuple-element.159), channel_id=1, source_target_pairs={{0,4},{1,5},{2,6},{3,7},{4,0},{5,1},{6,2},{7,3},{8,12},{9,13},{10,... | collective-permute-start | bytes 1327112 | tf_op jit(solution)/shard_map/ppermute | solution.py:674
  124.9 11.2 %collective-permute-start.12 = (bf16[3,384,256]{2,1,0:T(8,128)(2,1)S(1)}, bf16[3,384,256]{2,1,0:T(8,128)(2,1)S(1)}, u32[]{:S(2)}, u32[]{:S(2)}) collective-permute-start(bf16[3,384,256]{2,1,0:T(8,128)(2,1)S(1)} %get-tuple-element.167), channel_id=1, source_target_pairs={{0,16},{16,0},{1,17},{17,1},{2,18},{18,2},{3,19},{19,3},{4,20},{20... | collective-permute-start | bytes 1769480 | tf_op jit(solution)/shard_map/ppermute | solution.py:674
  128.8 8.8 %collective-permute-start.14 = (f32[8,768]{1,0:T(8,128)S(1)}, f32[8,768]{1,0:T(8,128)S(1)}, u32[]{:S(2)}, u32[]{:S(2)}) collective-permute-start(f32[8,768]{1,0:T(8,128)S(1)} %get-tuple-element.171.refs_4_), channel_id=1, source_target_pairs={{0,16},{16,0},{1,17},{17,1},{2,18},{18,2},{3,19},{19,3},{4,20},{20... | collective-permute-start | bytes 73736 | tf_op jit(solution)/shard_map/ppermute | solution.py:674
  132.2 5.5 %collective-permute-start.13 = (bf16[3,384,512]{2,1,0:T(8,128)(2,1)S(1)}, bf16[3,384,512]{2,1,0:T(8,128)(2,1)S(1)}, u32[]{:S(2)}, u32[]{:S(2)}) collective-permute-start(bf16[3,384,512]{2,1,0:T(8,128)(2,1)S(1)} %get-tuple-element.170), channel_id=1, source_target_pairs={{0,16},{16,0},{1,17},{17,1},{2,18},{18,2},{3,19},{19,3},{4,20},{20... | collective-permute-start | bytes 3538952 | tf_op jit(solution)/shard_map/ppermute | solution.py:674
  133.7 5.6 %copy-start.4 = (bf16[1,1,1024,768]{3,2,1,0:T(8,128)(2,1)S(1)}, bf16[1,1,1024,768]{3,2,1,0:T(8,128)(2,1)}, u32[]{:S(2)}) copy-start(bf16[1,1,1024,768]{3,2,1,0:T(8,128)(2,1)} %param.11) | copy-start | bytes 4718596
  134.1 10.4 %collective-permute-start.15 = (bf16[2,80,768]{2,1,0:T(8,128)(2,1)S(1)}, bf16[2,80,768]{2,1,0:T(8,128)(2,1)S(1)}, u32[]{:S(2)}, u32[]{:S(2)}) collective-permute-start(bf16[2,80,768]{2,1,0:T(8,128)(2,1)S(1)} %get-tuple-element.165), channel_id=1, source_target_pairs={{0,4},{1,5},{2,6},{3,7},{4,0},{5,1},{6,2},{7,3},{8,12},{9,13},{10,... | collective-permute-start | bytes 737288 | tf_op jit(solution)/shard_map/ppermute | solution.py:674
  134.4 7.4 %collective-permute-start.17 = (bf16[2,64,768]{2,1,0:T(8,128)(2,1)S(1)}, bf16[2,64,768]{2,1,0:T(8,128)(2,1)S(1)}, u32[]{:S(2)}, u32[]{:S(2)}) collective-permute-start(bf16[2,64,768]{2,1,0:T(8,128)(2,1)S(1)} %get-tuple-element.179), channel_id=1, source_target_pairs={{0,2},{1,3},{2,0},{3,1},{4,6},{5,7},{6,4},{7,5},{8,10},{9,11},{10,... | collective-permute-start | bytes 589832 | tf_op jit(solution)/shard_map/ppermute | solution.py:674
  136.1 8.4 %collective-permute-start.16 = (bf16[2,72,768]{2,1,0:T(8,128)(2,1)S(1)}, bf16[2,72,768]{2,1,0:T(8,128)(2,1)S(1)}, u32[]{:S(2)}, u32[]{:S(2)}) collective-permute-start(bf16[2,72,768]{2,1,0:T(8,128)(2,1)S(1)} %get-tuple-element.178), channel_id=1, source_target_pairs={{0,1},{1,0},{2,3},{3,2},{4,5},{5,4},{6,7},{7,6},{8,9},{9,8},{10,11... | collective-permute-start | bytes 663560 | tf_op jit(solution)/shard_map/ppermute | solution.py:674
  138.4 13.8 %collective-permute-start.18 = (bf16[816,256]{1,0:T(8,128)(2,1)S(1)}, bf16[816,256]{1,0:T(8,128)(2,1)S(1)}, u32[]{:S(2)}, u32[]{:S(2)}) collective-permute-start(bf16[816,256]{1,0:T(8,128)(2,1)S(1)} %get-tuple-element.172), channel_id=1, source_target_pairs={{0,1},{1,0},{2,3},{3,2},{4,5},{5,4},{6,7},{7,6},{8,9},{9,8},{10,11... | collective-permute-start | bytes 1253384 | tf_op jit(solution)/shard_map/ppermute | solution.py:674
  139.0 13.2 %collective-permute-start.19 = (bf16[8,120,256]{2,1,0:T(8,128)(2,1)S(1)}, bf16[8,120,256]{2,1,0:T(8,128)(2,1)S(1)}, u32[]{:S(2)}, u32[]{:S(2)}) collective-permute-start(bf16[8,120,256]{2,1,0:T(8,128)(2,1)S(1)} %get-tuple-element.186), channel_id=1, source_target_pairs={{0,2},{1,3},{2,0},{3,1},{4,6},{5,7},{6,4},{7,5},{8,10},{9,11},{10,... | collective-permute-start | bytes 1474568 | tf_op jit(solution)/shard_map/ppermute | solution.py:674
  144.6 14.7 %collective-permute-start.20 = (bf16[1,216,768]{2,1,0:T(8,128)(2,1)S(1)}, bf16[1,216,768]{2,1,0:T(8,128)(2,1)S(1)}, u32[]{:S(2)}, u32[]{:S(2)}) collective-permute-start(bf16[1,216,768]{2,1,0:T(8,128)(2,1)S(1)} %get-tuple-element.180), channel_id=1, source_target_pairs={{0,8},{1,9},{2,10},{3,11},{4,12},{5,13},{6,14},{7,15},{8,0},{9,1},... | collective-permute-start | bytes 995336 | tf_op jit(solution)/shard_map/ppermute | solution.py:674
  152.5 7.5 %collective-permute-start.22 = (bf16[4,120,256]{2,1,0:T(8,128)(2,1)S(1)}, bf16[4,120,256]{2,1,0:T(8,128)(2,1)S(1)}, u32[]{:S(2)}, u32[]{:S(2)}) collective-permute-start(bf16[4,120,256]{2,1,0:T(8,128)(2,1)S(1)} %get-tuple-element.193), channel_id=1, source_target_pairs={{0,1},{1,0},{2,3},{3,2},{4,5},{5,4},{6,7},{7,6},{8,9},{9,8},{10,11... | collective-permute-start | bytes 737288 | tf_op jit(solution)/shard_map/ppermute | solution.py:674
  154.0 5.9 %collective-permute-start.21 = (bf16[432,256]{1,0:T(8,128)(2,1)S(1)}, bf16[432,256]{1,0:T(8,128)(2,1)S(1)}, u32[]{:S(2)}, u32[]{:S(2)}) collective-permute-start(bf16[432,256]{1,0:T(8,128)(2,1)S(1)} %get-tuple-element.192), channel_id=1, source_target_pairs={{0,2},{1,3},{2,0},{3,1},{4,6},{5,7},{6,4},{7,5},{8,10},{9,11},{10,... | collective-permute-start | bytes 663560 | tf_op jit(solution)/shard_map/ppermute | solution.py:674
  160.1 6.3 %collective-permute-start.23 = (bf16[480,256]{1,0:T(8,128)(2,1)S(1)}, bf16[480,256]{1,0:T(8,128)(2,1)S(1)}, u32[]{:S(2)}, u32[]{:S(2)}) collective-permute-start(bf16[480,256]{1,0:T(8,128)(2,1)S(1)} %get-tuple-element.196), channel_id=1, source_target_pairs={{0,4},{1,5},{2,6},{3,7},{4,0},{5,1},{6,2},{7,3},{8,12},{9,13},{10,... | collective-permute-start | bytes 737288 | tf_op jit(solution)/shard_map/ppermute | solution.py:674
  166.4 7.8 %collective-permute-start.24 = (bf16[264,256]{1,0:T(8,128)(2,1)S(1)}, bf16[264,256]{1,0:T(8,128)(2,1)S(1)}, u32[]{:S(2)}, u32[]{:S(2)}) collective-permute-start(bf16[264,256]{1,0:T(8,128)(2,1)S(1)} %get-tuple-element.199), channel_id=1, source_target_pairs={{0,8},{1,9},{2,10},{3,11},{4,12},{5,13},{6,14},{7,15},{8,0},{9,1},... | collective-permute-start | bytes 405512 | tf_op jit(solution)/shard_map/ppermute | solution.py:674
  (8 other events, 31.0 us)
